TPU v7x, 256 devices: a whole 4x4x8 slice. The times are simulated.
256 devices in a mesh: row: 16 (over x_lo, z), col: 16 (over x_hi, y, core).
Axes of the slice: x: 4 (x_hi: 2, x_lo: 2; x = x_hi * 2 + x_lo), y: 4, z: 8, core: 2. Of those that a mesh axis runs over, the one named last changes fastest.
Arguments:
- adjoints: bfloat16 [4096, 16, 200], P(('row', 'col')), may hold values from -6 to 6
- jac_blocks: bfloat16 [16, 16, 128, 200, 200], P('row', 'col'), may hold values from -0.4375 to 0.4375
- jac_rows: int32 [16, 16, 128], P('row', 'col'), may hold values from 0 to 255, as said below
- jac_cols: int32 [16, 16, 128], P('row', 'col'), may hold values from 0 to 255, as said below
- tile_count: int32 [16, 16], P('row', 'col'), may hold values from 32 to 128, as said below
Outputs:
- transposed: bfloat16 [4096, 16, 200], P('col')
Inputs may be any that keep to these rules, and one draw needn't show every extreme that they name: `jac_rows`: row faces within a tile; both ends are named by some slot. `jac_cols`: column faces within a tile; both ends are named by some slot. `tile_count`: slots at or above the count are padding and are ignored; some tile has exactly 128 live slots.
All inputs are finite; a program needn't handle non-finite values.
Results may differ from a plain program's by a relative error of at most 0.001.
Values may be sent and summed in bfloat16 or wider, within the bound.
No kernel may reach another device: no remote copies, remote signals or barrier semaphores. Data moves between devices by JAX's collectives and lax.ppermute only.
A program may use at most 64 MiB of HBM per device.

v0:
```python
import jax
import jax.numpy as jnp
from jax import lax
from jax.experimental import pallas as pl
from jax.experimental.pallas import tpu as pltpu
from jax.sharding import Mesh, PartitionSpec as P


AXES = ("xlo", "z", "xhi", "y", "core")
SIZES = (2, 8, 2, 4, 2)
ROW = ("xlo", "z")
COL = ("xhi", "y", "core")

LANES = 128
DEPTH = 8
PITCH = 132
TERM_PITCH = 20
GROUP = 16
BITS = 15
LIMIT = 32767.0
TINY = 1e-30


def in_vmem():
    return pl.BlockSpec(memory_space=pltpu.VMEM)


def in_smem():
    return pl.BlockSpec(memory_space=pltpu.SMEM)


def params():
    return pltpu.CompilerParams(vmem_limit_bytes=24 << 20)


def flip_kernel(in_ref, out_ref):
    flipped = jnp.transpose(in_ref[...])
    for i in range(out_ref.shape[0]):
        out_ref[i] = flipped


def flip(faces, copies):
    rows, b = faces.shape
    return pl.pallas_call(
        flip_kernel,
        out_shape=pltpu.VMEM((copies, b, rows), faces.dtype),
        in_specs=[in_vmem()],
        out_specs=in_vmem(),
        compiler_params=params(),
        name="flip",
    )(faces)


def relayout_kernel(in_ref, out_ref, left_ref, right_ref):
    depth, b, slots = in_ref.shape
    for d in range(depth):
        block = in_ref[d].astype(jnp.float32)
        at = pl.ds(d * PITCH, slots)
        left_ref[at, :] = jnp.transpose(block[:LANES])
        right_ref[at, pl.ds(0, b - LANES)] = jnp.transpose(block[LANES:])
    for s in range(slots):
        at = pl.ds(s, depth, stride=PITCH)
        out_ref[s, :, pl.ds(0, LANES)] = left_ref[at, :].astype(jnp.bfloat16)
        out_ref[s, :, pl.ds(LANES, b - LANES)] = right_ref[at, :][:, : b - LANES].astype(jnp.bfloat16)


def relayout(jac):
    d, b, slots = jac.shape
    scratch = pltpu.VMEM((DEPTH * PITCH, LANES), jnp.float32)
    return pl.pallas_call(
        relayout_kernel,
        out_shape=pltpu.HBM((slots, d, b), jac.dtype),
        grid=(d // DEPTH,),
        in_specs=[pl.BlockSpec((DEPTH, b, slots), lambda i: (i, 0, 0))],
        out_specs=pl.BlockSpec((slots, DEPTH, b), lambda i: (0, i, 0)),
        scratch_shapes=[scratch, scratch],
        compiler_params=params(),
        name="relayout",
    )(pltpu.with_memory_space_constraint(jac, pltpu.HBM))


def pow2(exponent):
    return jnp.exp2(exponent).astype(jnp.bfloat16).astype(jnp.float32)


def terms_kernel(rows_ref, count_ref, cols_ref, own_ref, other_ref, jac_ref, out_ref, faces_ref, left_ref, right_ref):
    here, b, _ = jac_ref.shape
    k, _, slots = out_ref.shape
    pieces, _, per = own_ref.shape
    core = lax.axis_index("core")
    step = pl.program_id(0)

    @pl.when(step == 0)
    def _():
        for i in range(pieces):
            faces_ref[pl.ds(i * per, per), pl.ds(0, b)] = jnp.transpose(own_ref[i])
            faces_ref[pl.ds((pieces + i) * per, per), pl.ds(0, b)] = jnp.transpose(other_ref[i])

    for j in range(here):
        slot = step * here + j
        row = rows_ref[slot]
        home = row // k
        place = (((home & 1) ^ core) * pieces + home // 2) * per + (row & (k - 1)) * k
        lhs = faces_ref[pl.ds(pl.multiple_of(place, k), k), pl.ds(0, b)]
        term = jnp.dot(lhs, jac_ref[j], preferred_element_type=jnp.float32)
        at = pl.ds(pl.multiple_of(slot * TERM_PITCH, 4), k)
        left_ref[at, :] = term[:, :LANES]
        right_ref[at, pl.ds(0, b - LANES)] = term[:, LANES:]

    @pl.when(step == pl.num_programs(0) - 1)
    def _():
        meta_row = lax.broadcasted_iota(jnp.int32, (8, slots), 0)
        slot_index = lax.broadcasted_iota(jnp.int32, (1, slots), 1)
        cols = jnp.where(slot_index < count_ref[0, 0], cols_ref[...], -1).astype(jnp.float32)
        for i in range(k):
            at = pl.ds(i, slots, stride=TERM_PITCH)
            left = jnp.transpose(left_ref[at, :])
            right = jnp.transpose(right_ref[at, :])[: b - LANES]
            flipped = jnp.concatenate([left, right], axis=0)
            top = jnp.max(jnp.abs(flipped), axis=0, keepdims=True)
            exponent = jnp.ceil(jnp.log2(jnp.maximum(top, TINY)) + 0.01) - BITS
            scaled = jnp.clip(jnp.round(flipped * pow2(-exponent)), -LIMIT, LIMIT)
            meta = jnp.where(meta_row == 0, exponent, jnp.where(meta_row == 1, cols, 0.0))
            out_ref[i] = jnp.concatenate([scaled, meta], axis=0).astype(jnp.int32).astype(jnp.int16)


def make_terms(rows, count, cols, own, other, jac, k):
    slots, b, _ = jac.shape
    pieces, _, per = own.shape
    scratch = pltpu.VMEM((slots * TERM_PITCH, LANES), jnp.float32)
    return pl.pallas_call(
        terms_kernel,
        out_shape=pltpu.VMEM((k, b + 8, slots), jnp.int16),
        grid=(slots // GROUP,),
        in_specs=[in_smem(), in_smem(), in_vmem(), in_vmem(), in_vmem()]
        + [pl.BlockSpec((GROUP, b, b), lambda i: (i, 0, 0))],
        out_specs=in_vmem(),
        scratch_shapes=[pltpu.VMEM((2 * pieces * per, 2 * LANES), jnp.bfloat16), scratch, scratch],
        compiler_params=params(),
        name="terms",
    )(rows, count, cols, own, other, pltpu.with_memory_space_constraint(jac, pltpu.HBM))


def sum_kernel(got_ref, out_ref, lhs_ref, pick_ref):
    tiles, _, slots = got_ref.shape
    b, faces = out_ref.shape
    face = lax.broadcasted_iota(jnp.int32, (faces, slots), 0)
    for t in range(tiles):
        got = got_ref[t].astype(jnp.int32)
        high = got[:b] >> 8
        low = got[:b] & 255
        scale = pow2(got[b : b + 1].astype(jnp.float32))
        pick = jnp.where(face == got[b + 1 : b + 2], scale, 0.0)
        at = pl.ds(t * slots, slots)
        pick_ref[:, at] = pick.astype(jnp.bfloat16)
        lhs_ref[0:b, at] = (high.astype(jnp.float32) * 256.0).astype(jnp.bfloat16)
        lhs_ref[b : 2 * b, at] = low.astype(jnp.float32).astype(jnp.bfloat16)
    both = lax.dot_general(
        lhs_ref[...], pick_ref[...], (((1,), (1,)), ((), ())), preferred_element_type=jnp.float32
    )
    out_ref[...] = (both[:b] + both[b:]).astype(jnp.bfloat16)


def add_up(got, faces):
    tiles, rows, slots = got.shape
    b = rows - 8
    return pl.pallas_call(
        sum_kernel,
        out_shape=pltpu.VMEM((b, faces), jnp.bfloat16),
        in_specs=[in_vmem()],
        out_specs=in_vmem(),
        scratch_shapes=[
            pltpu.VMEM((2 * b, tiles * slots), jnp.bfloat16),
            pltpu.VMEM((faces, tiles * slots), jnp.bfloat16),
        ],
        compiler_params=params(),
        name="add_up",
    )(got)


def gather_result(mine):
    xlo = lax.axis_index("xlo")
    z = lax.axis_index("z")

    def up(piece):
        return lax.ppermute(piece, "z", [(i, (i + 1) % 8) for i in range(8)])

    def down(piece):
        return lax.ppermute(piece, "z", [(i, (i - 1) % 8) for i in range(8)])

    def across(piece):
        return lax.ppermute(piece, "xlo", [(0, 1), (1, 0)])

    held = {(0, 0): mine}
    held[0, -1], held[0, 1], held[1, 0] = up(mine), down(mine), across(mine)
    held[0, -2], held[0, 2], held[1, -1] = up(held[0, -1]), down(held[0, 1]), across(held[0, -1])
    held[0, -3], held[0, 3], held[1, 1] = up(held[0, -2]), down(held[0, 2]), across(held[0, 1])
    held[0, 4], held[1, 2], held[1, -2] = up(held[0, -3]), down(held[1, 1]), across(held[0, -2])
    held[1, -3], held[1, 3], held[1, 4] = up(held[1, -2]), down(held[1, 2]), across(held[0, 4])
    out = jnp.zeros((2, 8) + mine.shape, mine.dtype)
    for (x, d), piece in held.items():
        out = lax.dynamic_update_slice(out, piece[None, None], (xlo ^ x, (z + d + 8) % 8, 0, 0))
    return out


def on_device(adjoints, jac_blocks, jac_rows, jac_cols, tile_count):
    faces_here, k, b = adjoints.shape
    slots = jac_rows.shape[2]
    copies = flip(adjoints.reshape(faces_here * k, b), 8)
    own = lax.all_to_all(copies, ("xhi", "y"), 0, 0)
    other = lax.ppermute(own, "core", [(0, 1), (1, 0)])
    jac = relayout(jnp.transpose(jac_blocks[0, 0], (1, 2, 0)))
    terms = make_terms(jac_rows.reshape(slots), tile_count, jac_cols.reshape(1, slots), own, other, jac, k)
    got = lax.all_to_all(terms, ROW, 0, 0)
    mine = add_up(got, faces_here * 16)
    out = gather_result(mine).reshape(k, b, faces_here * 16)
    return jnp.transpose(out, (2, 0, 1))


def solution(mesh):
    parts = Mesh(mesh.devices.reshape(SIZES), AXES)
    placed = (
        P(AXES, None, None),
        P(ROW, COL, None, None, None),
        P(ROW, COL, None),
        P(ROW, COL, None),
        P(ROW, COL),
    )
    return jax.shard_map(
        on_device, mesh=parts, in_specs=placed, out_specs=P(COL, None, None), check_vma=False
    )
```

profile of v0, /device:TPU:2, one launch (start us, length us, event | category | flops | bytes accessed | tf_op | source)
XLA Modules:
  0.0 118.0 jit_solution(8865948706241687660)
XLA Ops:
  0.0 0.0 copy-start
  0.0 0.9 copy-done
  0.9 0.1 flip.1
  1.0 20.8 %all_to_all.10.own_ref = bf16[8,200,256]{2,1,0:T(8,128)(2,1)S(1)} all-to-all(bf16[8,200,256]{2,1,0:T(8,128)(2,1)S(1)} %flip.1), channel_id=1, replica_groups=mesh['xlo'=2,'z'=8,'xhi'=2,'y'=4,'core'=2] {'xhi','y'}, dimensions={0} | all-to-all | bytes 1638400 | tf_op jit(solution)/shard_map/all_to_all | solution.py:210
  21.8 0.0 collective-permute-start
  21.8 0.0 copy-start.1
  21.8 0.0 copy-start.2
  21.9 20.3 %relayout.1.jac_ref = bf16[128,200,200]{2,1,0:T(8,128)(2,1)} custom-call(bf16[200,200,128]{2,1,0:T(8,128)(2,1)} %bitcast.44), custom_call_target="tpu_custom_call" | custom-call | tf_op jit(solution)/shard_map/relayout/pallas_call | solution.py:70
  42.8 0.0 collective-permute-done.other_ref
  42.8 0.0 copy-done.1
  42.8 0.0 copy-done.2
  42.8 10.2 %terms.1 = s16[16,208,128]{2,1,0:T(8,128)(2,1)} custom-call(s32[128]{0:T(128)S(1)} %bitcast.42, s32[1,1]{1,0:T(1,128)S(6)} %copy.22.count_ref, s32[1,128]{1,0:T(1,128)S(1)} %bitcast.43, bf16[8,200,256]{2,1,0:T(8,128)(2,1)S(1)} %all_to_all.10.own_ref, bf16[8,200,256]{2,1,0:T(8,128)(2,1)S(1)} %collective-permute-done.other_ref, ...), custom_call_target="tpu_custom_call" | custom-call | tf_op jit(solution)/shard_map/terms/pallas_call | solution.py:131
  52.9 9.9 %all-to-all-start.1 = ((s16[16,208,128]{2,1,0:T(8,128)(2,1)}), s16[16,208,128]{2,1,0:T(8,128)(2,1)S(1)}, u32[]{:S(2)}, u32[]{:S(2)}) async-start(s16[16,208,128]{2,1,0:T(8,128)(2,1)} %terms.1), calls=%async_computation.1 | async-start | bytes 1703936 | tf_op jit(solution)/shard_map/all_to_all | solution.py:214
  62.9 22.3 %all-to-all-done.1.got_ref = s16[16,208,128]{2,1,0:T(8,128)(2,1)S(1)} async-done(((s16[16,208,128]{2,1,0:T(8,128)(2,1)}), s16[16,208,128]{2,1,0:T(8,128)(2,1)S(1)}, u32[]{:S(2)}, u32[]{:S(2)}) %all-to-all-start.1) | async-done | bytes 852000 | tf_op jit(solution)/shard_map/all_to_all | solution.py:214
  85.2 1.2 %add_up.1 = bf16[200,256]{1,0:T(8,128)(2,1)S(1)} custom-call(s16[16,208,128]{2,1,0:T(8,128)(2,1)S(1)} %all-to-all-done.1.got_ref), custom_call_target="tpu_custom_call" | custom-call | tf_op jit(solution)/shard_map/add_up/pallas_call | solution.py:167
  86.5 2.2 %collective-permute-start.1 = (bf16[200,256]{1,0:T(8,128)(2,1)S(1)}, bf16[200,256]{1,0:T(8,128)(2,1)S(1)}, u32[]{:S(2)}, u32[]{:S(2)}) collective-permute-start(bf16[200,256]{1,0:T(8,128)(2,1)S(1)} %add_up.1), channel_id=1, source_target_pairs={{0,16},{16,32},{32,48},{48,64},{64,80},{80,96},{96,112},{112,0},{1... | collective-permute-start | bytes 307208 | tf_op jit(solution)/shard_map/ppermute | solution.py:186
  88.7 1.1 collective-permute-start.2
  89.8 1.4 %collective-permute-start.3 = (bf16[200,256]{1,0:T(8,128)(2,1)S(1)}, bf16[200,256]{1,0:T(8,128)(2,1)S(1)}, u32[]{:S(2)}, u32[]{:S(2)}) collective-permute-start(bf16[200,256]{1,0:T(8,128)(2,1)S(1)} %add_up.1), channel_id=1, source_target_pairs={{0,128},{128,0},{1,129},{129,1},{2,130},{130,2},{3,131},{131,3},{4... | collective-permute-start | bytes 307208 | tf_op jit(solution)/shard_map/ppermute | solution.py:192
  91.2 0.1 broadcast_in_dim.51
  91.4 1.2 %collective-permute-done.1 = bf16[200,256]{1,0:T(8,128)(2,1)S(1)} collective-permute-done((bf16[200,256]{1,0:T(8,128)(2,1)S(1)}, bf16[200,256]{1,0:T(8,128)(2,1)S(1)}, u32[]{:S(2)}, u32[]{:S(2)}) %collective-permute-start.1) | collective-permute-done | bytes 102432 | tf_op jit(solution)/shard_map/ppermute | solution.py:186
  92.6 1.6 %collective-permute-start.4 = (bf16[200,256]{1,0:T(8,128)(2,1)S(1)}, bf16[200,256]{1,0:T(8,128)(2,1)S(1)}, u32[]{:S(2)}, u32[]{:S(2)}) collective-permute-start(bf16[200,256]{1,0:T(8,128)(2,1)S(1)} %collective-permute-done.1), channel_id=1, source_target_pairs={{0,16},{16,32},{32,48},{48,64},{64,80},{80,96},{96,112},{112,0},{1... | collective-permute-start | bytes 307208 | tf_op jit(solution)/shard_map/ppermute | solution.py:186
  94.2 0.1 collective-permute-start.6
  94.3 0.0 collective-permute-done.2
  94.3 2.8 %collective-permute-start.5 = (bf16[200,256]{1,0:T(8,128)(2,1)S(1)}, bf16[200,256]{1,0:T(8,128)(2,1)S(1)}, u32[]{:S(2)}, u32[]{:S(2)}) collective-permute-start(bf16[200,256]{1,0:T(8,128)(2,1)S(1)} %collective-permute-done.2), channel_id=1, source_target_pairs={{0,112},{16,0},{32,16},{48,32},{64,48},{80,64},{96,80},{112,96},{1... | collective-permute-start | bytes 307208 | tf_op jit(solution)/shard_map/ppermute | solution.py:189
  97.1 0.8 collective-permute-start.9
  97.9 0.0 collective-permute-done.3
  97.9 1.4 %collective-permute-done.4 = bf16[200,256]{1,0:T(8,128)(2,1)S(1)} collective-permute-done((bf16[200,256]{1,0:T(8,128)(2,1)S(1)}, bf16[200,256]{1,0:T(8,128)(2,1)S(1)}, u32[]{:S(2)}, u32[]{:S(2)}) %collective-permute-start.4) | collective-permute-done | bytes 102432 | tf_op jit(solution)/shard_map/ppermute | solution.py:186
  99.3 0.0 collective-permute-start.7
  99.3 1.4 %collective-permute-start.12 = (bf16[200,256]{1,0:T(8,128)(2,1)S(1)}, bf16[200,256]{1,0:T(8,128)(2,1)S(1)}, u32[]{:S(2)}, u32[]{:S(2)}) collective-permute-start(bf16[200,256]{1,0:T(8,128)(2,1)S(1)} %collective-permute-done.4), channel_id=1, source_target_pairs={{0,128},{128,0},{1,129},{129,1},{2,130},{130,2},{3,131},{131,3},{4... | collective-permute-start | bytes 307208 | tf_op jit(solution)/shard_map/ppermute | solution.py:192
  100.8 0.0 collective-permute-done.5
  100.8 3.3 %collective-permute-start.8 = (bf16[200,256]{1,0:T(8,128)(2,1)S(1)}, bf16[200,256]{1,0:T(8,128)(2,1)S(1)}, u32[]{:S(2)}, u32[]{:S(2)}) collective-permute-start(bf16[200,256]{1,0:T(8,128)(2,1)S(1)} %collective-permute-done.5), channel_id=1, source_target_pairs={{0,112},{16,0},{32,16},{48,32},{64,48},{80,64},{96,80},{112,96},{1... | collective-permute-start | bytes 307208 | tf_op jit(solution)/shard_map/ppermute | solution.py:189
  104.1 0.0 collective-permute-done.9
  104.1 0.0 collective-permute-start.11
  104.2 0.0 collective-permute-done.6
  104.2 2.1 %collective-permute-done.7 = bf16[200,256]{1,0:T(8,128)(2,1)S(1)} collective-permute-done((bf16[200,256]{1,0:T(8,128)(2,1)S(1)}, bf16[200,256]{1,0:T(8,128)(2,1)S(1)}, u32[]{:S(2)}, u32[]{:S(2)}) %collective-permute-start.7) | collective-permute-done | bytes 102432 | tf_op jit(solution)/shard_map/ppermute | solution.py:186
  106.3 0.0 collective-permute-start.10
  106.3 0.5 collective-permute-done.8
  106.8 0.0 collective-permute-done.12
  106.9 0.1 collective-permute-start.13
  106.9 1.8 %collective-permute-done.11 = bf16[200,256]{1,0:T(8,128)(2,1)S(1)} collective-permute-done((bf16[200,256]{1,0:T(8,128)(2,1)S(1)}, bf16[200,256]{1,0:T(8,128)(2,1)S(1)}, u32[]{:S(2)}, u32[]{:S(2)}) %collective-permute-start.11) | collective-permute-done | bytes 102432 | tf_op jit(solution)/shard_map/ppermute | solution.py:189
  108.7 2.9 %collective-permute-start.14 = (bf16[200,256]{1,0:T(8,128)(2,1)S(1)}, bf16[200,256]{1,0:T(8,128)(2,1)S(1)}, u32[]{:S(2)}, u32[]{:S(2)}) collective-permute-start(bf16[200,256]{1,0:T(8,128)(2,1)S(1)} %collective-permute-done.11), channel_id=1, source_target_pairs={{0,112},{16,0},{32,16},{48,32},{64,48},{80,64},{96,80},{112,96},{1... | collective-permute-start | bytes 307208 | tf_op jit(solution)/shard_map/ppermute | solution.py:189
  111.6 0.6 collective-permute-done.10
  112.2 1.4 %collective-permute-start.15 = (bf16[200,256]{1,0:T(8,128)(2,1)S(1)}, bf16[200,256]{1,0:T(8,128)(2,1)S(1)}, u32[]{:S(2)}, u32[]{:S(2)}) collective-permute-start(bf16[200,256]{1,0:T(8,128)(2,1)S(1)} %collective-permute-done.10), channel_id=1, source_target_pairs={{0,128},{128,0},{1,129},{129,1},{2,130},{130,2},{3,131},{131,3},{4... | collective-permute-start | bytes 307208 | tf_op jit(solution)/shard_map/ppermute | solution.py:192
  113.7 0.0 collective-permute-done.13
  113.7 0.2 collective-permute-done.14
  113.9 3.0 %collective-permute-done.15 = bf16[200,256]{1,0:T(8,128)(2,1)S(1)} collective-permute-done((bf16[200,256]{1,0:T(8,128)(2,1)S(1)}, bf16[200,256]{1,0:T(8,128)(2,1)S(1)}, u32[]{:S(2)}, u32[]{:S(2)}) %collective-permute-start.15) | collective-permute-done | bytes 102432 | tf_op jit(solution)/shard_map/ppermute | solution.py:192
  116.9 0.0 copy-start.3
  116.9 1.2 copy-done.3
  (16 shorter events, 0.2 us)
Async XLA Ops:
  0.0 0.9 copy-start
  21.8 20.9 %collective-permute-start = (bf16[8,200,256]{2,1,0:T(8,128)(2,1)S(1)}, bf16[8,200,256]{2,1,0:T(8,128)(2,1)S(1)}, u32[]{:S(2)}, u32[]{:S(2)}) collective-permute-start(bf16[8,200,256]{2,1,0:T(8,128)(2,1)S(1)} %all_to_all.10.own_ref), channel_id=1, source_target_pairs={{0,1},{1,0},{2,3},{3,2},{4,5},{5,4},{6,7},{7,6},{8,9},{9,8},{10,11... | collective-permute-start | bytes 2457608 | tf_op jit(solution)/shard_map/ppermute | solution.py:211
  21.8 20.9 %copy-start.1 = (s32[1,1,128]{2,1,0:T(1,128)S(1)}, s32[1,1,128]{2,1,0:T(1,128)}, u32[]{:S(2)}) copy-start(s32[1,1,128]{2,1,0:T(1,128)} %param.7) | copy-start | bytes 1540
  21.8 20.9 %copy-start.2 = (s32[1,1,128]{2,1,0:T(1,128)S(1)}, s32[1,1,128]{2,1,0:T(1,128)}, u32[]{:S(2)}) copy-start(s32[1,1,128]{2,1,0:T(1,128)} %param.8) | copy-start | bytes 1540
  52.9 32.3 %all-to-all-start.1 = ((s16[16,208,128]{2,1,0:T(8,128)(2,1)}), s16[16,208,128]{2,1,0:T(8,128)(2,1)S(1)}, u32[]{:S(2)}, u32[]{:S(2)}) async-start(s16[16,208,128]{2,1,0:T(8,128)(2,1)} %terms.1), calls=%async_computation.1 | async-start | bytes 1703936 | tf_op jit(solution)/shard_map/all_to_all | solution.py:214
  86.5 6.1 %collective-permute-start.1 = (bf16[200,256]{1,0:T(8,128)(2,1)S(1)}, bf16[200,256]{1,0:T(8,128)(2,1)S(1)}, u32[]{:S(2)}, u32[]{:S(2)}) collective-permute-start(bf16[200,256]{1,0:T(8,128)(2,1)S(1)} %add_up.1), channel_id=1, source_target_pairs={{0,16},{16,32},{32,48},{48,64},{64,80},{80,96},{96,112},{112,0},{1... | collective-permute-start | bytes 307208 | tf_op jit(solution)/shard_map/ppermute | solution.py:186
  88.7 5.6 %collective-permute-start.2 = (bf16[200,256]{1,0:T(8,128)(2,1)S(1)}, bf16[200,256]{1,0:T(8,128)(2,1)S(1)}, u32[]{:S(2)}, u32[]{:S(2)}) collective-permute-start(bf16[200,256]{1,0:T(8,128)(2,1)S(1)} %add_up.1), channel_id=1, source_target_pairs={{0,112},{16,0},{32,16},{48,32},{64,48},{80,64},{96,80},{112,96},{1... | collective-permute-start | bytes 307208 | tf_op jit(solution)/shard_map/ppermute | solution.py:189
  89.8 8.1 %collective-permute-start.3 = (bf16[200,256]{1,0:T(8,128)(2,1)S(1)}, bf16[200,256]{1,0:T(8,128)(2,1)S(1)}, u32[]{:S(2)}, u32[]{:S(2)}) collective-permute-start(bf16[200,256]{1,0:T(8,128)(2,1)S(1)} %add_up.1), channel_id=1, source_target_pairs={{0,128},{128,0},{1,129},{129,1},{2,130},{130,2},{3,131},{131,3},{4... | collective-permute-start | bytes 307208 | tf_op jit(solution)/shard_map/ppermute | solution.py:192
  92.6 6.8 %collective-permute-start.4 = (bf16[200,256]{1,0:T(8,128)(2,1)S(1)}, bf16[200,256]{1,0:T(8,128)(2,1)S(1)}, u32[]{:S(2)}, u32[]{:S(2)}) collective-permute-start(bf16[200,256]{1,0:T(8,128)(2,1)S(1)} %collective-permute-done.1), channel_id=1, source_target_pairs={{0,16},{16,32},{32,48},{48,64},{64,80},{80,96},{96,112},{112,0},{1... | collective-permute-start | bytes 307208 | tf_op jit(solution)/shard_map/ppermute | solution.py:186
  94.2 9.9 %collective-permute-start.6 = (bf16[200,256]{1,0:T(8,128)(2,1)S(1)}, bf16[200,256]{1,0:T(8,128)(2,1)S(1)}, u32[]{:S(2)}, u32[]{:S(2)}) collective-permute-start(bf16[200,256]{1,0:T(8,128)(2,1)S(1)} %collective-permute-done.1), channel_id=1, source_target_pairs={{0,128},{128,0},{1,129},{129,1},{2,130},{130,2},{3,131},{131,3},{4... | collective-permute-start | bytes 307208 | tf_op jit(solution)/shard_map/ppermute | solution.py:192
  94.3 6.5 %collective-permute-start.5 = (bf16[200,256]{1,0:T(8,128)(2,1)S(1)}, bf16[200,256]{1,0:T(8,128)(2,1)S(1)}, u32[]{:S(2)}, u32[]{:S(2)}) collective-permute-start(bf16[200,256]{1,0:T(8,128)(2,1)S(1)} %collective-permute-done.2), channel_id=1, source_target_pairs={{0,112},{16,0},{32,16},{48,32},{64,48},{80,64},{96,80},{112,96},{1... | collective-permute-start | bytes 307208 | tf_op jit(solution)/shard_map/ppermute | solution.py:189
  97.1 7.0 %collective-permute-start.9 = (bf16[200,256]{1,0:T(8,128)(2,1)S(1)}, bf16[200,256]{1,0:T(8,128)(2,1)S(1)}, u32[]{:S(2)}, u32[]{:S(2)}) collective-permute-start(bf16[200,256]{1,0:T(8,128)(2,1)S(1)} %collective-permute-done.2), channel_id=1, source_target_pairs={{0,128},{128,0},{1,129},{129,1},{2,130},{130,2},{3,131},{131,3},{4... | collective-permute-start | bytes 307208 | tf_op jit(solution)/shard_map/ppermute | solution.py:192
  99.3 7.0 %collective-permute-start.7 = (bf16[200,256]{1,0:T(8,128)(2,1)S(1)}, bf16[200,256]{1,0:T(8,128)(2,1)S(1)}, u32[]{:S(2)}, u32[]{:S(2)}) collective-permute-start(bf16[200,256]{1,0:T(8,128)(2,1)S(1)} %collective-permute-done.4), channel_id=1, source_target_pairs={{0,16},{16,32},{32,48},{48,64},{64,80},{80,96},{96,112},{112,0},{1... | collective-permute-start | bytes 307208 | tf_op jit(solution)/shard_map/ppermute | solution.py:186
  99.3 7.5 %collective-permute-start.12 = (bf16[200,256]{1,0:T(8,128)(2,1)S(1)}, bf16[200,256]{1,0:T(8,128)(2,1)S(1)}, u32[]{:S(2)}, u32[]{:S(2)}) collective-permute-start(bf16[200,256]{1,0:T(8,128)(2,1)S(1)} %collective-permute-done.4), channel_id=1, source_target_pairs={{0,128},{128,0},{1,129},{129,1},{2,130},{130,2},{3,131},{131,3},{4... | collective-permute-start | bytes 307208 | tf_op jit(solution)/shard_map/ppermute | solution.py:192
  100.8 6.0 %collective-permute-start.8 = (bf16[200,256]{1,0:T(8,128)(2,1)S(1)}, bf16[200,256]{1,0:T(8,128)(2,1)S(1)}, u32[]{:S(2)}, u32[]{:S(2)}) collective-permute-start(bf16[200,256]{1,0:T(8,128)(2,1)S(1)} %collective-permute-done.5), channel_id=1, source_target_pairs={{0,112},{16,0},{32,16},{48,32},{64,48},{80,64},{96,80},{112,96},{1... | collective-permute-start | bytes 307208 | tf_op jit(solution)/shard_map/ppermute | solution.py:189
  104.1 4.7 %collective-permute-start.11 = (bf16[200,256]{1,0:T(8,128)(2,1)S(1)}, bf16[200,256]{1,0:T(8,128)(2,1)S(1)}, u32[]{:S(2)}, u32[]{:S(2)}) collective-permute-start(bf16[200,256]{1,0:T(8,128)(2,1)S(1)} %collective-permute-done.9), channel_id=1, source_target_pairs={{0,112},{16,0},{32,16},{48,32},{64,48},{80,64},{96,80},{112,96},{1... | collective-permute-start | bytes 307208 | tf_op jit(solution)/shard_map/ppermute | solution.py:189
  106.3 5.9 %collective-permute-start.10 = (bf16[200,256]{1,0:T(8,128)(2,1)S(1)}, bf16[200,256]{1,0:T(8,128)(2,1)S(1)}, u32[]{:S(2)}, u32[]{:S(2)}) collective-permute-start(bf16[200,256]{1,0:T(8,128)(2,1)S(1)} %collective-permute-done.7), channel_id=1, source_target_pairs={{0,16},{16,32},{32,48},{48,64},{64,80},{80,96},{96,112},{112,0},{1... | collective-permute-start | bytes 307208 | tf_op jit(solution)/shard_map/ppermute | solution.py:186
  106.9 6.8 %collective-permute-start.13 = (bf16[200,256]{1,0:T(8,128)(2,1)S(1)}, bf16[200,256]{1,0:T(8,128)(2,1)S(1)}, u32[]{:S(2)}, u32[]{:S(2)}) collective-permute-start(bf16[200,256]{1,0:T(8,128)(2,1)S(1)} %collective-permute-done.12), channel_id=1, source_target_pairs={{0,16},{16,32},{32,48},{48,64},{64,80},{80,96},{96,112},{112,0},{1... | collective-permute-start | bytes 307208 | tf_op jit(solution)/shard_map/ppermute | solution.py:186
  108.7 5.1 %collective-permute-start.14 = (bf16[200,256]{1,0:T(8,128)(2,1)S(1)}, bf16[200,256]{1,0:T(8,128)(2,1)S(1)}, u32[]{:S(2)}, u32[]{:S(2)}) collective-permute-start(bf16[200,256]{1,0:T(8,128)(2,1)S(1)} %collective-permute-done.11), channel_id=1, source_target_pairs={{0,112},{16,0},{32,16},{48,32},{64,48},{80,64},{96,80},{112,96},{1... | collective-permute-start | bytes 307208 | tf_op jit(solution)/shard_map/ppermute | solution.py:189
  112.2 4.7 %collective-permute-start.15 = (bf16[200,256]{1,0:T(8,128)(2,1)S(1)}, bf16[200,256]{1,0:T(8,128)(2,1)S(1)}, u32[]{:S(2)}, u32[]{:S(2)}) collective-permute-start(bf16[200,256]{1,0:T(8,128)(2,1)S(1)} %collective-permute-done.10), channel_id=1, source_target_pairs={{0,128},{128,0},{1,129},{129,1},{2,130},{130,2},{3,131},{131,3},{4... | collective-permute-start | bytes 307208 | tf_op jit(solution)/shard_map/ppermute | solution.py:192
  116.9 1.2 copy-start.3
where the time goes:
time: 119 us; the launch traced here: 118 us
  waiting for transfers between devices  33.1 us (28%)
  Pallas kernels  31.7 us (27%)
  starting transfers between devices  29.1 us (24%)
  blocking collectives  20.8 us (17%)
  local copies, waits for them, and re-layouts  2.41 us (2%)
    all_to_all x1, waiting for transfers between devices, on_device(): got = lax.all_to_all(terms, ROW, 0, 0)  22.3 us
    all_to_all x1, blocking collectives, on_device(): own = lax.all_to_all(copies, ('xhi', 'y'), 0, 0)  20.8 us
    pallas_call x1, Pallas kernels, relayout(): pl.pallas_call(relayout_kernel, out_shape=pltpu.HBM((slots, d, b), jac.dt...  20.3 us
    pallas_call x1, Pallas kernels, make_terms(): pl.pallas_call(terms_kernel, out_shape=pltpu.VMEM((k, b + 8, slots), jnp....  10.2 us
    ppermute x5, starting transfers between devices, down(): return lax.ppermute(piece, 'z', [(i, (i - 1) % 8) for i in range(8)])  10.1 us
    all_to_all x1, starting transfers between devices, on_device(): got = lax.all_to_all(terms, ROW, 0, 0)  9.94 us
    ppermute x5, waiting for transfers between devices, up(): return lax.ppermute(piece, 'z', [(i, (i + 1) % 8) for i in range(8)])  5.34 us
    ppermute x5, starting transfers between devices, across(): return lax.ppermute(piece, 'xlo', [(0, 1), (1, 0)])  5.07 us
  transfers between devices with their start and end apart: 17, of which 9 were waited for; matrix products, arithmetic and copies ran while one was open for 0% of the time, Pallas kernels for 17%

commit v1 on v0

v1 whole, which is shorter than its diff:
```python
import jax
import jax.numpy as jnp
from jax import lax
from jax.experimental import pallas as pl
from jax.experimental.pallas import tpu as pltpu
from jax.sharding import Mesh, PartitionSpec as P


AXES = ("xlo", "z", "xhi", "y", "core")
SIZES = (2, 8, 2, 4, 2)
ROW = ("xlo", "z")
COL = ("xhi", "y", "core")

LANES = 128
DEPTH = 8
CHUNKS = 5
PITCH = 132
TERM_PITCH = 20
GROUP = 16
BITS = 15
LIMIT = 32767.0
TINY = 1e-30


def in_vmem():
    return pl.BlockSpec(memory_space=pltpu.VMEM)


def in_smem():
    return pl.BlockSpec(memory_space=pltpu.SMEM)


def in_hbm(array):
    return pltpu.with_memory_space_constraint(array, pltpu.HBM)


def params(mib=16):
    return pltpu.CompilerParams(vmem_limit_bytes=mib << 20)


def flip_kernel(in_ref, out_ref):
    flipped = jnp.transpose(in_ref[...])
    for i in range(out_ref.shape[0]):
        out_ref[i] = flipped


def flip(faces, copies):
    rows, b = faces.shape
    return pl.pallas_call(
        flip_kernel,
        out_shape=pltpu.VMEM((copies, b, rows), faces.dtype),
        in_specs=[in_vmem()],
        out_specs=in_vmem(),
        compiler_params=params(),
        name="flip",
    )(faces)


def relayout_kernel(jac_ref, out_ref, in_buf, out_buf, left_ref, right_ref, in_sem, out_sem):
    chunks, many, b, slots = in_buf.shape

    def bring(c):
        return pltpu.make_async_copy(jac_ref.at[pl.ds(c * many, many)], in_buf.at[c], in_sem.at[c])

    def send(c):
        return pltpu.make_async_copy(out_buf.at[c], out_ref.at[:, pl.ds(c * many, many), :], out_sem.at[c])

    for c in range(chunks):
        bring(c).start()
    for c in range(chunks):
        bring(c).wait()

        def some(group, _):
            for d in range(DEPTH):
                block = in_buf[c, group * DEPTH + d].astype(jnp.float32)
                at = pl.ds(d * PITCH, slots)
                left_ref[at, :] = jnp.transpose(block[:LANES])
                right_ref[at, pl.ds(0, b - LANES)] = jnp.transpose(block[LANES:])
            rows = pl.ds(pl.multiple_of(group * DEPTH, DEPTH), DEPTH)
            for s in range(slots):
                at = pl.ds(s, DEPTH, stride=PITCH)
                out_buf[c, s, rows, pl.ds(0, LANES)] = left_ref[at, :].astype(jnp.bfloat16)
                out_buf[c, s, rows, pl.ds(LANES, b - LANES)] = right_ref[at, :][:, : b - LANES].astype(jnp.bfloat16)
            return 0

        lax.fori_loop(0, many // DEPTH, some, 0)
        send(c).start()
    for c in range(chunks):
        send(c).wait()


def relayout(jac):
    d, b, slots = jac.shape
    many = d // CHUNKS
    scratch = pltpu.VMEM((DEPTH * PITCH, LANES), jnp.float32)
    anywhere = pl.BlockSpec(memory_space=pltpu.HBM)
    return pl.pallas_call(
        relayout_kernel,
        out_shape=pltpu.HBM((slots, d, b), jac.dtype),
        in_specs=[anywhere],
        out_specs=anywhere,
        scratch_shapes=[
            pltpu.VMEM((CHUNKS, many, b, slots), jac.dtype),
            pltpu.VMEM((CHUNKS, slots, many, b), jac.dtype),
            scratch,
            scratch,
            pltpu.SemaphoreType.DMA((CHUNKS,)),
            pltpu.SemaphoreType.DMA((CHUNKS,)),
        ],
        compiler_params=params(40),
        name="relayout",
    )(in_hbm(jac))


def pow2(exponent):
    return jnp.exp2(exponent).astype(jnp.bfloat16).astype(jnp.float32)


def terms_kernel(
    rows_ref, count_ref, cols_ref, own_ref, other_ref, jac_ref, out_ref, jac_buf, faces_ref, left_ref, right_ref, sem
):
    slots, b, _ = jac_buf.shape
    k = out_ref.shape[0]
    pieces, _, per = own_ref.shape
    core = lax.axis_index("core")

    def bring(c):
        at = pl.ds(c * GROUP, GROUP)
        return pltpu.make_async_copy(jac_ref.at[at], jac_buf.at[at], sem.at[c])

    for c in range(slots // GROUP):
        bring(c).start()
    for i in range(pieces):
        faces_ref[pl.ds(i * per, per), pl.ds(0, b)] = jnp.transpose(own_ref[i])
        faces_ref[pl.ds((pieces + i) * per, per), pl.ds(0, b)] = jnp.transpose(other_ref[i])

    def some(c, _):
        bring(c).wait()
        for j in range(GROUP):
            slot = c * GROUP + j
            row = rows_ref[slot]
            home = row // k
            place = (((home & 1) ^ core) * pieces + home // 2) * per + (row & (k - 1)) * k
            lhs = faces_ref[pl.ds(pl.multiple_of(place, k), k), pl.ds(0, b)]
            term = jnp.dot(lhs, jac_buf[slot], preferred_element_type=jnp.float32)
            at = pl.ds(pl.multiple_of(slot * TERM_PITCH, 4), k)
            left_ref[at, :] = term[:, :LANES]
            right_ref[at, pl.ds(0, b - LANES)] = term[:, LANES:]
        return 0

    lax.fori_loop(0, slots // GROUP, some, 0)
    meta_row = lax.broadcasted_iota(jnp.int32, (8, slots), 0)
    slot_index = lax.broadcasted_iota(jnp.int32, (1, slots), 1)
    cols = jnp.where(slot_index < count_ref[0, 0], cols_ref[...], -1).astype(jnp.float32)
    for i in range(k):
        at = pl.ds(i, slots, stride=TERM_PITCH)
        left = jnp.transpose(left_ref[at, :])
        right = jnp.transpose(right_ref[at, :])[: b - LANES]
        flipped = jnp.concatenate([left, right], axis=0)
        top = jnp.max(jnp.abs(flipped), axis=0, keepdims=True)
        exponent = jnp.ceil(jnp.log2(jnp.maximum(top, TINY)) + 0.01) - BITS
        scaled = jnp.clip(jnp.round(flipped * pow2(-exponent)), -LIMIT, LIMIT)
        meta = jnp.where(meta_row == 0, exponent, jnp.where(meta_row == 1, cols, 0.0))
        out_ref[i] = jnp.concatenate([scaled, meta], axis=0).astype(jnp.int32).astype(jnp.int16)


def make_terms(rows, count, cols, own, other, jac, k):
    slots, b, _ = jac.shape
    pieces, _, per = own.shape
    scratch = pltpu.VMEM((slots * TERM_PITCH, LANES), jnp.float32)
    return pl.pallas_call(
        terms_kernel,
        out_shape=jax.ShapeDtypeStruct((k, b + 8, slots), jnp.int16),
        in_specs=[in_smem(), in_smem(), in_vmem(), in_vmem(), in_vmem(), pl.BlockSpec(memory_space=pltpu.HBM)],
        out_specs=in_vmem(),
        scratch_shapes=[
            pltpu.VMEM((slots, b, b), jac.dtype),
            pltpu.VMEM((2 * pieces * per, 2 * LANES), jnp.bfloat16),
            scratch,
            scratch,
            pltpu.SemaphoreType.DMA((slots // GROUP,)),
        ],
        compiler_params=params(32),
        name="terms",
    )(rows, count, cols, own, other, in_hbm(jac))


def sum_kernel(got_ref, out_ref, lhs_ref, pick_ref):
    tiles, _, slots = got_ref.shape
    b, faces = out_ref.shape
    face = lax.broadcasted_iota(jnp.int32, (faces, slots), 0)
    for t in range(tiles):
        got = got_ref[t].astype(jnp.int32)
        high = got[:b] >> 8
        low = got[:b] & 255
        scale = pow2(got[b : b + 1].astype(jnp.float32))
        pick = jnp.where(face == got[b + 1 : b + 2], scale, 0.0)
        at = pl.ds(t * slots, slots)
        pick_ref[:, at] = pick.astype(jnp.bfloat16)
        lhs_ref[0:b, at] = (high.astype(jnp.float32) * 256.0).astype(jnp.bfloat16)
        lhs_ref[b : 2 * b, at] = low.astype(jnp.float32).astype(jnp.bfloat16)
    both = lax.dot_general(
        lhs_ref[...], pick_ref[...], (((1,), (1,)), ((), ())), preferred_element_type=jnp.float32
    )
    out_ref[...] = (both[:b] + both[b:]).astype(jnp.bfloat16)


def add_up(got, faces):
    tiles, rows, slots = got.shape
    b = rows - 8
    return pl.pallas_call(
        sum_kernel,
        out_shape=pltpu.VMEM((b, faces), jnp.bfloat16),
        in_specs=[in_vmem()],
        out_specs=in_vmem(),
        scratch_shapes=[
            pltpu.VMEM((2 * b, tiles * slots), jnp.bfloat16),
            pltpu.VMEM((faces, tiles * slots), jnp.bfloat16),
        ],
        compiler_params=params(),
        name="add_up",
    )(got)


def gather_result(mine):
    xlo = lax.axis_index("xlo")
    z = lax.axis_index("z")

    def up(piece):
        return lax.ppermute(piece, "z", [(i, (i + 1) % 8) for i in range(8)])

    def down(piece):
        return lax.ppermute(piece, "z", [(i, (i - 1) % 8) for i in range(8)])

    def across(piece):
        return lax.ppermute(piece, "xlo", [(0, 1), (1, 0)])

    held = {(0, 0): mine}
    held[0, -1], held[0, 1], held[1, 0] = up(mine), down(mine), across(mine)
    held[0, -2], held[0, 2] = up(held[0, -1]), down(held[0, 1])
    held[1, -1], held[1, 1] = across(jnp.stack([held[0, -1], held[0, 1]]))
    held[0, -3], held[0, 3] = up(held[0, -2]), down(held[0, 2])
    held[1, -2], held[1, 2] = across(jnp.stack([held[0, -2], held[0, 2]]))
    held[1, -3], held[0, 4] = up(jnp.stack([held[1, -2], held[0, -3]]))
    held[1, 3] = down(held[1, 2])
    held[1, 4] = across(held[0, 4])
    out = jnp.zeros((2, 8) + mine.shape, mine.dtype)
    for (x, d), piece in held.items():
        out = lax.dynamic_update_slice(out, piece[None, None], (xlo ^ x, (z + d + 8) % 8, 0, 0))
    return out


def on_device(adjoints, jac_blocks, jac_rows, jac_cols, tile_count):
    faces_here, k, b = adjoints.shape
    slots = jac_rows.shape[2]
    copies = flip(adjoints.reshape(faces_here * k, b), 8)
    own = lax.all_to_all(copies, ("xhi", "y"), 0, 0)
    other = lax.ppermute(own, "core", [(0, 1), (1, 0)])
    jac = relayout(jnp.transpose(jac_blocks[0, 0], (1, 2, 0)))
    terms = make_terms(jac_rows.reshape(slots), tile_count, jac_cols.reshape(1, slots), own, other, jac, k)
    got = lax.all_to_all(terms, ROW, 0, 0)
    mine = add_up(got, faces_here * 16)
    out = gather_result(mine).reshape(k, b, faces_here * 16)
    return jnp.transpose(out, (2, 0, 1))


def solution(mesh):
    parts = Mesh(mesh.devices.reshape(SIZES), AXES)
    placed = (
        P(AXES, None, None),
        P(ROW, COL, None, None, None),
        P(ROW, COL, None),
        P(ROW, COL, None),
        P(ROW, COL),
    )
    return jax.shard_map(
        on_device, mesh=parts, in_specs=placed, out_specs=P(COL, None, None), check_vma=False
    )
```

time: 119 us -> 109 us (0.916)
  Pallas kernels: 31.7 us -> 19 us
  waiting for transfers between devices: 33.1 us -> 38.6 us
  starting transfers between devices: 29.1 us -> 27.3 us
    pallas_call x1, Pallas kernels: 20.3 us -> 10.3 us  [relayout(): pl.pallas_call(relayout_kernel, out_shape=pltpu.HBM((slots, d, b), jac.dt...]
    ppermute x5 -> x4, waiting for transfers between devices: 5.34 us -> 10.9 us  [up(): return lax.ppermute(piece, 'z', [(i, (i + 1) % 8) for i in range(8)])]
    pallas_call x1, Pallas kernels: 10.2 us -> 7.42 us  [make_terms(): pl.pallas_call(terms_kernel, out_shape=jax.ShapeDtypeStruct((k, b + 8, sl...]
    ppermute x5 -> x4, waiting for transfers between devices: 2.43 us -> 0.91 us  [down(): return lax.ppermute(piece, 'z', [(i, (i - 1) % 8) for i in range(8)])]
    ppermute x5 -> x4, waiting for transfers between devices: 2.98 us -> 4.4 us  [across(): return lax.ppermute(piece, 'xlo', [(0, 1), (1, 0)])]
    ppermute x5 -> x4, starting transfers between devices: 5.07 us -> 4 us  [across(): return lax.ppermute(piece, 'xlo', [(0, 1), (1, 0)])]
    ppermute x5 -> x4, starting transfers between devices: 3.92 us -> 3.07 us  [up(): return lax.ppermute(piece, 'z', [(i, (i + 1) % 8) for i in range(8)])]
    ppermute x5 -> x4, starting transfers between devices: 10.1 us -> 10.3 us  [down(): return lax.ppermute(piece, 'z', [(i, (i - 1) % 8) for i in range(8)])]
  transfers between devices with their start and end apart: 17 -> 14, of which waited for: 9 -> 7; matrix products, arithmetic and copies ran while one was open for 0% -> 0% of each run, Pallas kernels for 17% -> 9%
where the time goes in v1:
time: 109 us
  waiting for transfers between devices  38.6 us (35%)
  starting transfers between devices  27.3 us (25%)
  blocking collectives  20.8 us (19%)
  Pallas kernels  19 us (17%)
  local copies, waits for them, and re-layouts  2.44 us (2%)
    all_to_all x1, waiting for transfers between devices, on_device(): got = lax.all_to_all(terms, ROW, 0, 0)  22.3 us
    all_to_all x1, blocking collectives, on_device(): own = lax.all_to_all(copies, ('xhi', 'y'), 0, 0)  20.8 us
    ppermute x4, waiting for transfers between devices, up(): return lax.ppermute(piece, 'z', [(i, (i + 1) % 8) for i in range(8)])  10.9 us
    ppermute x4, starting transfers between devices, down(): return lax.ppermute(piece, 'z', [(i, (i - 1) % 8) for i in range(8)])  10.3 us
    pallas_call x1, Pallas kernels, relayout(): pl.pallas_call(relayout_kernel, out_shape=pltpu.HBM((slots, d, b), jac.dt...  10.3 us
    all_to_all x1, starting transfers between devices, on_device(): got = lax.all_to_all(terms, ROW, 0, 0)  9.95 us
    pallas_call x1, Pallas kernels, make_terms(): pl.pallas_call(terms_kernel, out_shape=jax.ShapeDtypeStruct((k, b + 8, sl...  7.42 us
    ppermute x4, waiting for transfers between devices, across(): return lax.ppermute(piece, 'xlo', [(0, 1), (1, 0)])  4.4 us
  transfers between devices with their start and end apart: 14, of which 7 were waited for; matrix products, arithmetic and copies ran while one was open for 0% of the time, Pallas kernels for 9%

profile of v1, /device:TPU:2, one launch (start us, length us, event | category | flops | bytes accessed | tf_op | source)
XLA Modules:
  0.0 109.2 jit_solution(14971165357742166817)
XLA Ops:
  0.0 0.0 copy-start
  0.0 0.9 copy-done
  0.9 0.1 flip.1
  1.0 20.8 %all_to_all.10.own_ref = bf16[8,200,256]{2,1,0:T(8,128)(2,1)S(1)} all-to-all(bf16[8,200,256]{2,1,0:T(8,128)(2,1)S(1)} %flip.1), channel_id=1, replica_groups=mesh['xlo'=2,'z'=8,'xhi'=2,'y'=4,'core'=2] {'xhi','y'}, dimensions={0} | all-to-all | bytes 1638400 | tf_op jit(solution)/shard_map/all_to_all | solution.py:257
  21.8 0.0 collective-permute-start
  21.8 0.0 copy-start.1
  21.8 0.0 copy-start.2
  21.9 10.3 %relayout.1.jac_ref = bf16[128,200,200]{2,1,0:T(8,128)(2,1)} custom-call(bf16[200,200,128]{2,1,0:T(8,128)(2,1)} %bitcast.59), custom_call_target="tpu_custom_call" | custom-call | tf_op jit(solution)/shard_map/relayout/pallas_call | solution.py:97
  32.8 0.0 collective-permute-done.other_ref
  32.8 0.0 copy-done.1
  32.8 0.0 copy-done.2
  32.8 7.4 %terms.1 = s16[16,208,128]{2,1,0:T(8,128)(2,1)} custom-call(s32[128]{0:T(128)S(1)} %bitcast.57, s32[1,1]{1,0:T(1,128)S(6)} %copy.22.count_ref, s32[1,128]{1,0:T(1,128)S(1)} %bitcast.58, bf16[8,200,256]{2,1,0:T(8,128)(2,1)S(1)} %all_to_all.10.own_ref, bf16[8,200,256]{2,1,0:T(8,128)(2,1)S(1)} %collective-permute-done.other_ref, ...), custom_call_target="tpu_custom_call" | custom-call | tf_op jit(solution)/shard_map/terms/pallas_call | solution.py:171
  40.2 10.0 %all-to-all-start.1 = ((s16[16,208,128]{2,1,0:T(8,128)(2,1)}), s16[16,208,128]{2,1,0:T(8,128)(2,1)S(1)}, u32[]{:S(2)}, u32[]{:S(2)}) async-start(s16[16,208,128]{2,1,0:T(8,128)(2,1)} %terms.1), calls=%async_computation.1 | async-start | bytes 1703936 | tf_op jit(solution)/shard_map/all_to_all | solution.py:261
  50.2 22.3 %all-to-all-done.1.got_ref = s16[16,208,128]{2,1,0:T(8,128)(2,1)S(1)} async-done(((s16[16,208,128]{2,1,0:T(8,128)(2,1)}), s16[16,208,128]{2,1,0:T(8,128)(2,1)S(1)}, u32[]{:S(2)}, u32[]{:S(2)}) %all-to-all-start.1) | async-done | bytes 852000 | tf_op jit(solution)/shard_map/all_to_all | solution.py:261
  72.5 1.2 %add_up.1 = bf16[200,256]{1,0:T(8,128)(2,1)S(1)} custom-call(s16[16,208,128]{2,1,0:T(8,128)(2,1)S(1)} %all-to-all-done.1.got_ref), custom_call_target="tpu_custom_call" | custom-call | tf_op jit(solution)/shard_map/add_up/pallas_call | solution.py:211
  73.8 2.2 %collective-permute-start.1 = (bf16[200,256]{1,0:T(8,128)(2,1)S(1)}, bf16[200,256]{1,0:T(8,128)(2,1)S(1)}, u32[]{:S(2)}, u32[]{:S(2)}) collective-permute-start(bf16[200,256]{1,0:T(8,128)(2,1)S(1)} %add_up.1), channel_id=1, source_target_pairs={{0,16},{16,32},{32,48},{48,64},{64,80},{80,96},{96,112},{112,0},{1... | collective-permute-start | bytes 307208 | tf_op jit(solution)/shard_map/ppermute | solution.py:230
  76.0 1.1 %collective-permute-start.2 = (bf16[200,256]{1,0:T(8,128)(2,1)S(1)}, bf16[200,256]{1,0:T(8,128)(2,1)S(1)}, u32[]{:S(2)}, u32[]{:S(2)}) collective-permute-start(bf16[200,256]{1,0:T(8,128)(2,1)S(1)} %add_up.1), channel_id=1, source_target_pairs={{0,112},{16,0},{32,16},{48,32},{64,48},{80,64},{96,80},{112,96},{1... | collective-permute-start | bytes 307208 | tf_op jit(solution)/shard_map/ppermute | solution.py:233
  77.1 1.4 %collective-permute-start.3 = (bf16[200,256]{1,0:T(8,128)(2,1)S(1)}, bf16[200,256]{1,0:T(8,128)(2,1)S(1)}, u32[]{:S(2)}, u32[]{:S(2)}) collective-permute-start(bf16[200,256]{1,0:T(8,128)(2,1)S(1)} %add_up.1), channel_id=1, source_target_pairs={{0,128},{128,0},{1,129},{129,1},{2,130},{130,2},{3,131},{131,3},{4... | collective-permute-start | bytes 307208 | tf_op jit(solution)/shard_map/ppermute | solution.py:236
  78.5 0.1 broadcast_in_dim.33
  78.6 1.1 collective-permute-done.1
  79.7 0.9 collective-permute-done.2
  80.6 0.6 collective-permute-start.6
  81.3 0.1 collective-permute-start.4
  81.4 3.1 %collective-permute-start.5 = (bf16[200,256]{1,0:T(8,128)(2,1)S(1)}, bf16[200,256]{1,0:T(8,128)(2,1)S(1)}, u32[]{:S(2)}, u32[]{:S(2)}) collective-permute-start(bf16[200,256]{1,0:T(8,128)(2,1)S(1)} %collective-permute-done.2), channel_id=1, source_target_pairs={{0,112},{16,0},{32,16},{48,32},{64,48},{80,64},{96,80},{112,96},{1... | collective-permute-start | bytes 307208 | tf_op jit(solution)/shard_map/ppermute | solution.py:233
  84.6 0.0 collective-permute-done.3
  84.6 2.6 %collective-permute-done.4 = bf16[200,256]{1,0:T(8,128)(2,1)S(1)} collective-permute-done((bf16[200,256]{1,0:T(8,128)(2,1)S(1)}, bf16[200,256]{1,0:T(8,128)(2,1)S(1)}, u32[]{:S(2)}, u32[]{:S(2)}) %collective-permute-start.4) | collective-permute-done | bytes 102432 | tf_op jit(solution)/shard_map/ppermute | solution.py:230
  87.2 0.0 collective-permute-done.5
  87.2 1.6 %collective-permute-start.9 = (bf16[2,200,256]{2,1,0:T(8,128)(2,1)S(1)}, bf16[2,200,256]{2,1,0:T(8,128)(2,1)S(1)}, u32[]{:S(2)}, u32[]{:S(2)}) collective-permute-start(bf16[2,200,256]{2,1,0:T(8,128)(2,1)S(1)} %pad_maximum_fusion.1), channel_id=1, source_target_pairs={{0,128},{128,0},{1,129},{129,1},{2,130},{130,2},{3,131},{131,3},{4... | collective-permute-start | bytes 614408 | tf_op jit(solution)/shard_map/ppermute | solution.py:236
  88.8 0.6 collective-permute-start.7
  89.4 3.0 %collective-permute-start.8 = (bf16[200,256]{1,0:T(8,128)(2,1)S(1)}, bf16[200,256]{1,0:T(8,128)(2,1)S(1)}, u32[]{:S(2)}, u32[]{:S(2)}) collective-permute-start(bf16[200,256]{1,0:T(8,128)(2,1)S(1)} %collective-permute-done.5), channel_id=1, source_target_pairs={{0,112},{16,0},{32,16},{48,32},{64,48},{80,64},{96,80},{112,96},{1... | collective-permute-start | bytes 307208 | tf_op jit(solution)/shard_map/ppermute | solution.py:233
  92.4 0.0 collective-permute-done.6
  92.4 3.6 %collective-permute-done.7 = bf16[200,256]{1,0:T(8,128)(2,1)S(1)} collective-permute-done((bf16[200,256]{1,0:T(8,128)(2,1)S(1)}, bf16[200,256]{1,0:T(8,128)(2,1)S(1)}, u32[]{:S(2)}, u32[]{:S(2)}) %collective-permute-start.7) | collective-permute-done | bytes 102432 | tf_op jit(solution)/shard_map/ppermute | solution.py:230
  96.1 0.0 collective-permute-done.8
  96.1 0.0 collective-permute-done.9
  96.2 0.2 collective-permute-start.10
  96.4 3.1 %collective-permute-start.11 = (bf16[200,256]{1,0:T(8,128)(2,1)S(1)}, bf16[200,256]{1,0:T(8,128)(2,1)S(1)}, u32[]{:S(2)}, u32[]{:S(2)}) collective-permute-start(bf16[200,256]{1,0:T(8,128)(2,1)S(1)} %get-tuple-element.5), channel_id=1, source_target_pairs={{0,112},{16,0},{32,16},{48,32},{64,48},{80,64},{96,80},{112,96},{1... | collective-permute-start | bytes 307208 | tf_op jit(solution)/shard_map/ppermute | solution.py:233
  99.5 3.7 %collective-permute-done.10 = bf16[2,200,256]{2,1,0:T(8,128)(2,1)S(1)} collective-permute-done((bf16[2,200,256]{2,1,0:T(8,128)(2,1)S(1)}, bf16[2,200,256]{2,1,0:T(8,128)(2,1)S(1)}, u32[]{:S(2)}, u32[]{:S(2)}) %collective-permute-start.10) | collective-permute-done | bytes 204832 | tf_op jit(solution)/shard_map/ppermute | solution.py:230
  103.2 0.3 collective-permute-start.12
  103.6 0.0 collective-permute-done.11
  103.6 4.4 %collective-permute-done.12 = bf16[200,256]{1,0:T(8,128)(2,1)S(1)} collective-permute-done((bf16[200,256]{1,0:T(8,128)(2,1)S(1)}, bf16[200,256]{1,0:T(8,128)(2,1)S(1)}, u32[]{:S(2)}, u32[]{:S(2)}) %collective-permute-start.12) | collective-permute-done | bytes 102432 | tf_op jit(solution)/shard_map/ppermute | solution.py:236
  108.0 0.0 copy-start.3
  108.0 1.2 %copy-done.3 = bf16[2,8,200,256]{3,2,1,0:T(8,128)(2,1)} copy-done((bf16[2,8,200,256]{3,2,1,0:T(8,128)(2,1)}, bf16[2,8,200,256]{3,2,1,0:T(8,128)(2,1)S(1)}, u32[]{:S(2)}) %copy-start.3) | copy-done | bytes 1638424
  (21 shorter events, 0.3 us)
Async XLA Ops:
  0.0 0.9 copy-start
  21.8 10.9 %collective-permute-start = (bf16[8,200,256]{2,1,0:T(8,128)(2,1)S(1)}, bf16[8,200,256]{2,1,0:T(8,128)(2,1)S(1)}, u32[]{:S(2)}, u32[]{:S(2)}) collective-permute-start(bf16[8,200,256]{2,1,0:T(8,128)(2,1)S(1)} %all_to_all.10.own_ref), channel_id=1, source_target_pairs={{0,1},{1,0},{2,3},{3,2},{4,5},{5,4},{6,7},{7,6},{8,9},{9,8},{10,11... | collective-permute-start | bytes 2457608 | tf_op jit(solution)/shard_map/ppermute | solution.py:258
  21.8 10.9 %copy-start.1 = (s32[1,1,128]{2,1,0:T(1,128)S(1)}, s32[1,1,128]{2,1,0:T(1,128)}, u32[]{:S(2)}) copy-start(s32[1,1,128]{2,1,0:T(1,128)} %param.7) | copy-start | bytes 1540
  21.8 10.9 %copy-start.2 = (s32[1,1,128]{2,1,0:T(1,128)S(1)}, s32[1,1,128]{2,1,0:T(1,128)}, u32[]{:S(2)}) copy-start(s32[1,1,128]{2,1,0:T(1,128)} %param.8) | copy-start | bytes 1540
  40.2 32.3 %all-to-all-start.1 = ((s16[16,208,128]{2,1,0:T(8,128)(2,1)}), s16[16,208,128]{2,1,0:T(8,128)(2,1)S(1)}, u32[]{:S(2)}, u32[]{:S(2)}) async-start(s16[16,208,128]{2,1,0:T(8,128)(2,1)} %terms.1), calls=%async_computation.1 | async-start | bytes 1703936 | tf_op jit(solution)/shard_map/all_to_all | solution.py:261
  73.8 5.9 %collective-permute-start.1 = (bf16[200,256]{1,0:T(8,128)(2,1)S(1)}, bf16[200,256]{1,0:T(8,128)(2,1)S(1)}, u32[]{:S(2)}, u32[]{:S(2)}) collective-permute-start(bf16[200,256]{1,0:T(8,128)(2,1)S(1)} %add_up.1), channel_id=1, source_target_pairs={{0,16},{16,32},{32,48},{48,64},{64,80},{80,96},{96,112},{112,0},{1... | collective-permute-start | bytes 307208 | tf_op jit(solution)/shard_map/ppermute | solution.py:230
  76.0 4.7 %collective-permute-start.2 = (bf16[200,256]{1,0:T(8,128)(2,1)S(1)}, bf16[200,256]{1,0:T(8,128)(2,1)S(1)}, u32[]{:S(2)}, u32[]{:S(2)}) collective-permute-start(bf16[200,256]{1,0:T(8,128)(2,1)S(1)} %add_up.1), channel_id=1, source_target_pairs={{0,112},{16,0},{32,16},{48,32},{64,48},{80,64},{96,80},{112,96},{1... | collective-permute-start | bytes 307208 | tf_op jit(solution)/shard_map/ppermute | solution.py:233
  77.1 7.5 %collective-permute-start.3 = (bf16[200,256]{1,0:T(8,128)(2,1)S(1)}, bf16[200,256]{1,0:T(8,128)(2,1)S(1)}, u32[]{:S(2)}, u32[]{:S(2)}) collective-permute-start(bf16[200,256]{1,0:T(8,128)(2,1)S(1)} %add_up.1), channel_id=1, source_target_pairs={{0,128},{128,0},{1,129},{129,1},{2,130},{130,2},{3,131},{131,3},{4... | collective-permute-start | bytes 307208 | tf_op jit(solution)/shard_map/ppermute | solution.py:236
  80.6 11.7 %collective-permute-start.6 = (bf16[2,200,256]{2,1,0:T(8,128)(2,1)S(1)}, bf16[2,200,256]{2,1,0:T(8,128)(2,1)S(1)}, u32[]{:S(2)}, u32[]{:S(2)}) collective-permute-start(bf16[2,200,256]{2,1,0:T(8,128)(2,1)S(1)} %pad_maximum_fusion), channel_id=1, source_target_pairs={{0,128},{128,0},{1,129},{129,1},{2,130},{130,2},{3,131},{131,3},{4... | collective-permute-start | bytes 614408 | tf_op jit(solution)/shard_map/ppermute | solution.py:236
  81.3 5.9 %collective-permute-start.4 = (bf16[200,256]{1,0:T(8,128)(2,1)S(1)}, bf16[200,256]{1,0:T(8,128)(2,1)S(1)}, u32[]{:S(2)}, u32[]{:S(2)}) collective-permute-start(bf16[200,256]{1,0:T(8,128)(2,1)S(1)} %collective-permute-done.1), channel_id=1, source_target_pairs={{0,16},{16,32},{32,48},{48,64},{64,80},{80,96},{96,112},{112,0},{1... | collective-permute-start | bytes 307208 | tf_op jit(solution)/shard_map/ppermute | solution.py:230
  81.4 5.8 %collective-permute-start.5 = (bf16[200,256]{1,0:T(8,128)(2,1)S(1)}, bf16[200,256]{1,0:T(8,128)(2,1)S(1)}, u32[]{:S(2)}, u32[]{:S(2)}) collective-permute-start(bf16[200,256]{1,0:T(8,128)(2,1)S(1)} %collective-permute-done.2), channel_id=1, source_target_pairs={{0,112},{16,0},{32,16},{48,32},{64,48},{80,64},{96,80},{112,96},{1... | collective-permute-start | bytes 307208 | tf_op jit(solution)/shard_map/ppermute | solution.py:233
  87.2 8.9 %collective-permute-start.9 = (bf16[2,200,256]{2,1,0:T(8,128)(2,1)S(1)}, bf16[2,200,256]{2,1,0:T(8,128)(2,1)S(1)}, u32[]{:S(2)}, u32[]{:S(2)}) collective-permute-start(bf16[2,200,256]{2,1,0:T(8,128)(2,1)S(1)} %pad_maximum_fusion.1), channel_id=1, source_target_pairs={{0,128},{128,0},{1,129},{129,1},{2,130},{130,2},{3,131},{131,3},{4... | collective-permute-start | bytes 614408 | tf_op jit(solution)/shard_map/ppermute | solution.py:236
  88.8 7.2 %collective-permute-start.7 = (bf16[200,256]{1,0:T(8,128)(2,1)S(1)}, bf16[200,256]{1,0:T(8,128)(2,1)S(1)}, u32[]{:S(2)}, u32[]{:S(2)}) collective-permute-start(bf16[200,256]{1,0:T(8,128)(2,1)S(1)} %collective-permute-done.4), channel_id=1, source_target_pairs={{0,16},{16,32},{32,48},{48,64},{64,80},{80,96},{96,112},{112,0},{1... | collective-permute-start | bytes 307208 | tf_op jit(solution)/shard_map/ppermute | solution.py:230
  89.4 6.7 %collective-permute-start.8 = (bf16[200,256]{1,0:T(8,128)(2,1)S(1)}, bf16[200,256]{1,0:T(8,128)(2,1)S(1)}, u32[]{:S(2)}, u32[]{:S(2)}) collective-permute-start(bf16[200,256]{1,0:T(8,128)(2,1)S(1)} %collective-permute-done.5), channel_id=1, source_target_pairs={{0,112},{16,0},{32,16},{48,32},{64,48},{80,64},{96,80},{112,96},{1... | collective-permute-start | bytes 307208 | tf_op jit(solution)/shard_map/ppermute | solution.py:233
  96.2 7.0 %collective-permute-start.10 = (bf16[2,200,256]{2,1,0:T(8,128)(2,1)S(1)}, bf16[2,200,256]{2,1,0:T(8,128)(2,1)S(1)}, u32[]{:S(2)}, u32[]{:S(2)}) collective-permute-start(bf16[2,200,256]{2,1,0:T(8,128)(2,1)S(1)} %pad_maximum_fusion.2), channel_id=1, source_target_pairs={{0,16},{16,32},{32,48},{48,64},{64,80},{80,96},{96,112},{112,0},{1... | collective-permute-start | bytes 614408 | tf_op jit(solution)/shard_map/ppermute | solution.py:230
  96.4 7.2 %collective-permute-start.11 = (bf16[200,256]{1,0:T(8,128)(2,1)S(1)}, bf16[200,256]{1,0:T(8,128)(2,1)S(1)}, u32[]{:S(2)}, u32[]{:S(2)}) collective-permute-start(bf16[200,256]{1,0:T(8,128)(2,1)S(1)} %get-tuple-element.5), channel_id=1, source_target_pairs={{0,112},{16,0},{32,16},{48,32},{64,48},{80,64},{96,80},{112,96},{1... | collective-permute-start | bytes 307208 | tf_op jit(solution)/shard_map/ppermute | solution.py:233
  103.2 4.7 %collective-permute-start.12 = (bf16[200,256]{1,0:T(8,128)(2,1)S(1)}, bf16[200,256]{1,0:T(8,128)(2,1)S(1)}, u32[]{:S(2)}, u32[]{:S(2)}) collective-permute-start(bf16[200,256]{1,0:T(8,128)(2,1)S(1)} %slice_bitcast_fusion.3), channel_id=1, source_target_pairs={{0,128},{128,0},{1,129},{129,1},{2,130},{130,2},{3,131},{131,3},{4... | collective-permute-start | bytes 307208 | tf_op jit(solution)/shard_map/ppermute | solution.py:236
  108.0 1.2 %copy-start.3 = (bf16[2,8,200,256]{3,2,1,0:T(8,128)(2,1)}, bf16[2,8,200,256]{3,2,1,0:T(8,128)(2,1)S(1)}, u32[]{:S(2)}) copy-start(bf16[2,8,200,256]{3,2,1,0:T(8,128)(2,1)S(1)} %bitcast_dynamic-update-slice_fusion) | copy-start | bytes 4915204

commit v2 on v1

--- a/solution.py
+++ b/solution.py
@@ -235,15 +235,23 @@
     def across(piece):
         return lax.ppermute(piece, "xlo", [(0, 1), (1, 0)])
 
+    def corner(piece):
+        pairs = [(x * 8 + i, (1 - x) * 8 + (i + 1) % 8) for x in range(2) for i in range(8)]
+        return lax.ppermute(piece, ROW, pairs)
+
+    def both(one, two):
+        return jnp.stack([one, two])
+
     held = {(0, 0): mine}
-    held[0, -1], held[0, 1], held[1, 0] = up(mine), down(mine), across(mine)
+    held[0, -1], held[0, 1] = up(mine), down(mine)
+    held[1, 0] = across(mine)
     held[0, -2], held[0, 2] = up(held[0, -1]), down(held[0, 1])
-    held[1, -1], held[1, 1] = across(jnp.stack([held[0, -1], held[0, 1]]))
+    held[1, -1], held[1, 1] = across(both(held[0, -1], held[0, 1]))
     held[0, -3], held[0, 3] = up(held[0, -2]), down(held[0, 2])
-    held[1, -2], held[1, 2] = across(jnp.stack([held[0, -2], held[0, 2]]))
-    held[1, -3], held[0, 4] = up(jnp.stack([held[1, -2], held[0, -3]]))
-    held[1, 3] = down(held[1, 2])
-    held[1, 4] = across(held[0, 4])
+    held[1, -2], held[1, 2] = across(both(held[0, -2], held[0, 2]))
+    held[1, -3], held[1, 3] = across(both(held[0, -3], held[0, 3]))
+    held[0, 4] = down(held[0, 3])
+    held[1, -4] = corner(held[0, -3])
     out = jnp.zeros((2, 8) + mine.shape, mine.dtype)
     for (x, d), piece in held.items():
         out = lax.dynamic_update_slice(out, piece[None, None], (xlo ^ x, (z + d + 8) % 8, 0, 0))

time: 109 us -> 108 us (level)
  waiting for transfers between devices: 38.6 us -> 36 us
    ppermute x4 -> x3, waiting for transfers between devices: 10.9 us -> 6.16 us  [up(): return lax.ppermute(piece, 'z', [(i, (i + 1) % 8) for i in range(8)])]
    ppermute x0 -> x1, waiting for transfers between devices: none -> 4.5 us  [corner(): return lax.ppermute(piece, ROW, pairs)]
    ppermute x4, waiting for transfers between devices: 4.4 us -> 1.23 us  [across(): return lax.ppermute(piece, 'xlo', [(0, 1), (1, 0)])]
    ppermute x4 -> x3, starting transfers between devices: 3.07 us -> 2.83 us  [up(): return lax.ppermute(piece, 'z', [(i, (i + 1) % 8) for i in range(8)])]
  transfers between devices with their start and end apart: 14 -> 14, of which waited for: 7 -> 8; matrix products, arithmetic and copies ran while one was open for 0% -> 0% of each run, Pallas kernels for 9% -> 10%
where the time goes in v2:
time: 108 us; the launch traced here: 107 us
  waiting for transfers between devices  36 us (33%)
  starting transfers between devices  28.3 us (26%)
  blocking collectives  20.8 us (19%)
  Pallas kernels  19 us (18%)
  local copies, waits for them, and re-layouts  2.41 us (2%)
    all_to_all x1, waiting for transfers between devices, on_device(): got = lax.all_to_all(terms, ROW, 0, 0)  22.3 us
    all_to_all x1, blocking collectives, on_device(): own = lax.all_to_all(copies, ('xhi', 'y'), 0, 0)  20.8 us
    ppermute x4, starting transfers between devices, down(): return lax.ppermute(piece, 'z', [(i, (i - 1) % 8) for i in range(8)])  10.9 us
    pallas_call x1, Pallas kernels, relayout(): pl.pallas_call(relayout_kernel, out_shape=pltpu.HBM((slots, d, b), jac.dt...  10.3 us
    all_to_all x1, starting transfers between devices, on_device(): got = lax.all_to_all(terms, ROW, 0, 0)  9.95 us
    pallas_call x1, Pallas kernels, make_terms(): pl.pallas_call(terms_kernel, out_shape=jax.ShapeDtypeStruct((k, b + 8, sl...  7.42 us
    ppermute x3, waiting for transfers between devices, up(): return lax.ppermute(piece, 'z', [(i, (i + 1) % 8) for i in range(8)])  6.16 us
    ppermute x4, starting transfers between devices, across(): return lax.ppermute(piece, 'xlo', [(0, 1), (1, 0)])  4.55 us
  transfers between devices with their start and end apart: 14, of which 8 were waited for; matrix products, arithmetic and copies ran while one was open for 0% of the time, Pallas kernels for 10%

profile of v2, /device:TPU:2, one launch (start us, length us, event | category | flops | bytes accessed | tf_op | source)
XLA Modules:
  0.0 107.5 jit_solution(16944790705948465220)
XLA Ops:
  0.0 0.0 copy-start
  0.0 0.9 copy-done
  0.9 0.1 flip.1
  1.0 20.8 %all_to_all.10.own_ref = bf16[8,200,256]{2,1,0:T(8,128)(2,1)S(1)} all-to-all(bf16[8,200,256]{2,1,0:T(8,128)(2,1)S(1)} %flip.1), channel_id=1, replica_groups=mesh['xlo'=2,'z'=8,'xhi'=2,'y'=4,'core'=2] {'xhi','y'}, dimensions={0} | all-to-all | bytes 1638400 | tf_op jit(solution)/shard_map/all_to_all | solution.py:265
  21.8 0.0 collective-permute-start
  21.8 0.0 copy-start.1
  21.8 0.0 copy-start.2
  21.9 10.3 %relayout.1.jac_ref = bf16[128,200,200]{2,1,0:T(8,128)(2,1)} custom-call(bf16[200,200,128]{2,1,0:T(8,128)(2,1)} %bitcast.62), custom_call_target="tpu_custom_call" | custom-call | tf_op jit(solution)/shard_map/relayout/pallas_call | solution.py:97
  32.8 0.0 collective-permute-done.other_ref
  32.8 0.0 copy-done.1
  32.8 0.0 copy-done.2
  32.8 7.4 %terms.1 = s16[16,208,128]{2,1,0:T(8,128)(2,1)} custom-call(s32[128]{0:T(128)S(1)} %bitcast.60, s32[1,1]{1,0:T(1,128)S(6)} %copy.22.count_ref, s32[1,128]{1,0:T(1,128)S(1)} %bitcast.61, bf16[8,200,256]{2,1,0:T(8,128)(2,1)S(1)} %all_to_all.10.own_ref, bf16[8,200,256]{2,1,0:T(8,128)(2,1)S(1)} %collective-permute-done.other_ref, ...), custom_call_target="tpu_custom_call" | custom-call | tf_op jit(solution)/shard_map/terms/pallas_call | solution.py:171
  40.2 10.0 %all-to-all-start.1 = ((s16[16,208,128]{2,1,0:T(8,128)(2,1)}), s16[16,208,128]{2,1,0:T(8,128)(2,1)S(1)}, u32[]{:S(2)}, u32[]{:S(2)}) async-start(s16[16,208,128]{2,1,0:T(8,128)(2,1)} %terms.1), calls=%async_computation.1 | async-start | bytes 1703936 | tf_op jit(solution)/shard_map/all_to_all | solution.py:269
  50.2 22.3 %all-to-all-done.1.got_ref = s16[16,208,128]{2,1,0:T(8,128)(2,1)S(1)} async-done(((s16[16,208,128]{2,1,0:T(8,128)(2,1)}), s16[16,208,128]{2,1,0:T(8,128)(2,1)S(1)}, u32[]{:S(2)}, u32[]{:S(2)}) %all-to-all-start.1) | async-done | bytes 852000 | tf_op jit(solution)/shard_map/all_to_all | solution.py:269
  72.5 1.2 %add_up.1 = bf16[200,256]{1,0:T(8,128)(2,1)S(1)} custom-call(s16[16,208,128]{2,1,0:T(8,128)(2,1)S(1)} %all-to-all-done.1.got_ref), custom_call_target="tpu_custom_call" | custom-call | tf_op jit(solution)/shard_map/add_up/pallas_call | solution.py:211
  73.8 2.2 %collective-permute-start.1 = (bf16[200,256]{1,0:T(8,128)(2,1)S(1)}, bf16[200,256]{1,0:T(8,128)(2,1)S(1)}, u32[]{:S(2)}, u32[]{:S(2)}) collective-permute-start(bf16[200,256]{1,0:T(8,128)(2,1)S(1)} %add_up.1), channel_id=1, source_target_pairs={{0,16},{16,32},{32,48},{48,64},{64,80},{80,96},{96,112},{112,0},{1... | collective-permute-start | bytes 307208 | tf_op jit(solution)/shard_map/ppermute | solution.py:230
  76.0 1.1 %collective-permute-start.2 = (bf16[200,256]{1,0:T(8,128)(2,1)S(1)}, bf16[200,256]{1,0:T(8,128)(2,1)S(1)}, u32[]{:S(2)}, u32[]{:S(2)}) collective-permute-start(bf16[200,256]{1,0:T(8,128)(2,1)S(1)} %add_up.1), channel_id=1, source_target_pairs={{0,112},{16,0},{32,16},{48,32},{64,48},{80,64},{96,80},{112,96},{1... | collective-permute-start | bytes 307208 | tf_op jit(solution)/shard_map/ppermute | solution.py:233
  77.1 1.4 %collective-permute-start.3 = (bf16[200,256]{1,0:T(8,128)(2,1)S(1)}, bf16[200,256]{1,0:T(8,128)(2,1)S(1)}, u32[]{:S(2)}, u32[]{:S(2)}) collective-permute-start(bf16[200,256]{1,0:T(8,128)(2,1)S(1)} %add_up.1), channel_id=1, source_target_pairs={{0,128},{128,0},{1,129},{129,1},{2,130},{130,2},{3,131},{131,3},{4... | collective-permute-start | bytes 307208 | tf_op jit(solution)/shard_map/ppermute | solution.py:236
  78.5 0.1 broadcast_in_dim.33
  78.7 1.1 collective-permute-done.1
  79.7 0.9 collective-permute-done.2
  80.6 0.6 collective-permute-start.6
  81.3 0.1 collective-permute-start.4
  81.4 3.1 %collective-permute-start.5 = (bf16[200,256]{1,0:T(8,128)(2,1)S(1)}, bf16[200,256]{1,0:T(8,128)(2,1)S(1)}, u32[]{:S(2)}, u32[]{:S(2)}) collective-permute-start(bf16[200,256]{1,0:T(8,128)(2,1)S(1)} %collective-permute-done.2), channel_id=1, source_target_pairs={{0,112},{16,0},{32,16},{48,32},{64,48},{80,64},{96,80},{112,96},{1... | collective-permute-start | bytes 307208 | tf_op jit(solution)/shard_map/ppermute | solution.py:233
  84.6 0.0 collective-permute-done.3
  84.6 2.6 %collective-permute-done.4 = bf16[200,256]{1,0:T(8,128)(2,1)S(1)} collective-permute-done((bf16[200,256]{1,0:T(8,128)(2,1)S(1)}, bf16[200,256]{1,0:T(8,128)(2,1)S(1)}, u32[]{:S(2)}, u32[]{:S(2)}) %collective-permute-start.4) | collective-permute-done | bytes 102432 | tf_op jit(solution)/shard_map/ppermute | solution.py:230
  87.2 0.0 collective-permute-done.5
  87.2 1.6 %collective-permute-start.9 = (bf16[2,200,256]{2,1,0:T(8,128)(2,1)S(1)}, bf16[2,200,256]{2,1,0:T(8,128)(2,1)S(1)}, u32[]{:S(2)}, u32[]{:S(2)}) collective-permute-start(bf16[2,200,256]{2,1,0:T(8,128)(2,1)S(1)} %pad_maximum_fusion.1), channel_id=1, source_target_pairs={{0,128},{128,0},{1,129},{129,1},{2,130},{130,2},{3,131},{131,3},{4... | collective-permute-start | bytes 614408 | tf_op jit(solution)/shard_map/ppermute | solution.py:236
  88.8 0.5 collective-permute-start.7
  89.4 3.0 %collective-permute-start.8 = (bf16[200,256]{1,0:T(8,128)(2,1)S(1)}, bf16[200,256]{1,0:T(8,128)(2,1)S(1)}, u32[]{:S(2)}, u32[]{:S(2)}) collective-permute-start(bf16[200,256]{1,0:T(8,128)(2,1)S(1)} %collective-permute-done.5), channel_id=1, source_target_pairs={{0,112},{16,0},{32,16},{48,32},{64,48},{80,64},{96,80},{112,96},{1... | collective-permute-start | bytes 307208 | tf_op jit(solution)/shard_map/ppermute | solution.py:233
  92.4 0.0 collective-permute-done.6
  92.5 2.5 %collective-permute-done.7 = bf16[200,256]{1,0:T(8,128)(2,1)S(1)} collective-permute-done((bf16[200,256]{1,0:T(8,128)(2,1)S(1)}, bf16[200,256]{1,0:T(8,128)(2,1)S(1)}, u32[]{:S(2)}, u32[]{:S(2)}) %collective-permute-start.7) | collective-permute-done | bytes 102432 | tf_op jit(solution)/shard_map/ppermute | solution.py:230
  95.0 0.0 collective-permute-done.8
  95.0 0.8 collective-permute-start.10
  95.8 3.7 %collective-permute-start.11 = (bf16[200,256]{1,0:T(8,128)(2,1)S(1)}, bf16[200,256]{1,0:T(8,128)(2,1)S(1)}, u32[]{:S(2)}, u32[]{:S(2)}) collective-permute-start(bf16[200,256]{1,0:T(8,128)(2,1)S(1)} %collective-permute-done.8), channel_id=1, source_target_pairs={{0,112},{16,0},{32,16},{48,32},{64,48},{80,64},{96,80},{112,96},{1... | collective-permute-start | bytes 307208 | tf_op jit(solution)/shard_map/ppermute | solution.py:233
  99.5 0.0 collective-permute-start.12
  99.6 0.0 collective-permute-done.9
  99.6 1.2 %collective-permute-done.10 = bf16[2,200,256]{2,1,0:T(8,128)(2,1)S(1)} collective-permute-done((bf16[2,200,256]{2,1,0:T(8,128)(2,1)S(1)}, bf16[2,200,256]{2,1,0:T(8,128)(2,1)S(1)}, u32[]{:S(2)}, u32[]{:S(2)}) %collective-permute-start.10) | collective-permute-done | bytes 204832 | tf_op jit(solution)/shard_map/ppermute | solution.py:236
  100.9 0.9 collective-permute-done.11
  101.8 4.5 %collective-permute-done.12 = bf16[200,256]{1,0:T(8,128)(2,1)S(1)} collective-permute-done((bf16[200,256]{1,0:T(8,128)(2,1)S(1)}, bf16[200,256]{1,0:T(8,128)(2,1)S(1)}, u32[]{:S(2)}, u32[]{:S(2)}) %collective-permute-start.12) | collective-permute-done | bytes 102432 | tf_op jit(solution)/shard_map/ppermute | solution.py:240
  106.3 0.0 copy-start.3
  106.3 1.2 %copy-done.3 = bf16[2,8,200,256]{3,2,1,0:T(8,128)(2,1)} copy-done((bf16[2,8,200,256]{3,2,1,0:T(8,128)(2,1)}, bf16[2,8,200,256]{3,2,1,0:T(8,128)(2,1)S(1)}, u32[]{:S(2)}) %copy-start.3) | copy-done | bytes 1638424
  (19 shorter events, 0.3 us)
Async XLA Ops:
  0.0 0.9 copy-start
  21.8 10.9 %collective-permute-start = (bf16[8,200,256]{2,1,0:T(8,128)(2,1)S(1)}, bf16[8,200,256]{2,1,0:T(8,128)(2,1)S(1)}, u32[]{:S(2)}, u32[]{:S(2)}) collective-permute-start(bf16[8,200,256]{2,1,0:T(8,128)(2,1)S(1)} %all_to_all.10.own_ref), channel_id=1, source_target_pairs={{0,1},{1,0},{2,3},{3,2},{4,5},{5,4},{6,7},{7,6},{8,9},{9,8},{10,11... | collective-permute-start | bytes 2457608 | tf_op jit(solution)/shard_map/ppermute | solution.py:266
  21.8 10.9 %copy-start.1 = (s32[1,1,128]{2,1,0:T(1,128)S(1)}, s32[1,1,128]{2,1,0:T(1,128)}, u32[]{:S(2)}) copy-start(s32[1,1,128]{2,1,0:T(1,128)} %param.7) | copy-start | bytes 1540
  21.8 10.9 %copy-start.2 = (s32[1,1,128]{2,1,0:T(1,128)S(1)}, s32[1,1,128]{2,1,0:T(1,128)}, u32[]{:S(2)}) copy-start(s32[1,1,128]{2,1,0:T(1,128)} %param.8) | copy-start | bytes 1540
  40.2 32.3 %all-to-all-start.1 = ((s16[16,208,128]{2,1,0:T(8,128)(2,1)}), s16[16,208,128]{2,1,0:T(8,128)(2,1)S(1)}, u32[]{:S(2)}, u32[]{:S(2)}) async-start(s16[16,208,128]{2,1,0:T(8,128)(2,1)} %terms.1), calls=%async_computation.1 | async-start | bytes 1703936 | tf_op jit(solution)/shard_map/all_to_all | solution.py:269
  73.8 5.9 %collective-permute-start.1 = (bf16[200,256]{1,0:T(8,128)(2,1)S(1)}, bf16[200,256]{1,0:T(8,128)(2,1)S(1)}, u32[]{:S(2)}, u32[]{:S(2)}) collective-permute-start(bf16[200,256]{1,0:T(8,128)(2,1)S(1)} %add_up.1), channel_id=1, source_target_pairs={{0,16},{16,32},{32,48},{48,64},{64,80},{80,96},{96,112},{112,0},{1... | collective-permute-start | bytes 307208 | tf_op jit(solution)/shard_map/ppermute | solution.py:230
  76.0 4.7 %collective-permute-start.2 = (bf16[200,256]{1,0:T(8,128)(2,1)S(1)}, bf16[200,256]{1,0:T(8,128)(2,1)S(1)}, u32[]{:S(2)}, u32[]{:S(2)}) collective-permute-start(bf16[200,256]{1,0:T(8,128)(2,1)S(1)} %add_up.1), channel_id=1, source_target_pairs={{0,112},{16,0},{32,16},{48,32},{64,48},{80,64},{96,80},{112,96},{1... | collective-permute-start | bytes 307208 | tf_op jit(solution)/shard_map/ppermute | solution.py:233
  77.1 7.5 %collective-permute-start.3 = (bf16[200,256]{1,0:T(8,128)(2,1)S(1)}, bf16[200,256]{1,0:T(8,128)(2,1)S(1)}, u32[]{:S(2)}, u32[]{:S(2)}) collective-permute-start(bf16[200,256]{1,0:T(8,128)(2,1)S(1)} %add_up.1), channel_id=1, source_target_pairs={{0,128},{128,0},{1,129},{129,1},{2,130},{130,2},{3,131},{131,3},{4... | collective-permute-start | bytes 307208 | tf_op jit(solution)/shard_map/ppermute | solution.py:236
  80.6 11.7 %collective-permute-start.6 = (bf16[2,200,256]{2,1,0:T(8,128)(2,1)S(1)}, bf16[2,200,256]{2,1,0:T(8,128)(2,1)S(1)}, u32[]{:S(2)}, u32[]{:S(2)}) collective-permute-start(bf16[2,200,256]{2,1,0:T(8,128)(2,1)S(1)} %pad_maximum_fusion), channel_id=1, source_target_pairs={{0,128},{128,0},{1,129},{129,1},{2,130},{130,2},{3,131},{131,3},{4... | collective-permute-start | bytes 614408 | tf_op jit(solution)/shard_map/ppermute | solution.py:236
  81.3 5.9 %collective-permute-start.4 = (bf16[200,256]{1,0:T(8,128)(2,1)S(1)}, bf16[200,256]{1,0:T(8,128)(2,1)S(1)}, u32[]{:S(2)}, u32[]{:S(2)}) collective-permute-start(bf16[200,256]{1,0:T(8,128)(2,1)S(1)} %collective-permute-done.1), channel_id=1, source_target_pairs={{0,16},{16,32},{32,48},{48,64},{64,80},{80,96},{96,112},{112,0},{1... | collective-permute-start | bytes 307208 | tf_op jit(solution)/shard_map/ppermute | solution.py:230
  81.4 5.8 %collective-permute-start.5 = (bf16[200,256]{1,0:T(8,128)(2,1)S(1)}, bf16[200,256]{1,0:T(8,128)(2,1)S(1)}, u32[]{:S(2)}, u32[]{:S(2)}) collective-permute-start(bf16[200,256]{1,0:T(8,128)(2,1)S(1)} %collective-permute-done.2), channel_id=1, source_target_pairs={{0,112},{16,0},{32,16},{48,32},{64,48},{80,64},{96,80},{112,96},{1... | collective-permute-start | bytes 307208 | tf_op jit(solution)/shard_map/ppermute | solution.py:233
  87.2 12.4 %collective-permute-start.9 = (bf16[2,200,256]{2,1,0:T(8,128)(2,1)S(1)}, bf16[2,200,256]{2,1,0:T(8,128)(2,1)S(1)}, u32[]{:S(2)}, u32[]{:S(2)}) collective-permute-start(bf16[2,200,256]{2,1,0:T(8,128)(2,1)S(1)} %pad_maximum_fusion.1), channel_id=1, source_target_pairs={{0,128},{128,0},{1,129},{129,1},{2,130},{130,2},{3,131},{131,3},{4... | collective-permute-start | bytes 614408 | tf_op jit(solution)/shard_map/ppermute | solution.py:236
  88.8 6.1 %collective-permute-start.7 = (bf16[200,256]{1,0:T(8,128)(2,1)S(1)}, bf16[200,256]{1,0:T(8,128)(2,1)S(1)}, u32[]{:S(2)}, u32[]{:S(2)}) collective-permute-start(bf16[200,256]{1,0:T(8,128)(2,1)S(1)} %collective-permute-done.4), channel_id=1, source_target_pairs={{0,16},{16,32},{32,48},{48,64},{64,80},{80,96},{96,112},{112,0},{1... | collective-permute-start | bytes 307208 | tf_op jit(solution)/shard_map/ppermute | solution.py:230
  89.4 5.6 %collective-permute-start.8 = (bf16[200,256]{1,0:T(8,128)(2,1)S(1)}, bf16[200,256]{1,0:T(8,128)(2,1)S(1)}, u32[]{:S(2)}, u32[]{:S(2)}) collective-permute-start(bf16[200,256]{1,0:T(8,128)(2,1)S(1)} %collective-permute-done.5), channel_id=1, source_target_pairs={{0,112},{16,0},{32,16},{48,32},{64,48},{80,64},{96,80},{112,96},{1... | collective-permute-start | bytes 307208 | tf_op jit(solution)/shard_map/ppermute | solution.py:233
  95.0 5.8 %collective-permute-start.10 = (bf16[2,200,256]{2,1,0:T(8,128)(2,1)S(1)}, bf16[2,200,256]{2,1,0:T(8,128)(2,1)S(1)}, u32[]{:S(2)}, u32[]{:S(2)}) collective-permute-start(bf16[2,200,256]{2,1,0:T(8,128)(2,1)S(1)} %pad_maximum_fusion.2), channel_id=1, source_target_pairs={{0,128},{128,0},{1,129},{129,1},{2,130},{130,2},{3,131},{131,3},{4... | collective-permute-start | bytes 614408 | tf_op jit(solution)/shard_map/ppermute | solution.py:236
  95.8 5.9 %collective-permute-start.11 = (bf16[200,256]{1,0:T(8,128)(2,1)S(1)}, bf16[200,256]{1,0:T(8,128)(2,1)S(1)}, u32[]{:S(2)}, u32[]{:S(2)}) collective-permute-start(bf16[200,256]{1,0:T(8,128)(2,1)S(1)} %collective-permute-done.8), channel_id=1, source_target_pairs={{0,112},{16,0},{32,16},{48,32},{64,48},{80,64},{96,80},{112,96},{1... | collective-permute-start | bytes 307208 | tf_op jit(solution)/shard_map/ppermute | solution.py:233
  99.5 6.8 %collective-permute-start.12 = (bf16[200,256]{1,0:T(8,128)(2,1)S(1)}, bf16[200,256]{1,0:T(8,128)(2,1)S(1)}, u32[]{:S(2)}, u32[]{:S(2)}) collective-permute-start(bf16[200,256]{1,0:T(8,128)(2,1)S(1)} %collective-permute-done.7), channel_id=1, source_target_pairs={{0,144},{16,160},{32,176},{48,192},{64,208},{80,224},{96,240},{112... | collective-permute-start | bytes 307208 | tf_op jit(solution)/shard_map/ppermute | solution.py:240
  106.3 1.2 %copy-start.3 = (bf16[2,8,200,256]{3,2,1,0:T(8,128)(2,1)}, bf16[2,8,200,256]{3,2,1,0:T(8,128)(2,1)S(1)}, u32[]{:S(2)}) copy-start(bf16[2,8,200,256]{3,2,1,0:T(8,128)(2,1)S(1)} %bitcast_dynamic-update-slice_fusion) | copy-start | bytes 4915204

commit v3 on v2

--- a/solution.py
+++ b/solution.py
@@ -38,22 +38,39 @@
     return pltpu.CompilerParams(vmem_limit_bytes=mib << 20)
 
 
-def flip_kernel(in_ref, out_ref):
-    flipped = jnp.transpose(in_ref[...])
-    for i in range(out_ref.shape[0]):
-        out_ref[i] = flipped
+def flip_kernel(in_ref, out_ref, in_buf, out_buf, in_sem, out_sem):
+    bring = pltpu.make_async_copy(in_ref, in_buf, in_sem)
+    bring.start()
+    bring.wait()
+    out_buf[...] = jnp.transpose(in_buf[...])
+
+    def send(i):
+        return pltpu.make_async_copy(out_buf, out_ref.at[i], out_sem.at[i])
+
+    copies = out_ref.shape[0]
+    for i in range(copies):
+        send(i).start()
+    for i in range(copies):
+        send(i).wait()
 
 
 def flip(faces, copies):
     rows, b = faces.shape
+    anywhere = pl.BlockSpec(memory_space=pltpu.HBM)
     return pl.pallas_call(
         flip_kernel,
-        out_shape=pltpu.VMEM((copies, b, rows), faces.dtype),
-        in_specs=[in_vmem()],
-        out_specs=in_vmem(),
+        out_shape=pltpu.HBM((copies, b, rows), faces.dtype),
+        in_specs=[anywhere],
+        out_specs=anywhere,
+        scratch_shapes=[
+            pltpu.VMEM((rows, b), faces.dtype),
+            pltpu.VMEM((b, rows), faces.dtype),
+            pltpu.SemaphoreType.DMA,
+            pltpu.SemaphoreType.DMA((copies,)),
+        ],
         compiler_params=params(),
         name="flip",
-    )(faces)
+    )(in_hbm(faces))
 
 
 def relayout_kernel(jac_ref, out_ref, in_buf, out_buf, left_ref, right_ref, in_sem, out_sem):
@@ -117,16 +134,19 @@
 
 
 def terms_kernel(
-    rows_ref, count_ref, cols_ref, own_ref, other_ref, jac_ref, out_ref, jac_buf, faces_ref, left_ref, right_ref, sem
+    rows_ref, count_ref, cols_ref, own_ref, other_ref, jac_ref, out_ref, jac_buf, faces_ref, left_ref, right_ref, out_buf, sem, out_sem
 ):
     slots, b, _ = jac_buf.shape
-    k = out_ref.shape[0]
+    k = out_buf.shape[0]
     pieces, _, per = own_ref.shape
     core = lax.axis_index("core")
 
     def bring(c):
         at = pl.ds(c * GROUP, GROUP)
         return pltpu.make_async_copy(jac_ref.at[at], jac_buf.at[at], sem.at[c])
+
+    def send(i):
+        return pltpu.make_async_copy(out_buf.at[i], out_ref.at[i], out_sem.at[i])
 
     for c in range(slots // GROUP):
         bring(c).start()
@@ -161,7 +181,10 @@
         exponent = jnp.ceil(jnp.log2(jnp.maximum(top, TINY)) + 0.01) - BITS
         scaled = jnp.clip(jnp.round(flipped * pow2(-exponent)), -LIMIT, LIMIT)
         meta = jnp.where(meta_row == 0, exponent, jnp.where(meta_row == 1, cols, 0.0))
-        out_ref[i] = jnp.concatenate([scaled, meta], axis=0).astype(jnp.int32).astype(jnp.int16)
+        out_buf[i] = jnp.concatenate([scaled, meta], axis=0).astype(jnp.int32).astype(jnp.int16)
+        send(i).start()
+    for i in range(k):
+        send(i).wait()
 
 
 def make_terms(rows, count, cols, own, other, jac, k):
@@ -170,15 +193,17 @@
     scratch = pltpu.VMEM((slots * TERM_PITCH, LANES), jnp.float32)
     return pl.pallas_call(
         terms_kernel,
-        out_shape=jax.ShapeDtypeStruct((k, b + 8, slots), jnp.int16),
+        out_shape=pltpu.HBM((k, b + 8, slots), jnp.int16),
         in_specs=[in_smem(), in_smem(), in_vmem(), in_vmem(), in_vmem(), pl.BlockSpec(memory_space=pltpu.HBM)],
-        out_specs=in_vmem(),
+        out_specs=pl.BlockSpec(memory_space=pltpu.HBM),
         scratch_shapes=[
             pltpu.VMEM((slots, b, b), jac.dtype),
             pltpu.VMEM((2 * pieces * per, 2 * LANES), jnp.bfloat16),
             scratch,
             scratch,
+            pltpu.VMEM((k, b + 8, slots), jnp.int16),
             pltpu.SemaphoreType.DMA((slots // GROUP,)),
+            pltpu.SemaphoreType.DMA((k,)),
         ],
         compiler_params=params(32),
         name="terms",
@@ -249,9 +274,10 @@
     held[1, -1], held[1, 1] = across(both(held[0, -1], held[0, 1]))
     held[0, -3], held[0, 3] = up(held[0, -2]), down(held[0, 2])
     held[1, -2], held[1, 2] = across(both(held[0, -2], held[0, 2]))
-    held[1, -3], held[1, 3] = across(both(held[0, -3], held[0, 3]))
+    held[1, -4] = corner(held[0, -3])
     held[0, 4] = down(held[0, 3])
-    held[1, -4] = corner(held[0, -3])
+    held[1, 3] = across(held[0, 3])
+    held[1, -3] = up(held[1, -2])
     out = jnp.zeros((2, 8) + mine.shape, mine.dtype)
     for (x, d), piece in held.items():
         out = lax.dynamic_update_slice(out, piece[None, None], (xlo ^ x, (z + d + 8) % 8, 0, 0))

time: 108 us -> 109 us (level)
  Pallas kernels: 19 us -> 20.7 us
    pallas_call x2, Pallas kernels: 7.52 us -> 9.22 us  [the longest x1 7.28 us: make_terms(): pl.pallas_call(terms_kernel, out_shape=pltpu.HBM((k, b + 8, slots), jnp.i...]
    ppermute x3 -> x4, waiting for transfers between devices: 6.16 us -> 4.64 us  [up(): return lax.ppermute(piece, 'z', [(i, (i + 1) % 8) for i in range(8)])]
    ppermute x1, waiting for transfers between devices: 4.5 us -> 5.82 us  [corner(): return lax.ppermute(piece, ROW, pairs)]
    ppermute x4, waiting for transfers between devices: 1.8 us -> 3.07 us  [down(): return lax.ppermute(piece, 'z', [(i, (i - 1) % 8) for i in range(8)])]
    ppermute x4, waiting for transfers between devices: 1.23 us -> 0.01 us  [across(): return lax.ppermute(piece, 'xlo', [(0, 1), (1, 0)])]
    ppermute x3 -> x4, starting transfers between devices: 2.83 us -> 3.68 us  [up(): return lax.ppermute(piece, 'z', [(i, (i + 1) % 8) for i in range(8)])]
  transfers between devices with their start and end apart: 14 -> 15, of which waited for: 8 -> 7; matrix products, arithmetic and copies ran while one was open for 0% -> 0% of each run, Pallas kernels for 10% -> 9%
where the time goes in v3:
time: 109 us
  waiting for transfers between devices  35.9 us (33%)
  starting transfers between devices  28.8 us (26%)
  blocking collectives  21 us (19%)
  Pallas kernels  20.7 us (19%)
  local copies, waits for them, and re-layouts  1.52 us (1%)
    all_to_all x1, waiting for transfers between devices, on_device(): got = lax.all_to_all(terms, ROW, 0, 0)  22.3 us
    all_to_all x1, blocking collectives, on_device(): own = lax.all_to_all(copies, ('xhi', 'y'), 0, 0)  21 us
    ppermute x4, starting transfers between devices, down(): return lax.ppermute(piece, 'z', [(i, (i - 1) % 8) for i in range(8)])  10.8 us
    pallas_call x1, Pallas kernels, relayout(): pl.pallas_call(relayout_kernel, out_shape=pltpu.HBM((slots, d, b), jac.dt...  10.3 us
    all_to_all x1, starting transfers between devices, on_device(): got = lax.all_to_all(terms, ROW, 0, 0)  9.95 us
    pallas_call x1, Pallas kernels, make_terms(): pl.pallas_call(terms_kernel, out_shape=pltpu.HBM((k, b + 8, slots), jnp.i...  7.28 us
    ppermute x1, waiting for transfers between devices, corner(): return lax.ppermute(piece, ROW, pairs)  5.82 us
    ppermute x4, waiting for transfers between devices, up(): return lax.ppermute(piece, 'z', [(i, (i + 1) % 8) for i in range(8)])  4.64 us
  transfers between devices with their start and end apart: 15, of which 7 were waited for; matrix products, arithmetic and copies ran while one was open for 0% of the time, Pallas kernels for 9%

profile of v3, /device:TPU:2, one launch (start us, length us, event | category | flops | bytes accessed | tf_op | source)
XLA Modules:
  0.0 108.9 jit_solution(1409404333107422567)
XLA Ops:
  0.0 1.9 %flip.1 = bf16[8,200,256]{2,1,0:T(8,128)(2,1)} custom-call(bf16[256,200]{1,0:T(8,128)(2,1)} %bitcast.60), custom_call_target="tpu_custom_call" | custom-call | tf_op jit(solution)/shard_map/flip/pallas_call | solution.py:60
  1.9 21.0 %all_to_all.10.own_ref = bf16[8,200,256]{2,1,0:T(8,128)(2,1)S(1)} all-to-all(bf16[8,200,256]{2,1,0:T(8,128)(2,1)} %flip.1), channel_id=1, replica_groups=mesh['xlo'=2,'z'=8,'xhi'=2,'y'=4,'core'=2] {'xhi','y'}, dimensions={0} | all-to-all | bytes 1638400 | tf_op jit(solution)/shard_map/all_to_all | solution.py:291
  23.0 0.0 collective-permute-start
  23.0 0.0 copy-start
  23.0 0.0 copy-start.1
  23.0 10.3 %relayout.1.jac_ref = bf16[128,200,200]{2,1,0:T(8,128)(2,1)} custom-call(bf16[200,200,128]{2,1,0:T(8,128)(2,1)} %bitcast.55), custom_call_target="tpu_custom_call" | custom-call | tf_op jit(solution)/shard_map/relayout/pallas_call | solution.py:114
  33.9 0.0 collective-permute-done.other_ref
  33.9 0.0 copy-done
  33.9 0.0 copy-done.1
  33.9 7.3 %terms.1 = s16[16,208,128]{2,1,0:T(8,128)(2,1)} custom-call(s32[128]{0:T(128)S(1)} %bitcast.53, s32[1,1]{1,0:T(1,128)S(6)} %copy.22.count_ref, s32[1,128]{1,0:T(1,128)S(1)} %bitcast.54, bf16[8,200,256]{2,1,0:T(8,128)(2,1)S(1)} %all_to_all.10.own_ref, bf16[8,200,256]{2,1,0:T(8,128)(2,1)S(1)} %collective-permute-done.other_ref, ...), custom_call_target="tpu_custom_call" | custom-call | tf_op jit(solution)/shard_map/terms/pallas_call | solution.py:194
  41.2 10.0 %all-to-all-start.1 = ((s16[16,208,128]{2,1,0:T(8,128)(2,1)}), s16[16,208,128]{2,1,0:T(8,128)(2,1)S(1)}, u32[]{:S(2)}, u32[]{:S(2)}) async-start(s16[16,208,128]{2,1,0:T(8,128)(2,1)} %terms.1), calls=%async_computation.1 | async-start | bytes 1703936 | tf_op jit(solution)/shard_map/all_to_all | solution.py:295
  51.2 22.3 %all-to-all-done.1.got_ref = s16[16,208,128]{2,1,0:T(8,128)(2,1)S(1)} async-done(((s16[16,208,128]{2,1,0:T(8,128)(2,1)}), s16[16,208,128]{2,1,0:T(8,128)(2,1)S(1)}, u32[]{:S(2)}, u32[]{:S(2)}) %all-to-all-start.1) | async-done | bytes 852000 | tf_op jit(solution)/shard_map/all_to_all | solution.py:295
  73.5 1.2 %add_up.1 = bf16[200,256]{1,0:T(8,128)(2,1)S(1)} custom-call(s16[16,208,128]{2,1,0:T(8,128)(2,1)S(1)} %all-to-all-done.1.got_ref), custom_call_target="tpu_custom_call" | custom-call | tf_op jit(solution)/shard_map/add_up/pallas_call | solution.py:236
  74.8 2.2 %collective-permute-start.1 = (bf16[200,256]{1,0:T(8,128)(2,1)S(1)}, bf16[200,256]{1,0:T(8,128)(2,1)S(1)}, u32[]{:S(2)}, u32[]{:S(2)}) collective-permute-start(bf16[200,256]{1,0:T(8,128)(2,1)S(1)} %add_up.1), channel_id=1, source_target_pairs={{0,16},{16,32},{32,48},{48,64},{64,80},{80,96},{96,112},{112,0},{1... | collective-permute-start | bytes 307208 | tf_op jit(solution)/shard_map/ppermute | solution.py:255
  77.0 1.1 %collective-permute-start.2 = (bf16[200,256]{1,0:T(8,128)(2,1)S(1)}, bf16[200,256]{1,0:T(8,128)(2,1)S(1)}, u32[]{:S(2)}, u32[]{:S(2)}) collective-permute-start(bf16[200,256]{1,0:T(8,128)(2,1)S(1)} %add_up.1), channel_id=1, source_target_pairs={{0,112},{16,0},{32,16},{48,32},{64,48},{80,64},{96,80},{112,96},{1... | collective-permute-start | bytes 307208 | tf_op jit(solution)/shard_map/ppermute | solution.py:258
  78.1 1.4 %collective-permute-start.3 = (bf16[200,256]{1,0:T(8,128)(2,1)S(1)}, bf16[200,256]{1,0:T(8,128)(2,1)S(1)}, u32[]{:S(2)}, u32[]{:S(2)}) collective-permute-start(bf16[200,256]{1,0:T(8,128)(2,1)S(1)} %add_up.1), channel_id=1, source_target_pairs={{0,128},{128,0},{1,129},{129,1},{2,130},{130,2},{3,131},{131,3},{4... | collective-permute-start | bytes 307208 | tf_op jit(solution)/shard_map/ppermute | solution.py:261
  79.5 0.1 broadcast_in_dim.39
  79.7 1.1 collective-permute-done.1
  80.7 0.9 collective-permute-done.2
  81.7 0.6 collective-permute-start.6
  82.3 0.1 collective-permute-start.4
  82.4 3.1 %collective-permute-start.5 = (bf16[200,256]{1,0:T(8,128)(2,1)S(1)}, bf16[200,256]{1,0:T(8,128)(2,1)S(1)}, u32[]{:S(2)}, u32[]{:S(2)}) collective-permute-start(bf16[200,256]{1,0:T(8,128)(2,1)S(1)} %collective-permute-done.2), channel_id=1, source_target_pairs={{0,112},{16,0},{32,16},{48,32},{64,48},{80,64},{96,80},{112,96},{1... | collective-permute-start | bytes 307208 | tf_op jit(solution)/shard_map/ppermute | solution.py:258
  85.6 0.0 collective-permute-done.3
  85.6 2.6 %collective-permute-done.4 = bf16[200,256]{1,0:T(8,128)(2,1)S(1)} collective-permute-done((bf16[200,256]{1,0:T(8,128)(2,1)S(1)}, bf16[200,256]{1,0:T(8,128)(2,1)S(1)}, u32[]{:S(2)}, u32[]{:S(2)}) %collective-permute-start.4) | collective-permute-done | bytes 102432 | tf_op jit(solution)/shard_map/ppermute | solution.py:255
  88.2 0.0 collective-permute-done.5
  88.2 1.6 %collective-permute-start.9 = (bf16[2,200,256]{2,1,0:T(8,128)(2,1)S(1)}, bf16[2,200,256]{2,1,0:T(8,128)(2,1)S(1)}, u32[]{:S(2)}, u32[]{:S(2)}) collective-permute-start(bf16[2,200,256]{2,1,0:T(8,128)(2,1)S(1)} %pad_maximum_fusion.1), channel_id=1, source_target_pairs={{0,128},{128,0},{1,129},{129,1},{2,130},{130,2},{3,131},{131,3},{4... | collective-permute-start | bytes 614408 | tf_op jit(solution)/shard_map/ppermute | solution.py:261
  89.8 0.6 collective-permute-start.7
  90.4 3.0 %collective-permute-start.8 = (bf16[200,256]{1,0:T(8,128)(2,1)S(1)}, bf16[200,256]{1,0:T(8,128)(2,1)S(1)}, u32[]{:S(2)}, u32[]{:S(2)}) collective-permute-start(bf16[200,256]{1,0:T(8,128)(2,1)S(1)} %collective-permute-done.5), channel_id=1, source_target_pairs={{0,112},{16,0},{32,16},{48,32},{64,48},{80,64},{96,80},{112,96},{1... | collective-permute-start | bytes 307208 | tf_op jit(solution)/shard_map/ppermute | solution.py:258
  93.4 0.0 collective-permute-done.6
  93.5 2.2 %collective-permute-done.8 = bf16[200,256]{1,0:T(8,128)(2,1)S(1)} collective-permute-done((bf16[200,256]{1,0:T(8,128)(2,1)S(1)}, bf16[200,256]{1,0:T(8,128)(2,1)S(1)}, u32[]{:S(2)}, u32[]{:S(2)}) %collective-permute-start.8) | collective-permute-done | bytes 102432 | tf_op jit(solution)/shard_map/ppermute | solution.py:258
  95.6 3.6 %collective-permute-start.11 = (bf16[200,256]{1,0:T(8,128)(2,1)S(1)}, bf16[200,256]{1,0:T(8,128)(2,1)S(1)}, u32[]{:S(2)}, u32[]{:S(2)}) collective-permute-start(bf16[200,256]{1,0:T(8,128)(2,1)S(1)} %collective-permute-done.8), channel_id=1, source_target_pairs={{0,112},{16,0},{32,16},{48,32},{64,48},{80,64},{96,80},{112,96},{1... | collective-permute-start | bytes 307208 | tf_op jit(solution)/shard_map/ppermute | solution.py:258
  99.2 0.6 collective-permute-start.12
  99.8 0.0 collective-permute-done.7
  99.8 0.0 collective-permute-start.10
  99.8 0.0 collective-permute-done.9
  99.9 0.8 collective-permute-start.13
  100.8 5.8 %collective-permute-done.10 = bf16[200,256]{1,0:T(8,128)(2,1)S(1)} collective-permute-done((bf16[200,256]{1,0:T(8,128)(2,1)S(1)}, bf16[200,256]{1,0:T(8,128)(2,1)S(1)}, u32[]{:S(2)}, u32[]{:S(2)}) %collective-permute-start.10) | collective-permute-done | bytes 102432 | tf_op jit(solution)/shard_map/ppermute | solution.py:265
  106.6 0.0 collective-permute-done.11
  106.6 0.0 collective-permute-done.12
  106.7 1.0 collective-permute-done.13
  107.7 0.0 copy-start.2
  107.7 1.2 %copy-done.2 = bf16[2,8,200,256]{3,2,1,0:T(8,128)(2,1)} copy-done((bf16[2,8,200,256]{3,2,1,0:T(8,128)(2,1)}, bf16[2,8,200,256]{3,2,1,0:T(8,128)(2,1)S(1)}, u32[]{:S(2)}) %copy-start.2) | copy-done | bytes 1638424
  (19 shorter events, 0.3 us)
Async XLA Ops:
  23.0 10.9 %collective-permute-start = (bf16[8,200,256]{2,1,0:T(8,128)(2,1)S(1)}, bf16[8,200,256]{2,1,0:T(8,128)(2,1)S(1)}, u32[]{:S(2)}, u32[]{:S(2)}) collective-permute-start(bf16[8,200,256]{2,1,0:T(8,128)(2,1)S(1)} %all_to_all.10.own_ref), channel_id=1, source_target_pairs={{0,1},{1,0},{2,3},{3,2},{4,5},{5,4},{6,7},{7,6},{8,9},{9,8},{10,11... | collective-permute-start | bytes 2457608 | tf_op jit(solution)/shard_map/ppermute | solution.py:292
  23.0 10.9 %copy-start = (s32[1,1,128]{2,1,0:T(1,128)S(1)}, s32[1,1,128]{2,1,0:T(1,128)}, u32[]{:S(2)}) copy-start(s32[1,1,128]{2,1,0:T(1,128)} %param.7) | copy-start | bytes 1540
  23.0 10.9 %copy-start.1 = (s32[1,1,128]{2,1,0:T(1,128)S(1)}, s32[1,1,128]{2,1,0:T(1,128)}, u32[]{:S(2)}) copy-start(s32[1,1,128]{2,1,0:T(1,128)} %param.8) | copy-start | bytes 1540
  41.2 32.3 %all-to-all-start.1 = ((s16[16,208,128]{2,1,0:T(8,128)(2,1)}), s16[16,208,128]{2,1,0:T(8,128)(2,1)S(1)}, u32[]{:S(2)}, u32[]{:S(2)}) async-start(s16[16,208,128]{2,1,0:T(8,128)(2,1)} %terms.1), calls=%async_computation.1 | async-start | bytes 1703936 | tf_op jit(solution)/shard_map/all_to_all | solution.py:295
  74.8 5.9 %collective-permute-start.1 = (bf16[200,256]{1,0:T(8,128)(2,1)S(1)}, bf16[200,256]{1,0:T(8,128)(2,1)S(1)}, u32[]{:S(2)}, u32[]{:S(2)}) collective-permute-start(bf16[200,256]{1,0:T(8,128)(2,1)S(1)} %add_up.1), channel_id=1, source_target_pairs={{0,16},{16,32},{32,48},{48,64},{64,80},{80,96},{96,112},{112,0},{1... | collective-permute-start | bytes 307208 | tf_op jit(solution)/shard_map/ppermute | solution.py:255
  77.0 4.7 %collective-permute-start.2 = (bf16[200,256]{1,0:T(8,128)(2,1)S(1)}, bf16[200,256]{1,0:T(8,128)(2,1)S(1)}, u32[]{:S(2)}, u32[]{:S(2)}) collective-permute-start(bf16[200,256]{1,0:T(8,128)(2,1)S(1)} %add_up.1), channel_id=1, source_target_pairs={{0,112},{16,0},{32,16},{48,32},{64,48},{80,64},{96,80},{112,96},{1... | collective-permute-start | bytes 307208 | tf_op jit(solution)/shard_map/ppermute | solution.py:258
  78.1 7.5 %collective-permute-start.3 = (bf16[200,256]{1,0:T(8,128)(2,1)S(1)}, bf16[200,256]{1,0:T(8,128)(2,1)S(1)}, u32[]{:S(2)}, u32[]{:S(2)}) collective-permute-start(bf16[200,256]{1,0:T(8,128)(2,1)S(1)} %add_up.1), channel_id=1, source_target_pairs={{0,128},{128,0},{1,129},{129,1},{2,130},{130,2},{3,131},{131,3},{4... | collective-permute-start | bytes 307208 | tf_op jit(solution)/shard_map/ppermute | solution.py:261
  81.7 11.7 %collective-permute-start.6 = (bf16[2,200,256]{2,1,0:T(8,128)(2,1)S(1)}, bf16[2,200,256]{2,1,0:T(8,128)(2,1)S(1)}, u32[]{:S(2)}, u32[]{:S(2)}) collective-permute-start(bf16[2,200,256]{2,1,0:T(8,128)(2,1)S(1)} %pad_maximum_fusion), channel_id=1, source_target_pairs={{0,128},{128,0},{1,129},{129,1},{2,130},{130,2},{3,131},{131,3},{4... | collective-permute-start | bytes 614408 | tf_op jit(solution)/shard_map/ppermute | solution.py:261
  82.3 5.9 %collective-permute-start.4 = (bf16[200,256]{1,0:T(8,128)(2,1)S(1)}, bf16[200,256]{1,0:T(8,128)(2,1)S(1)}, u32[]{:S(2)}, u32[]{:S(2)}) collective-permute-start(bf16[200,256]{1,0:T(8,128)(2,1)S(1)} %collective-permute-done.1), channel_id=1, source_target_pairs={{0,16},{16,32},{32,48},{48,64},{64,80},{80,96},{96,112},{112,0},{1... | collective-permute-start | bytes 307208 | tf_op jit(solution)/shard_map/ppermute | solution.py:255
  82.4 5.8 %collective-permute-start.5 = (bf16[200,256]{1,0:T(8,128)(2,1)S(1)}, bf16[200,256]{1,0:T(8,128)(2,1)S(1)}, u32[]{:S(2)}, u32[]{:S(2)}) collective-permute-start(bf16[200,256]{1,0:T(8,128)(2,1)S(1)} %collective-permute-done.2), channel_id=1, source_target_pairs={{0,112},{16,0},{32,16},{48,32},{64,48},{80,64},{96,80},{112,96},{1... | collective-permute-start | bytes 307208 | tf_op jit(solution)/shard_map/ppermute | solution.py:258
  88.2 11.6 %collective-permute-start.9 = (bf16[2,200,256]{2,1,0:T(8,128)(2,1)S(1)}, bf16[2,200,256]{2,1,0:T(8,128)(2,1)S(1)}, u32[]{:S(2)}, u32[]{:S(2)}) collective-permute-start(bf16[2,200,256]{2,1,0:T(8,128)(2,1)S(1)} %pad_maximum_fusion.1), channel_id=1, source_target_pairs={{0,128},{128,0},{1,129},{129,1},{2,130},{130,2},{3,131},{131,3},{4... | collective-permute-start | bytes 614408 | tf_op jit(solution)/shard_map/ppermute | solution.py:261
  89.8 10.0 %collective-permute-start.7 = (bf16[200,256]{1,0:T(8,128)(2,1)S(1)}, bf16[200,256]{1,0:T(8,128)(2,1)S(1)}, u32[]{:S(2)}, u32[]{:S(2)}) collective-permute-start(bf16[200,256]{1,0:T(8,128)(2,1)S(1)} %collective-permute-done.4), channel_id=1, source_target_pairs={{0,16},{16,32},{32,48},{48,64},{64,80},{80,96},{96,112},{112,0},{1... | collective-permute-start | bytes 307208 | tf_op jit(solution)/shard_map/ppermute | solution.py:255
  90.4 5.2 %collective-permute-start.8 = (bf16[200,256]{1,0:T(8,128)(2,1)S(1)}, bf16[200,256]{1,0:T(8,128)(2,1)S(1)}, u32[]{:S(2)}, u32[]{:S(2)}) collective-permute-start(bf16[200,256]{1,0:T(8,128)(2,1)S(1)} %collective-permute-done.5), channel_id=1, source_target_pairs={{0,112},{16,0},{32,16},{48,32},{64,48},{80,64},{96,80},{112,96},{1... | collective-permute-start | bytes 307208 | tf_op jit(solution)/shard_map/ppermute | solution.py:258
  95.6 11.0 %collective-permute-start.11 = (bf16[200,256]{1,0:T(8,128)(2,1)S(1)}, bf16[200,256]{1,0:T(8,128)(2,1)S(1)}, u32[]{:S(2)}, u32[]{:S(2)}) collective-permute-start(bf16[200,256]{1,0:T(8,128)(2,1)S(1)} %collective-permute-done.8), channel_id=1, source_target_pairs={{0,112},{16,0},{32,16},{48,32},{64,48},{80,64},{96,80},{112,96},{1... | collective-permute-start | bytes 307208 | tf_op jit(solution)/shard_map/ppermute | solution.py:258
  99.2 7.4 %collective-permute-start.12 = (bf16[200,256]{1,0:T(8,128)(2,1)S(1)}, bf16[200,256]{1,0:T(8,128)(2,1)S(1)}, u32[]{:S(2)}, u32[]{:S(2)}) collective-permute-start(bf16[200,256]{1,0:T(8,128)(2,1)S(1)} %collective-permute-done.8), channel_id=1, source_target_pairs={{0,128},{128,0},{1,129},{129,1},{2,130},{130,2},{3,131},{131,3},{4... | collective-permute-start | bytes 307208 | tf_op jit(solution)/shard_map/ppermute | solution.py:261
  99.8 6.8 %collective-permute-start.10 = (bf16[200,256]{1,0:T(8,128)(2,1)S(1)}, bf16[200,256]{1,0:T(8,128)(2,1)S(1)}, u32[]{:S(2)}, u32[]{:S(2)}) collective-permute-start(bf16[200,256]{1,0:T(8,128)(2,1)S(1)} %collective-permute-done.7), channel_id=1, source_target_pairs={{0,144},{16,160},{32,176},{48,192},{64,208},{80,224},{96,240},{112... | collective-permute-start | bytes 307208 | tf_op jit(solution)/shard_map/ppermute | solution.py:265
  99.9 7.8 %collective-permute-start.13 = (bf16[200,256]{1,0:T(8,128)(2,1)S(1)}, bf16[200,256]{1,0:T(8,128)(2,1)S(1)}, u32[]{:S(2)}, u32[]{:S(2)}) collective-permute-start(bf16[200,256]{1,0:T(8,128)(2,1)S(1)} %slice_bitcast_fusion.3), channel_id=1, source_target_pairs={{0,16},{16,32},{32,48},{48,64},{64,80},{80,96},{96,112},{112,0},{1... | collective-permute-start | bytes 307208 | tf_op jit(solution)/shard_map/ppermute | solution.py:255
  107.7 1.2 %copy-start.2 = (bf16[2,8,200,256]{3,2,1,0:T(8,128)(2,1)}, bf16[2,8,200,256]{3,2,1,0:T(8,128)(2,1)S(1)}, u32[]{:S(2)}) copy-start(bf16[2,8,200,256]{3,2,1,0:T(8,128)(2,1)S(1)} %bitcast_dynamic-update-slice_fusion) | copy-start | bytes 4915204

commit v4 on v3

--- a/solution.py
+++ b/solution.py
@@ -160,7 +160,9 @@
             slot = c * GROUP + j
             row = rows_ref[slot]
             home = row // k
-            place = (((home & 1) ^ core) * pieces + home // 2) * per + (row & (k - 1)) * k
+            owner = home & 1
+            piece = (home // 2) ^ (owner * (pieces - 1))
+            place = ((owner ^ core) * pieces + piece) * per + (row & (k - 1)) * k
             lhs = faces_ref[pl.ds(pl.multiple_of(place, k), k), pl.ds(0, b)]
             term = jnp.dot(lhs, jac_buf[slot], preferred_element_type=jnp.float32)
             at = pl.ds(pl.multiple_of(slot * TERM_PITCH, 4), k)
@@ -247,22 +249,35 @@
     )(got)
 
 
+def both_ways(groups):
+    return [[2 * i for i in groups], [2 * i + 1 for i in reversed(groups)]]
+
+
 def gather_result(mine):
     xlo = lax.axis_index("xlo")
     z = lax.axis_index("z")
+    core = lax.axis_index("core")
+
+    def shift(turn, cross):
+        steps = (turn, -turn)
+        return [
+            (x * 16 + i * 2 + c, (x ^ cross) * 16 + (i + steps[c]) % 8 * 2 + c)
+            for x in range(2)
+            for i in range(8)
+            for c in range(2)
+        ]
+
+    def send(piece, turn, cross):
+        return lax.ppermute(piece, ("xlo", "z", "core"), shift(turn, cross))
 
     def up(piece):
-        return lax.ppermute(piece, "z", [(i, (i + 1) % 8) for i in range(8)])
+        return send(piece, 1, 0)
 
     def down(piece):
-        return lax.ppermute(piece, "z", [(i, (i - 1) % 8) for i in range(8)])
+        return send(piece, -1, 0)
 
     def across(piece):
-        return lax.ppermute(piece, "xlo", [(0, 1), (1, 0)])
-
-    def corner(piece):
-        pairs = [(x * 8 + i, (1 - x) * 8 + (i + 1) % 8) for x in range(2) for i in range(8)]
-        return lax.ppermute(piece, ROW, pairs)
+        return send(piece, 0, 1)
 
     def both(one, two):
         return jnp.stack([one, two])
@@ -274,13 +289,13 @@
     held[1, -1], held[1, 1] = across(both(held[0, -1], held[0, 1]))
     held[0, -3], held[0, 3] = up(held[0, -2]), down(held[0, 2])
     held[1, -2], held[1, 2] = across(both(held[0, -2], held[0, 2]))
-    held[1, -4] = corner(held[0, -3])
+    held[1, -3], held[1, 3] = across(both(held[0, -3], held[0, 3]))
     held[0, 4] = down(held[0, 3])
-    held[1, 3] = across(held[0, 3])
-    held[1, -3] = up(held[1, -2])
+    held[1, -4] = send(held[0, -3], 1, 1)
     out = jnp.zeros((2, 8) + mine.shape, mine.dtype)
     for (x, d), piece in held.items():
-        out = lax.dynamic_update_slice(out, piece[None, None], (xlo ^ x, (z + d + 8) % 8, 0, 0))
+        at = (z + (1 - 2 * core) * d + 8) % 8
+        out = lax.dynamic_update_slice(out, piece[None, None], (xlo ^ x ^ core, at ^ (7 * core), 0, 0))
     return out
 
 
@@ -288,11 +303,11 @@
     faces_here, k, b = adjoints.shape
     slots = jac_rows.shape[2]
     copies = flip(adjoints.reshape(faces_here * k, b), 8)
-    own = lax.all_to_all(copies, ("xhi", "y"), 0, 0)
+    own = lax.all_to_all(copies, COL, 0, 0, axis_index_groups=both_ways(range(8)))
     other = lax.ppermute(own, "core", [(0, 1), (1, 0)])
     jac = relayout(jnp.transpose(jac_blocks[0, 0], (1, 2, 0)))
     terms = make_terms(jac_rows.reshape(slots), tile_count, jac_cols.reshape(1, slots), own, other, jac, k)
-    got = lax.all_to_all(terms, ROW, 0, 0)
+    got = lax.all_to_all(terms, ROW + ("core",), 0, 0, axis_index_groups=both_ways(range(16)))
     mine = add_up(got, faces_here * 16)
     out = gather_result(mine).reshape(k, b, faces_here * 16)
     return jnp.transpose(out, (2, 0, 1))

time: 109 us -> 106 us (0.972); the launches traced: 109 us -> 104 us
  starting transfers between devices: 28.8 us -> 25.9 us
  blocking collectives: 21 us -> 18.8 us
    ppermute x13 -> x12, starting transfers between devices: 18.8 us -> 16 us  [send(): return lax.ppermute(piece, ('xlo', 'z', 'core'), shift(turn, cross))]
    all_to_all x1, blocking collectives: 21 us -> 18.8 us  [on_device(): lax.all_to_all(copies, COL, 0, 0, axis_index_groups=both_ways(range(8)))]
    ppermute x13 -> x12, waiting for transfers between devices: 13.5 us -> 14.8 us  [send(): return lax.ppermute(piece, ('xlo', 'z', 'core'), shift(turn, cross))]
  transfers between devices with their start and end apart: 15 -> 14, of which waited for: 7 -> 7; matrix products, arithmetic and copies ran while one was open for 0% -> 0% of each run, Pallas kernels for 9% -> 10%
where the time goes in v4:
time: 106 us; the launch traced here: 104 us
  waiting for transfers between devices  36.2 us (34%)
  starting transfers between devices  25.9 us (24%)
  Pallas kernels  20.7 us (20%)
  blocking collectives  18.8 us (18%)
  local copies, waits for them, and re-layouts  1.51 us (1%)
    all_to_all x1, waiting for transfers between devices, on_device(): lax.all_to_all(terms, ROW + ('core',), 0, 0, axis_index_groups=both_ways(...  21.5 us
    all_to_all x1, blocking collectives, on_device(): lax.all_to_all(copies, COL, 0, 0, axis_index_groups=both_ways(range(8)))  18.8 us
    ppermute x12, starting transfers between devices, send(): return lax.ppermute(piece, ('xlo', 'z', 'core'), shift(turn, cross))  16 us
    ppermute x12, waiting for transfers between devices, send(): return lax.ppermute(piece, ('xlo', 'z', 'core'), shift(turn, cross))  14.8 us
    pallas_call x1, Pallas kernels, relayout(): pl.pallas_call(relayout_kernel, out_shape=pltpu.HBM((slots, d, b), jac.dt...  10.2 us
    all_to_all x1, starting transfers between devices, on_device(): lax.all_to_all(terms, ROW + ('core',), 0, 0, axis_index_groups=both_ways(...  9.95 us
    pallas_call x1, Pallas kernels, make_terms(): pl.pallas_call(terms_kernel, out_shape=pltpu.HBM((k, b + 8, slots), jnp.i...  7.29 us
  transfers between devices with their start and end apart: 14, of which 7 were waited for; matrix products, arithmetic and copies ran while one was open for 0% of the time, Pallas kernels for 10%

profile of v4, /device:TPU:2, one launch (start us, length us, event | category | flops | bytes accessed | tf_op | source)
XLA Modules:
  0.0 104.1 jit_solution(4150303337414031275)
XLA Ops:
  0.0 1.9 %flip.1 = bf16[8,200,256]{2,1,0:T(8,128)(2,1)} custom-call(bf16[256,200]{1,0:T(8,128)(2,1)} %bitcast.68), custom_call_target="tpu_custom_call" | custom-call | tf_op jit(solution)/shard_map/flip/pallas_call | solution.py:60
  1.9 18.8 %all_to_all.10.own_ref = bf16[8,200,256]{2,1,0:T(8,128)(2,1)S(1)} all-to-all(bf16[8,200,256]{2,1,0:T(8,128)(2,1)} %flip.1), channel_id=1, replica_groups={{0,2,4,6,8,10,12,14},{15,13,11,9,7,5,3,1},{16,18,20,22,24,26,28,30},{31..., dimensions={0} | all-to-all | bytes 1638400 | tf_op jit(solution)/shard_map/all_to_all | solution.py:306
  20.7 0.0 collective-permute-start
  20.7 0.0 copy-start
  20.7 0.0 copy-start.1
  20.7 10.2 %relayout.1.jac_ref = bf16[128,200,200]{2,1,0:T(8,128)(2,1)} custom-call(bf16[200,200,128]{2,1,0:T(8,128)(2,1)} %bitcast.61), custom_call_target="tpu_custom_call" | custom-call | tf_op jit(solution)/shard_map/relayout/pallas_call | solution.py:114
  31.6 0.0 collective-permute-done.other_ref
  31.6 0.0 copy-done
  31.6 0.0 copy-done.1
  31.6 7.3 %terms.1 = s16[16,208,128]{2,1,0:T(8,128)(2,1)} custom-call(s32[128]{0:T(128)S(1)} %bitcast.59, s32[1,1]{1,0:T(1,128)S(6)} %copy.22.count_ref, s32[1,128]{1,0:T(1,128)S(1)} %bitcast.60, bf16[8,200,256]{2,1,0:T(8,128)(2,1)S(1)} %all_to_all.10.own_ref, bf16[8,200,256]{2,1,0:T(8,128)(2,1)S(1)} %collective-permute-done.other_ref, ...), custom_call_target="tpu_custom_call" | custom-call | tf_op jit(solution)/shard_map/terms/pallas_call | solution.py:196
  38.9 10.0 %all-to-all-start.1 = ((s16[16,208,128]{2,1,0:T(8,128)(2,1)}), s16[16,208,128]{2,1,0:T(8,128)(2,1)S(1)}, u32[]{:S(2)}, u32[]{:S(2)}) async-start(s16[16,208,128]{2,1,0:T(8,128)(2,1)} %terms.1), calls=%async_computation.1 | async-start | bytes 1703936 | tf_op jit(solution)/shard_map/all_to_all | solution.py:310
  48.9 21.5 %all-to-all-done.1.got_ref = s16[16,208,128]{2,1,0:T(8,128)(2,1)S(1)} async-done(((s16[16,208,128]{2,1,0:T(8,128)(2,1)}), s16[16,208,128]{2,1,0:T(8,128)(2,1)S(1)}, u32[]{:S(2)}, u32[]{:S(2)}) %all-to-all-start.1) | async-done | bytes 852000 | tf_op jit(solution)/shard_map/all_to_all | solution.py:310
  70.3 1.2 %add_up.1 = bf16[200,256]{1,0:T(8,128)(2,1)S(1)} custom-call(s16[16,208,128]{2,1,0:T(8,128)(2,1)S(1)} %all-to-all-done.1.got_ref), custom_call_target="tpu_custom_call" | custom-call | tf_op jit(solution)/shard_map/add_up/pallas_call | solution.py:238
  71.6 0.5 collective-permute-start.1
  72.1 2.8 %collective-permute-start.2 = (bf16[200,256]{1,0:T(8,128)(2,1)S(1)}, bf16[200,256]{1,0:T(8,128)(2,1)S(1)}, u32[]{:S(2)}, u32[]{:S(2)}) collective-permute-start(bf16[200,256]{1,0:T(8,128)(2,1)S(1)} %add_up.1), channel_id=1, source_target_pairs={{0,112},{1,17},{16,0},{17,33},{32,16},{33,49},{48,32},{49,65},{64,... | collective-permute-start | bytes 307208 | tf_op jit(solution)/shard_map/ppermute | solution.py:271
  74.9 0.4 collective-permute-start.3
  75.3 0.1 broadcast_in_dim.33
  75.4 2.8 %collective-permute-done.1 = bf16[200,256]{1,0:T(8,128)(2,1)S(1)} collective-permute-done((bf16[200,256]{1,0:T(8,128)(2,1)S(1)}, bf16[200,256]{1,0:T(8,128)(2,1)S(1)}, u32[]{:S(2)}, u32[]{:S(2)}) %collective-permute-start.1) | collective-permute-done | bytes 102432 | tf_op jit(solution)/shard_map/ppermute | solution.py:271
  78.2 0.0 collective-permute-done.2
  78.3 0.4 collective-permute-start.6
  78.7 1.1 %collective-permute-start.4 = (bf16[200,256]{1,0:T(8,128)(2,1)S(1)}, bf16[200,256]{1,0:T(8,128)(2,1)S(1)}, u32[]{:S(2)}, u32[]{:S(2)}) collective-permute-start(bf16[200,256]{1,0:T(8,128)(2,1)S(1)} %collective-permute-done.1), channel_id=1, source_target_pairs={{0,16},{1,113},{16,32},{17,1},{32,48},{33,17},{48,64},{49,33},{64,... | collective-permute-start | bytes 307208 | tf_op jit(solution)/shard_map/ppermute | solution.py:271
  79.8 2.1 %collective-permute-start.5 = (bf16[200,256]{1,0:T(8,128)(2,1)S(1)}, bf16[200,256]{1,0:T(8,128)(2,1)S(1)}, u32[]{:S(2)}, u32[]{:S(2)}) collective-permute-start(bf16[200,256]{1,0:T(8,128)(2,1)S(1)} %collective-permute-done.2), channel_id=1, source_target_pairs={{0,112},{1,17},{16,0},{17,33},{32,16},{33,49},{48,32},{49,65},{64,... | collective-permute-start | bytes 307208 | tf_op jit(solution)/shard_map/ppermute | solution.py:271
  82.0 0.0 collective-permute-done.3
  82.0 2.8 %collective-permute-done.4 = bf16[200,256]{1,0:T(8,128)(2,1)S(1)} collective-permute-done((bf16[200,256]{1,0:T(8,128)(2,1)S(1)}, bf16[200,256]{1,0:T(8,128)(2,1)S(1)}, u32[]{:S(2)}, u32[]{:S(2)}) %collective-permute-start.4) | collective-permute-done | bytes 102432 | tf_op jit(solution)/shard_map/ppermute | solution.py:271
  84.7 0.0 collective-permute-done.5
  84.8 1.7 %collective-permute-start.9 = (bf16[2,200,256]{2,1,0:T(8,128)(2,1)S(1)}, bf16[2,200,256]{2,1,0:T(8,128)(2,1)S(1)}, u32[]{:S(2)}, u32[]{:S(2)}) collective-permute-start(bf16[2,200,256]{2,1,0:T(8,128)(2,1)S(1)} %pad_maximum_fusion.1), channel_id=1, source_target_pairs={{0,128},{1,129},{16,144},{17,145},{32,160},{33,161},{48,176},{49,1... | collective-permute-start | bytes 614408 | tf_op jit(solution)/shard_map/ppermute | solution.py:271
  86.4 1.2 %collective-permute-start.7 = (bf16[200,256]{1,0:T(8,128)(2,1)S(1)}, bf16[200,256]{1,0:T(8,128)(2,1)S(1)}, u32[]{:S(2)}, u32[]{:S(2)}) collective-permute-start(bf16[200,256]{1,0:T(8,128)(2,1)S(1)} %collective-permute-done.4), channel_id=1, source_target_pairs={{0,16},{1,113},{16,32},{17,1},{32,48},{33,17},{48,64},{49,33},{64,... | collective-permute-start | bytes 307208 | tf_op jit(solution)/shard_map/ppermute | solution.py:271
  87.7 2.0 %collective-permute-start.8 = (bf16[200,256]{1,0:T(8,128)(2,1)S(1)}, bf16[200,256]{1,0:T(8,128)(2,1)S(1)}, u32[]{:S(2)}, u32[]{:S(2)}) collective-permute-start(bf16[200,256]{1,0:T(8,128)(2,1)S(1)} %collective-permute-done.5), channel_id=1, source_target_pairs={{0,112},{1,17},{16,0},{17,33},{32,16},{33,49},{48,32},{49,65},{64,... | collective-permute-start | bytes 307208 | tf_op jit(solution)/shard_map/ppermute | solution.py:271
  89.7 0.0 collective-permute-done.6
  89.8 2.5 %collective-permute-done.7 = bf16[200,256]{1,0:T(8,128)(2,1)S(1)} collective-permute-done((bf16[200,256]{1,0:T(8,128)(2,1)S(1)}, bf16[200,256]{1,0:T(8,128)(2,1)S(1)}, u32[]{:S(2)}, u32[]{:S(2)}) %collective-permute-start.7) | collective-permute-done | bytes 102432 | tf_op jit(solution)/shard_map/ppermute | solution.py:271
  92.3 0.0 collective-permute-done.8
  92.4 0.9 collective-permute-start.10
  93.3 2.8 %collective-permute-start.11 = (bf16[200,256]{1,0:T(8,128)(2,1)S(1)}, bf16[200,256]{1,0:T(8,128)(2,1)S(1)}, u32[]{:S(2)}, u32[]{:S(2)}) collective-permute-start(bf16[200,256]{1,0:T(8,128)(2,1)S(1)} %collective-permute-done.8), channel_id=1, source_target_pairs={{0,112},{1,17},{16,0},{17,33},{32,16},{33,49},{48,32},{49,65},{64,... | collective-permute-start | bytes 307208 | tf_op jit(solution)/shard_map/ppermute | solution.py:271
  96.1 0.0 collective-permute-start.12
  96.1 0.0 collective-permute-done.9
  96.2 2.0 %collective-permute-done.10 = bf16[2,200,256]{2,1,0:T(8,128)(2,1)S(1)} collective-permute-done((bf16[2,200,256]{2,1,0:T(8,128)(2,1)S(1)}, bf16[2,200,256]{2,1,0:T(8,128)(2,1)S(1)}, u32[]{:S(2)}, u32[]{:S(2)}) %collective-permute-start.10) | collective-permute-done | bytes 204832 | tf_op jit(solution)/shard_map/ppermute | solution.py:271
  98.2 0.1 collective-permute-done.11
  98.4 4.5 %collective-permute-done.12 = bf16[200,256]{1,0:T(8,128)(2,1)S(1)} collective-permute-done((bf16[200,256]{1,0:T(8,128)(2,1)S(1)}, bf16[200,256]{1,0:T(8,128)(2,1)S(1)}, u32[]{:S(2)}, u32[]{:S(2)}) %collective-permute-start.12) | collective-permute-done | bytes 102432 | tf_op jit(solution)/shard_map/ppermute | solution.py:271
  102.9 0.0 copy-start.2
  102.9 1.2 %copy-done.2 = bf16[2,8,200,256]{3,2,1,0:T(8,128)(2,1)} copy-done((bf16[2,8,200,256]{3,2,1,0:T(8,128)(2,1)}, bf16[2,8,200,256]{3,2,1,0:T(8,128)(2,1)S(1)}, u32[]{:S(2)}) %copy-start.2) | copy-done | bytes 1638424
  (19 shorter events, 0.3 us)
Async XLA Ops:
  20.7 10.9 %collective-permute-start = (bf16[8,200,256]{2,1,0:T(8,128)(2,1)S(1)}, bf16[8,200,256]{2,1,0:T(8,128)(2,1)S(1)}, u32[]{:S(2)}, u32[]{:S(2)}) collective-permute-start(bf16[8,200,256]{2,1,0:T(8,128)(2,1)S(1)} %all_to_all.10.own_ref), channel_id=1, source_target_pairs={{0,1},{1,0},{2,3},{3,2},{4,5},{5,4},{6,7},{7,6},{8,9},{9,8},{10,11... | collective-permute-start | bytes 2457608 | tf_op jit(solution)/shard_map/ppermute | solution.py:307
  20.7 10.9 %copy-start = (s32[1,1,128]{2,1,0:T(1,128)S(1)}, s32[1,1,128]{2,1,0:T(1,128)}, u32[]{:S(2)}) copy-start(s32[1,1,128]{2,1,0:T(1,128)} %param.7) | copy-start | bytes 1540
  20.7 10.9 %copy-start.1 = (s32[1,1,128]{2,1,0:T(1,128)S(1)}, s32[1,1,128]{2,1,0:T(1,128)}, u32[]{:S(2)}) copy-start(s32[1,1,128]{2,1,0:T(1,128)} %param.8) | copy-start | bytes 1540
  38.9 31.4 %all-to-all-start.1 = ((s16[16,208,128]{2,1,0:T(8,128)(2,1)}), s16[16,208,128]{2,1,0:T(8,128)(2,1)S(1)}, u32[]{:S(2)}, u32[]{:S(2)}) async-start(s16[16,208,128]{2,1,0:T(8,128)(2,1)} %terms.1), calls=%async_computation.1 | async-start | bytes 1703936 | tf_op jit(solution)/shard_map/all_to_all | solution.py:310
  71.6 6.6 %collective-permute-start.1 = (bf16[200,256]{1,0:T(8,128)(2,1)S(1)}, bf16[200,256]{1,0:T(8,128)(2,1)S(1)}, u32[]{:S(2)}, u32[]{:S(2)}) collective-permute-start(bf16[200,256]{1,0:T(8,128)(2,1)S(1)} %add_up.1), channel_id=1, source_target_pairs={{0,16},{1,113},{16,32},{17,1},{32,48},{33,17},{48,64},{49,33},{64,... | collective-permute-start | bytes 307208 | tf_op jit(solution)/shard_map/ppermute | solution.py:271
  72.1 6.1 %collective-permute-start.2 = (bf16[200,256]{1,0:T(8,128)(2,1)S(1)}, bf16[200,256]{1,0:T(8,128)(2,1)S(1)}, u32[]{:S(2)}, u32[]{:S(2)}) collective-permute-start(bf16[200,256]{1,0:T(8,128)(2,1)S(1)} %add_up.1), channel_id=1, source_target_pairs={{0,112},{1,17},{16,0},{17,33},{32,16},{33,49},{48,32},{49,65},{64,... | collective-permute-start | bytes 307208 | tf_op jit(solution)/shard_map/ppermute | solution.py:271
  74.9 7.1 %collective-permute-start.3 = (bf16[200,256]{1,0:T(8,128)(2,1)S(1)}, bf16[200,256]{1,0:T(8,128)(2,1)S(1)}, u32[]{:S(2)}, u32[]{:S(2)}) collective-permute-start(bf16[200,256]{1,0:T(8,128)(2,1)S(1)} %add_up.1), channel_id=1, source_target_pairs={{0,128},{1,129},{16,144},{17,145},{32,160},{33,161},{48,176},{49,1... | collective-permute-start | bytes 307208 | tf_op jit(solution)/shard_map/ppermute | solution.py:271
  78.3 11.4 %collective-permute-start.6 = (bf16[2,200,256]{2,1,0:T(8,128)(2,1)S(1)}, bf16[2,200,256]{2,1,0:T(8,128)(2,1)S(1)}, u32[]{:S(2)}, u32[]{:S(2)}) collective-permute-start(bf16[2,200,256]{2,1,0:T(8,128)(2,1)S(1)} %pad_maximum_fusion), channel_id=1, source_target_pairs={{0,128},{1,129},{16,144},{17,145},{32,160},{33,161},{48,176},{49,1... | collective-permute-start | bytes 614408 | tf_op jit(solution)/shard_map/ppermute | solution.py:271
  78.7 6.1 %collective-permute-start.4 = (bf16[200,256]{1,0:T(8,128)(2,1)S(1)}, bf16[200,256]{1,0:T(8,128)(2,1)S(1)}, u32[]{:S(2)}, u32[]{:S(2)}) collective-permute-start(bf16[200,256]{1,0:T(8,128)(2,1)S(1)} %collective-permute-done.1), channel_id=1, source_target_pairs={{0,16},{1,113},{16,32},{17,1},{32,48},{33,17},{48,64},{49,33},{64,... | collective-permute-start | bytes 307208 | tf_op jit(solution)/shard_map/ppermute | solution.py:271
  79.8 5.0 %collective-permute-start.5 = (bf16[200,256]{1,0:T(8,128)(2,1)S(1)}, bf16[200,256]{1,0:T(8,128)(2,1)S(1)}, u32[]{:S(2)}, u32[]{:S(2)}) collective-permute-start(bf16[200,256]{1,0:T(8,128)(2,1)S(1)} %collective-permute-done.2), channel_id=1, source_target_pairs={{0,112},{1,17},{16,0},{17,33},{32,16},{33,49},{48,32},{49,65},{64,... | collective-permute-start | bytes 307208 | tf_op jit(solution)/shard_map/ppermute | solution.py:271
  84.8 11.4 %collective-permute-start.9 = (bf16[2,200,256]{2,1,0:T(8,128)(2,1)S(1)}, bf16[2,200,256]{2,1,0:T(8,128)(2,1)S(1)}, u32[]{:S(2)}, u32[]{:S(2)}) collective-permute-start(bf16[2,200,256]{2,1,0:T(8,128)(2,1)S(1)} %pad_maximum_fusion.1), channel_id=1, source_target_pairs={{0,128},{1,129},{16,144},{17,145},{32,160},{33,161},{48,176},{49,1... | collective-permute-start | bytes 614408 | tf_op jit(solution)/shard_map/ppermute | solution.py:271
  86.4 5.9 %collective-permute-start.7 = (bf16[200,256]{1,0:T(8,128)(2,1)S(1)}, bf16[200,256]{1,0:T(8,128)(2,1)S(1)}, u32[]{:S(2)}, u32[]{:S(2)}) collective-permute-start(bf16[200,256]{1,0:T(8,128)(2,1)S(1)} %collective-permute-done.4), channel_id=1, source_target_pairs={{0,16},{1,113},{16,32},{17,1},{32,48},{33,17},{48,64},{49,33},{64,... | collective-permute-start | bytes 307208 | tf_op jit(solution)/shard_map/ppermute | solution.py:271
  87.7 4.7 %collective-permute-start.8 = (bf16[200,256]{1,0:T(8,128)(2,1)S(1)}, bf16[200,256]{1,0:T(8,128)(2,1)S(1)}, u32[]{:S(2)}, u32[]{:S(2)}) collective-permute-start(bf16[200,256]{1,0:T(8,128)(2,1)S(1)} %collective-permute-done.5), channel_id=1, source_target_pairs={{0,112},{1,17},{16,0},{17,33},{32,16},{33,49},{48,32},{49,65},{64,... | collective-permute-start | bytes 307208 | tf_op jit(solution)/shard_map/ppermute | solution.py:271
  92.4 5.8 %collective-permute-start.10 = (bf16[2,200,256]{2,1,0:T(8,128)(2,1)S(1)}, bf16[2,200,256]{2,1,0:T(8,128)(2,1)S(1)}, u32[]{:S(2)}, u32[]{:S(2)}) collective-permute-start(bf16[2,200,256]{2,1,0:T(8,128)(2,1)S(1)} %pad_maximum_fusion.2), channel_id=1, source_target_pairs={{0,128},{1,129},{16,144},{17,145},{32,160},{33,161},{48,176},{49,1... | collective-permute-start | bytes 614408 | tf_op jit(solution)/shard_map/ppermute | solution.py:271
  93.3 5.1 %collective-permute-start.11 = (bf16[200,256]{1,0:T(8,128)(2,1)S(1)}, bf16[200,256]{1,0:T(8,128)(2,1)S(1)}, u32[]{:S(2)}, u32[]{:S(2)}) collective-permute-start(bf16[200,256]{1,0:T(8,128)(2,1)S(1)} %collective-permute-done.8), channel_id=1, source_target_pairs={{0,112},{1,17},{16,0},{17,33},{32,16},{33,49},{48,32},{49,65},{64,... | collective-permute-start | bytes 307208 | tf_op jit(solution)/shard_map/ppermute | solution.py:271
  96.1 6.8 %collective-permute-start.12 = (bf16[200,256]{1,0:T(8,128)(2,1)S(1)}, bf16[200,256]{1,0:T(8,128)(2,1)S(1)}, u32[]{:S(2)}, u32[]{:S(2)}) collective-permute-start(bf16[200,256]{1,0:T(8,128)(2,1)S(1)} %collective-permute-done.7), channel_id=1, source_target_pairs={{0,144},{1,241},{16,160},{17,129},{32,176},{33,145},{48,192},{49,1... | collective-permute-start | bytes 307208 | tf_op jit(solution)/shard_map/ppermute | solution.py:271
  102.9 1.2 %copy-start.2 = (bf16[2,8,200,256]{3,2,1,0:T(8,128)(2,1)}, bf16[2,8,200,256]{3,2,1,0:T(8,128)(2,1)S(1)}, u32[]{:S(2)}) copy-start(bf16[2,8,200,256]{3,2,1,0:T(8,128)(2,1)S(1)} %bitcast_dynamic-update-slice_fusion) | copy-start | bytes 4915204

commit v5 on v4

--- a/solution.py
+++ b/solution.py
@@ -74,22 +74,27 @@
 
 
 def relayout_kernel(jac_ref, out_ref, in_buf, out_buf, left_ref, right_ref, in_sem, out_sem):
-    chunks, many, b, slots = in_buf.shape
-
-    def bring(c):
-        return pltpu.make_async_copy(jac_ref.at[pl.ds(c * many, many)], in_buf.at[c], in_sem.at[c])
-
-    def send(c):
-        return pltpu.make_async_copy(out_buf.at[c], out_ref.at[:, pl.ds(c * many, many), :], out_sem.at[c])
-
-    for c in range(chunks):
-        bring(c).start()
-    for c in range(chunks):
-        bring(c).wait()
-
+    groups, _, b, slots = in_buf.shape
+    chunks, _, many, _ = out_buf.shape
+    per_chunk = many // DEPTH
+    head = per_chunk // 2 * DEPTH
+
+    def bring(g):
+        return pltpu.make_async_copy(jac_ref.at[pl.ds(g * DEPTH, DEPTH)], in_buf.at[g], in_sem.at[g])
+
+    def send(c, start, count, sem):
+        at = pl.ds(c * many + start, count)
+        return pltpu.make_async_copy(out_buf.at[c, :, pl.ds(start, count), :], out_ref.at[:, at, :], out_sem.at[sem])
+
+    for g in range(groups):
+        bring(g).start()
+
+    def lay(c, first, last):
         def some(group, _):
+            g = c * per_chunk + group
+            bring(g).wait()
             for d in range(DEPTH):
-                block = in_buf[c, group * DEPTH + d].astype(jnp.float32)
+                block = in_buf[g, d].astype(jnp.float32)
                 at = pl.ds(d * PITCH, slots)
                 left_ref[at, :] = jnp.transpose(block[:LANES])
                 right_ref[at, pl.ds(0, b - LANES)] = jnp.transpose(block[LANES:])
@@ -100,10 +105,15 @@
                 out_buf[c, s, rows, pl.ds(LANES, b - LANES)] = right_ref[at, :][:, : b - LANES].astype(jnp.bfloat16)
             return 0
 
-        lax.fori_loop(0, many // DEPTH, some, 0)
-        send(c).start()
-    for c in range(chunks):
-        send(c).wait()
+        lax.fori_loop(first, last, some, 0)
+
+    parts = [(c, 0, many, c) for c in range(chunks - 1)]
+    parts += [(chunks - 1, 0, head, chunks - 1), (chunks - 1, head, many - head, chunks)]
+    for c, start, count, sem in parts:
+        lay(c, start // DEPTH, (start + count) // DEPTH)
+        send(c, start, count, sem).start()
+    for c, start, count, sem in parts:
+        send(c, start, count, sem).wait()
 
 
 def relayout(jac):
@@ -117,12 +127,12 @@
         in_specs=[anywhere],
         out_specs=anywhere,
         scratch_shapes=[
-            pltpu.VMEM((CHUNKS, many, b, slots), jac.dtype),
+            pltpu.VMEM((d // DEPTH, DEPTH, b, slots), jac.dtype),
             pltpu.VMEM((CHUNKS, slots, many, b), jac.dtype),
             scratch,
             scratch,
-            pltpu.SemaphoreType.DMA((CHUNKS,)),
-            pltpu.SemaphoreType.DMA((CHUNKS,)),
+            pltpu.SemaphoreType.DMA((d // DEPTH,)),
+            pltpu.SemaphoreType.DMA((CHUNKS + 1,)),
         ],
         compiler_params=params(40),
         name="relayout",

time: 106 us -> 105 us (level)
  transfers between devices with their start and end apart: 14 -> 14, of which waited for: 7 -> 7; matrix products, arithmetic and copies ran while one was open for 0% -> 0% of each run, Pallas kernels for 10% -> 9%
where the time goes in v5:
time: 105 us; the launch traced here: 103 us
  waiting for transfers between devices  36.2 us (34%)
  starting transfers between devices  25.9 us (25%)
  Pallas kernels  20 us (19%)
  blocking collectives  18.8 us (18%)
  local copies, waits for them, and re-layouts  1.51 us (1%)
    all_to_all x1, waiting for transfers between devices, on_device(): lax.all_to_all(terms, ROW + ('core',), 0, 0, axis_index_groups=both_ways(...  21.5 us
    all_to_all x1, blocking collectives, on_device(): lax.all_to_all(copies, COL, 0, 0, axis_index_groups=both_ways(range(8)))  18.8 us
    ppermute x12, starting transfers between devices, send(): return lax.ppermute(piece, ('xlo', 'z', 'core'), shift(turn, cross))  16 us
    ppermute x12, waiting for transfers between devices, send(): return lax.ppermute(piece, ('xlo', 'z', 'core'), shift(turn, cross))  14.8 us
    all_to_all x1, starting transfers between devices, on_device(): lax.all_to_all(terms, ROW + ('core',), 0, 0, axis_index_groups=both_ways(...  9.95 us
    pallas_call x1, Pallas kernels, relayout(): pl.pallas_call(relayout_kernel, out_shape=pltpu.HBM((slots, d, b), jac.dt...  9.56 us
    pallas_call x1, Pallas kernels, make_terms(): pl.pallas_call(terms_kernel, out_shape=pltpu.HBM((k, b + 8, slots), jnp.i...  7.29 us
  transfers between devices with their start and end apart: 14, of which 7 were waited for; matrix products, arithmetic and copies ran while one was open for 0% of the time, Pallas kernels for 9%

profile of v5, /device:TPU:2, one launch (start us, length us, event | category | flops | bytes accessed | tf_op | source)
XLA Modules:
  0.0 103.4 jit_solution(12639865004271714443)
XLA Ops:
  0.0 1.9 %flip.1 = bf16[8,200,256]{2,1,0:T(8,128)(2,1)} custom-call(bf16[256,200]{1,0:T(8,128)(2,1)} %bitcast.68), custom_call_target="tpu_custom_call" | custom-call | tf_op jit(solution)/shard_map/flip/pallas_call | solution.py:60
  1.9 18.8 %all_to_all.10.own_ref = bf16[8,200,256]{2,1,0:T(8,128)(2,1)S(1)} all-to-all(bf16[8,200,256]{2,1,0:T(8,128)(2,1)} %flip.1), channel_id=1, replica_groups={{0,2,4,6,8,10,12,14},{15,13,11,9,7,5,3,1},{16,18,20,22,24,26,28,30},{31..., dimensions={0} | all-to-all | bytes 1638400 | tf_op jit(solution)/shard_map/all_to_all | solution.py:316
  20.7 0.0 collective-permute-start
  20.7 0.0 copy-start
  20.7 0.0 copy-start.1
  20.7 9.6 %relayout.1.jac_ref = bf16[128,200,200]{2,1,0:T(8,128)(2,1)} custom-call(bf16[200,200,128]{2,1,0:T(8,128)(2,1)} %bitcast.61), custom_call_target="tpu_custom_call" | custom-call | tf_op jit(solution)/shard_map/relayout/pallas_call | solution.py:124
  31.0 0.0 collective-permute-done.other_ref
  31.0 0.0 copy-done
  31.0 0.0 copy-done.1
  31.0 7.3 %terms.1 = s16[16,208,128]{2,1,0:T(8,128)(2,1)} custom-call(s32[128]{0:T(128)S(1)} %bitcast.59, s32[1,1]{1,0:T(1,128)S(6)} %copy.22.count_ref, s32[1,128]{1,0:T(1,128)S(1)} %bitcast.60, bf16[8,200,256]{2,1,0:T(8,128)(2,1)S(1)} %all_to_all.10.own_ref, bf16[8,200,256]{2,1,0:T(8,128)(2,1)S(1)} %collective-permute-done.other_ref, ...), custom_call_target="tpu_custom_call" | custom-call | tf_op jit(solution)/shard_map/terms/pallas_call | solution.py:206
  38.3 10.0 %all-to-all-start.1 = ((s16[16,208,128]{2,1,0:T(8,128)(2,1)}), s16[16,208,128]{2,1,0:T(8,128)(2,1)S(1)}, u32[]{:S(2)}, u32[]{:S(2)}) async-start(s16[16,208,128]{2,1,0:T(8,128)(2,1)} %terms.1), calls=%async_computation.1 | async-start | bytes 1703936 | tf_op jit(solution)/shard_map/all_to_all | solution.py:320
  48.2 21.5 %all-to-all-done.1.got_ref = s16[16,208,128]{2,1,0:T(8,128)(2,1)S(1)} async-done(((s16[16,208,128]{2,1,0:T(8,128)(2,1)}), s16[16,208,128]{2,1,0:T(8,128)(2,1)S(1)}, u32[]{:S(2)}, u32[]{:S(2)}) %all-to-all-start.1) | async-done | bytes 852000 | tf_op jit(solution)/shard_map/all_to_all | solution.py:320
  69.7 1.2 %add_up.1 = bf16[200,256]{1,0:T(8,128)(2,1)S(1)} custom-call(s16[16,208,128]{2,1,0:T(8,128)(2,1)S(1)} %all-to-all-done.1.got_ref), custom_call_target="tpu_custom_call" | custom-call | tf_op jit(solution)/shard_map/add_up/pallas_call | solution.py:248
  70.9 0.5 collective-permute-start.1
  71.5 2.8 %collective-permute-start.2 = (bf16[200,256]{1,0:T(8,128)(2,1)S(1)}, bf16[200,256]{1,0:T(8,128)(2,1)S(1)}, u32[]{:S(2)}, u32[]{:S(2)}) collective-permute-start(bf16[200,256]{1,0:T(8,128)(2,1)S(1)} %add_up.1), channel_id=1, source_target_pairs={{0,112},{1,17},{16,0},{17,33},{32,16},{33,49},{48,32},{49,65},{64,... | collective-permute-start | bytes 307208 | tf_op jit(solution)/shard_map/ppermute | solution.py:281
  74.3 0.4 collective-permute-start.3
  74.6 0.1 broadcast_in_dim.33
  74.8 2.8 %collective-permute-done.1 = bf16[200,256]{1,0:T(8,128)(2,1)S(1)} collective-permute-done((bf16[200,256]{1,0:T(8,128)(2,1)S(1)}, bf16[200,256]{1,0:T(8,128)(2,1)S(1)}, u32[]{:S(2)}, u32[]{:S(2)}) %collective-permute-start.1) | collective-permute-done | bytes 102432 | tf_op jit(solution)/shard_map/ppermute | solution.py:281
  77.6 0.0 collective-permute-done.2
  77.6 0.4 collective-permute-start.6
  78.0 1.1 %collective-permute-start.4 = (bf16[200,256]{1,0:T(8,128)(2,1)S(1)}, bf16[200,256]{1,0:T(8,128)(2,1)S(1)}, u32[]{:S(2)}, u32[]{:S(2)}) collective-permute-start(bf16[200,256]{1,0:T(8,128)(2,1)S(1)} %collective-permute-done.1), channel_id=1, source_target_pairs={{0,16},{1,113},{16,32},{17,1},{32,48},{33,17},{48,64},{49,33},{64,... | collective-permute-start | bytes 307208 | tf_op jit(solution)/shard_map/ppermute | solution.py:281
  79.1 2.1 %collective-permute-start.5 = (bf16[200,256]{1,0:T(8,128)(2,1)S(1)}, bf16[200,256]{1,0:T(8,128)(2,1)S(1)}, u32[]{:S(2)}, u32[]{:S(2)}) collective-permute-start(bf16[200,256]{1,0:T(8,128)(2,1)S(1)} %collective-permute-done.2), channel_id=1, source_target_pairs={{0,112},{1,17},{16,0},{17,33},{32,16},{33,49},{48,32},{49,65},{64,... | collective-permute-start | bytes 307208 | tf_op jit(solution)/shard_map/ppermute | solution.py:281
  81.3 0.0 collective-permute-done.3
  81.4 2.7 %collective-permute-done.4 = bf16[200,256]{1,0:T(8,128)(2,1)S(1)} collective-permute-done((bf16[200,256]{1,0:T(8,128)(2,1)S(1)}, bf16[200,256]{1,0:T(8,128)(2,1)S(1)}, u32[]{:S(2)}, u32[]{:S(2)}) %collective-permute-start.4) | collective-permute-done | bytes 102432 | tf_op jit(solution)/shard_map/ppermute | solution.py:281
  84.1 0.0 collective-permute-done.5
  84.1 1.7 %collective-permute-start.9 = (bf16[2,200,256]{2,1,0:T(8,128)(2,1)S(1)}, bf16[2,200,256]{2,1,0:T(8,128)(2,1)S(1)}, u32[]{:S(2)}, u32[]{:S(2)}) collective-permute-start(bf16[2,200,256]{2,1,0:T(8,128)(2,1)S(1)} %pad_maximum_fusion.1), channel_id=1, source_target_pairs={{0,128},{1,129},{16,144},{17,145},{32,160},{33,161},{48,176},{49,1... | collective-permute-start | bytes 614408 | tf_op jit(solution)/shard_map/ppermute | solution.py:281
  85.8 1.2 %collective-permute-start.7 = (bf16[200,256]{1,0:T(8,128)(2,1)S(1)}, bf16[200,256]{1,0:T(8,128)(2,1)S(1)}, u32[]{:S(2)}, u32[]{:S(2)}) collective-permute-start(bf16[200,256]{1,0:T(8,128)(2,1)S(1)} %collective-permute-done.4), channel_id=1, source_target_pairs={{0,16},{1,113},{16,32},{17,1},{32,48},{33,17},{48,64},{49,33},{64,... | collective-permute-start | bytes 307208 | tf_op jit(solution)/shard_map/ppermute | solution.py:281
  87.0 2.0 %collective-permute-start.8 = (bf16[200,256]{1,0:T(8,128)(2,1)S(1)}, bf16[200,256]{1,0:T(8,128)(2,1)S(1)}, u32[]{:S(2)}, u32[]{:S(2)}) collective-permute-start(bf16[200,256]{1,0:T(8,128)(2,1)S(1)} %collective-permute-done.5), channel_id=1, source_target_pairs={{0,112},{1,17},{16,0},{17,33},{32,16},{33,49},{48,32},{49,65},{64,... | collective-permute-start | bytes 307208 | tf_op jit(solution)/shard_map/ppermute | solution.py:281
  89.1 0.0 collective-permute-done.6
  89.1 2.5 %collective-permute-done.7 = bf16[200,256]{1,0:T(8,128)(2,1)S(1)} collective-permute-done((bf16[200,256]{1,0:T(8,128)(2,1)S(1)}, bf16[200,256]{1,0:T(8,128)(2,1)S(1)}, u32[]{:S(2)}, u32[]{:S(2)}) %collective-permute-start.7) | collective-permute-done | bytes 102432 | tf_op jit(solution)/shard_map/ppermute | solution.py:281
  91.7 0.0 collective-permute-done.8
  91.7 0.9 collective-permute-start.10
  92.6 2.8 %collective-permute-start.11 = (bf16[200,256]{1,0:T(8,128)(2,1)S(1)}, bf16[200,256]{1,0:T(8,128)(2,1)S(1)}, u32[]{:S(2)}, u32[]{:S(2)}) collective-permute-start(bf16[200,256]{1,0:T(8,128)(2,1)S(1)} %collective-permute-done.8), channel_id=1, source_target_pairs={{0,112},{1,17},{16,0},{17,33},{32,16},{33,49},{48,32},{49,65},{64,... | collective-permute-start | bytes 307208 | tf_op jit(solution)/shard_map/ppermute | solution.py:281
  95.5 0.0 collective-permute-start.12
  95.5 0.0 collective-permute-done.9
  95.6 2.0 %collective-permute-done.10 = bf16[2,200,256]{2,1,0:T(8,128)(2,1)S(1)} collective-permute-done((bf16[2,200,256]{2,1,0:T(8,128)(2,1)S(1)}, bf16[2,200,256]{2,1,0:T(8,128)(2,1)S(1)}, u32[]{:S(2)}, u32[]{:S(2)}) %collective-permute-start.10) | collective-permute-done | bytes 204832 | tf_op jit(solution)/shard_map/ppermute | solution.py:281
  97.6 0.1 collective-permute-done.11
  97.7 4.5 %collective-permute-done.12 = bf16[200,256]{1,0:T(8,128)(2,1)S(1)} collective-permute-done((bf16[200,256]{1,0:T(8,128)(2,1)S(1)}, bf16[200,256]{1,0:T(8,128)(2,1)S(1)}, u32[]{:S(2)}, u32[]{:S(2)}) %collective-permute-start.12) | collective-permute-done | bytes 102432 | tf_op jit(solution)/shard_map/ppermute | solution.py:281
  102.2 0.0 copy-start.2
  102.3 1.2 %copy-done.2 = bf16[2,8,200,256]{3,2,1,0:T(8,128)(2,1)} copy-done((bf16[2,8,200,256]{3,2,1,0:T(8,128)(2,1)}, bf16[2,8,200,256]{3,2,1,0:T(8,128)(2,1)S(1)}, u32[]{:S(2)}) %copy-start.2) | copy-done | bytes 1638424
  (19 shorter events, 0.3 us)
Async XLA Ops:
  20.7 10.2 %collective-permute-start = (bf16[8,200,256]{2,1,0:T(8,128)(2,1)S(1)}, bf16[8,200,256]{2,1,0:T(8,128)(2,1)S(1)}, u32[]{:S(2)}, u32[]{:S(2)}) collective-permute-start(bf16[8,200,256]{2,1,0:T(8,128)(2,1)S(1)} %all_to_all.10.own_ref), channel_id=1, source_target_pairs={{0,1},{1,0},{2,3},{3,2},{4,5},{5,4},{6,7},{7,6},{8,9},{9,8},{10,11... | collective-permute-start | bytes 2457608 | tf_op jit(solution)/shard_map/ppermute | solution.py:317
  20.7 10.2 %copy-start = (s32[1,1,128]{2,1,0:T(1,128)S(1)}, s32[1,1,128]{2,1,0:T(1,128)}, u32[]{:S(2)}) copy-start(s32[1,1,128]{2,1,0:T(1,128)} %param.7) | copy-start | bytes 1540
  20.7 10.2 %copy-start.1 = (s32[1,1,128]{2,1,0:T(1,128)S(1)}, s32[1,1,128]{2,1,0:T(1,128)}, u32[]{:S(2)}) copy-start(s32[1,1,128]{2,1,0:T(1,128)} %param.8) | copy-start | bytes 1540
  38.3 31.4 %all-to-all-start.1 = ((s16[16,208,128]{2,1,0:T(8,128)(2,1)}), s16[16,208,128]{2,1,0:T(8,128)(2,1)S(1)}, u32[]{:S(2)}, u32[]{:S(2)}) async-start(s16[16,208,128]{2,1,0:T(8,128)(2,1)} %terms.1), calls=%async_computation.1 | async-start | bytes 1703936 | tf_op jit(solution)/shard_map/all_to_all | solution.py:320
  70.9 6.6 %collective-permute-start.1 = (bf16[200,256]{1,0:T(8,128)(2,1)S(1)}, bf16[200,256]{1,0:T(8,128)(2,1)S(1)}, u32[]{:S(2)}, u32[]{:S(2)}) collective-permute-start(bf16[200,256]{1,0:T(8,128)(2,1)S(1)} %add_up.1), channel_id=1, source_target_pairs={{0,16},{1,113},{16,32},{17,1},{32,48},{33,17},{48,64},{49,33},{64,... | collective-permute-start | bytes 307208 | tf_op jit(solution)/shard_map/ppermute | solution.py:281
  71.5 6.1 %collective-permute-start.2 = (bf16[200,256]{1,0:T(8,128)(2,1)S(1)}, bf16[200,256]{1,0:T(8,128)(2,1)S(1)}, u32[]{:S(2)}, u32[]{:S(2)}) collective-permute-start(bf16[200,256]{1,0:T(8,128)(2,1)S(1)} %add_up.1), channel_id=1, source_target_pairs={{0,112},{1,17},{16,0},{17,33},{32,16},{33,49},{48,32},{49,65},{64,... | collective-permute-start | bytes 307208 | tf_op jit(solution)/shard_map/ppermute | solution.py:281
  74.3 7.1 %collective-permute-start.3 = (bf16[200,256]{1,0:T(8,128)(2,1)S(1)}, bf16[200,256]{1,0:T(8,128)(2,1)S(1)}, u32[]{:S(2)}, u32[]{:S(2)}) collective-permute-start(bf16[200,256]{1,0:T(8,128)(2,1)S(1)} %add_up.1), channel_id=1, source_target_pairs={{0,128},{1,129},{16,144},{17,145},{32,160},{33,161},{48,176},{49,1... | collective-permute-start | bytes 307208 | tf_op jit(solution)/shard_map/ppermute | solution.py:281
  77.6 11.4 %collective-permute-start.6 = (bf16[2,200,256]{2,1,0:T(8,128)(2,1)S(1)}, bf16[2,200,256]{2,1,0:T(8,128)(2,1)S(1)}, u32[]{:S(2)}, u32[]{:S(2)}) collective-permute-start(bf16[2,200,256]{2,1,0:T(8,128)(2,1)S(1)} %pad_maximum_fusion), channel_id=1, source_target_pairs={{0,128},{1,129},{16,144},{17,145},{32,160},{33,161},{48,176},{49,1... | collective-permute-start | bytes 614408 | tf_op jit(solution)/shard_map/ppermute | solution.py:281
  78.0 6.1 %collective-permute-start.4 = (bf16[200,256]{1,0:T(8,128)(2,1)S(1)}, bf16[200,256]{1,0:T(8,128)(2,1)S(1)}, u32[]{:S(2)}, u32[]{:S(2)}) collective-permute-start(bf16[200,256]{1,0:T(8,128)(2,1)S(1)} %collective-permute-done.1), channel_id=1, source_target_pairs={{0,16},{1,113},{16,32},{17,1},{32,48},{33,17},{48,64},{49,33},{64,... | collective-permute-start | bytes 307208 | tf_op jit(solution)/shard_map/ppermute | solution.py:281
  79.1 5.0 %collective-permute-start.5 = (bf16[200,256]{1,0:T(8,128)(2,1)S(1)}, bf16[200,256]{1,0:T(8,128)(2,1)S(1)}, u32[]{:S(2)}, u32[]{:S(2)}) collective-permute-start(bf16[200,256]{1,0:T(8,128)(2,1)S(1)} %collective-permute-done.2), channel_id=1, source_target_pairs={{0,112},{1,17},{16,0},{17,33},{32,16},{33,49},{48,32},{49,65},{64,... | collective-permute-start | bytes 307208 | tf_op jit(solution)/shard_map/ppermute | solution.py:281
  84.1 11.4 %collective-permute-start.9 = (bf16[2,200,256]{2,1,0:T(8,128)(2,1)S(1)}, bf16[2,200,256]{2,1,0:T(8,128)(2,1)S(1)}, u32[]{:S(2)}, u32[]{:S(2)}) collective-permute-start(bf16[2,200,256]{2,1,0:T(8,128)(2,1)S(1)} %pad_maximum_fusion.1), channel_id=1, source_target_pairs={{0,128},{1,129},{16,144},{17,145},{32,160},{33,161},{48,176},{49,1... | collective-permute-start | bytes 614408 | tf_op jit(solution)/shard_map/ppermute | solution.py:281
  85.8 5.9 %collective-permute-start.7 = (bf16[200,256]{1,0:T(8,128)(2,1)S(1)}, bf16[200,256]{1,0:T(8,128)(2,1)S(1)}, u32[]{:S(2)}, u32[]{:S(2)}) collective-permute-start(bf16[200,256]{1,0:T(8,128)(2,1)S(1)} %collective-permute-done.4), channel_id=1, source_target_pairs={{0,16},{1,113},{16,32},{17,1},{32,48},{33,17},{48,64},{49,33},{64,... | collective-permute-start | bytes 307208 | tf_op jit(solution)/shard_map/ppermute | solution.py:281
  87.0 4.7 %collective-permute-start.8 = (bf16[200,256]{1,0:T(8,128)(2,1)S(1)}, bf16[200,256]{1,0:T(8,128)(2,1)S(1)}, u32[]{:S(2)}, u32[]{:S(2)}) collective-permute-start(bf16[200,256]{1,0:T(8,128)(2,1)S(1)} %collective-permute-done.5), channel_id=1, source_target_pairs={{0,112},{1,17},{16,0},{17,33},{32,16},{33,49},{48,32},{49,65},{64,... | collective-permute-start | bytes 307208 | tf_op jit(solution)/shard_map/ppermute | solution.py:281
  91.7 5.8 %collective-permute-start.10 = (bf16[2,200,256]{2,1,0:T(8,128)(2,1)S(1)}, bf16[2,200,256]{2,1,0:T(8,128)(2,1)S(1)}, u32[]{:S(2)}, u32[]{:S(2)}) collective-permute-start(bf16[2,200,256]{2,1,0:T(8,128)(2,1)S(1)} %pad_maximum_fusion.2), channel_id=1, source_target_pairs={{0,128},{1,129},{16,144},{17,145},{32,160},{33,161},{48,176},{49,1... | collective-permute-start | bytes 614408 | tf_op jit(solution)/shard_map/ppermute | solution.py:281
  92.6 5.1 %collective-permute-start.11 = (bf16[200,256]{1,0:T(8,128)(2,1)S(1)}, bf16[200,256]{1,0:T(8,128)(2,1)S(1)}, u32[]{:S(2)}, u32[]{:S(2)}) collective-permute-start(bf16[200,256]{1,0:T(8,128)(2,1)S(1)} %collective-permute-done.8), channel_id=1, source_target_pairs={{0,112},{1,17},{16,0},{17,33},{32,16},{33,49},{48,32},{49,65},{64,... | collective-permute-start | bytes 307208 | tf_op jit(solution)/shard_map/ppermute | solution.py:281
  95.5 6.8 %collective-permute-start.12 = (bf16[200,256]{1,0:T(8,128)(2,1)S(1)}, bf16[200,256]{1,0:T(8,128)(2,1)S(1)}, u32[]{:S(2)}, u32[]{:S(2)}) collective-permute-start(bf16[200,256]{1,0:T(8,128)(2,1)S(1)} %collective-permute-done.7), channel_id=1, source_target_pairs={{0,144},{1,241},{16,160},{17,129},{32,176},{33,145},{48,192},{49,1... | collective-permute-start | bytes 307208 | tf_op jit(solution)/shard_map/ppermute | solution.py:281
  102.2 1.2 %copy-start.2 = (bf16[2,8,200,256]{3,2,1,0:T(8,128)(2,1)}, bf16[2,8,200,256]{3,2,1,0:T(8,128)(2,1)S(1)}, u32[]{:S(2)}) copy-start(bf16[2,8,200,256]{3,2,1,0:T(8,128)(2,1)S(1)} %bitcast_dynamic-update-slice_fusion) | copy-start | bytes 4915204

commit v6 on v5

--- a/solution.py
+++ b/solution.py
@@ -16,7 +16,7 @@
 CHUNKS = 5
 PITCH = 132
 TERM_PITCH = 20
-GROUP = 16
+GROUP = 8
 BITS = 15
 LIMIT = 32767.0
 TINY = 1e-30
@@ -158,8 +158,14 @@
     def send(i):
         return pltpu.make_async_copy(out_buf.at[i], out_ref.at[i], out_sem.at[i])
 
-    for c in range(slots // GROUP):
+    groups = slots // GROUP
+    live = jnp.minimum((count_ref[0, 0] + GROUP - 1) // GROUP, groups)
+
+    def fetch(c, _):
         bring(c).start()
+        return 0
+
+    lax.fori_loop(0, live, fetch, 0)
     for i in range(pieces):
         faces_ref[pl.ds(i * per, per), pl.ds(0, b)] = jnp.transpose(own_ref[i])
         faces_ref[pl.ds((pieces + i) * per, per), pl.ds(0, b)] = jnp.transpose(other_ref[i])
@@ -180,7 +186,15 @@
             right_ref[at, pl.ds(0, b - LANES)] = term[:, LANES:]
         return 0
 
-    lax.fori_loop(0, slots // GROUP, some, 0)
+    def clear(c, _):
+        height = GROUP * TERM_PITCH
+        at = pl.ds(pl.multiple_of(c * height, 8), height)
+        left_ref[at, :] = jnp.zeros((height, LANES), jnp.float32)
+        right_ref[at, :] = jnp.zeros((height, LANES), jnp.float32)
+        return 0
+
+    lax.fori_loop(0, live, some, 0)
+    lax.fori_loop(live, groups, clear, 0)
     meta_row = lax.broadcasted_iota(jnp.int32, (8, slots), 0)
     slot_index = lax.broadcasted_iota(jnp.int32, (1, slots), 1)
     cols = jnp.where(slot_index < count_ref[0, 0], cols_ref[...], -1).astype(jnp.float32)

time: 105 us -> 104 us (level)
  Pallas kernels: 20 us -> 17.6 us
  waiting for transfers between devices: 36.2 us -> 37.5 us
    pallas_call x1, Pallas kernels: 7.29 us -> 4.86 us  [make_terms(): pl.pallas_call(terms_kernel, out_shape=pltpu.HBM((k, b + 8, slots), jnp.i...]
  transfers between devices with their start and end apart: 14 -> 14, of which waited for: 7 -> 6; matrix products, arithmetic and copies ran while one was open for 0% -> 0% of each run, Pallas kernels for 9% -> 9%
where the time goes in v6:
time: 104 us; the launch traced here: 102 us
  waiting for transfers between devices  37.5 us (36%)
  starting transfers between devices  25.8 us (25%)
  blocking collectives  18.8 us (18%)
  Pallas kernels  17.6 us (17%)
  local copies, waits for them, and re-layouts  1.52 us (1%)
    all_to_all x1, waiting for transfers between devices, on_device(): lax.all_to_all(terms, ROW + ('core',), 0, 0, axis_index_groups=both_ways(...  21.9 us
    all_to_all x1, blocking collectives, on_device(): lax.all_to_all(copies, COL, 0, 0, axis_index_groups=both_ways(range(8)))  18.8 us
    ppermute x12, starting transfers between devices, send(): return lax.ppermute(piece, ('xlo', 'z', 'core'), shift(turn, cross))  15.8 us
    ppermute x12, waiting for transfers between devices, send(): return lax.ppermute(piece, ('xlo', 'z', 'core'), shift(turn, cross))  15.5 us
    all_to_all x1, starting transfers between devices, on_device(): lax.all_to_all(terms, ROW + ('core',), 0, 0, axis_index_groups=both_ways(...  9.98 us
    pallas_call x1, Pallas kernels, relayout(): pl.pallas_call(relayout_kernel, out_shape=pltpu.HBM((slots, d, b), jac.dt...  9.56 us
    pallas_call x1, Pallas kernels, make_terms(): pl.pallas_call(terms_kernel, out_shape=pltpu.HBM((k, b + 8, slots), jnp.i...  4.86 us
  transfers between devices with their start and end apart: 14, of which 6 were waited for; matrix products, arithmetic and copies ran while one was open for 0% of the time, Pallas kernels for 9%

profile of v6, /device:TPU:2, one launch (start us, length us, event | category | flops | bytes accessed | tf_op | source)
XLA Modules:
  0.0 102.1 jit_solution(8683277813613000415)
XLA Ops:
  0.0 1.9 %flip.1 = bf16[8,200,256]{2,1,0:T(8,128)(2,1)} custom-call(bf16[256,200]{1,0:T(8,128)(2,1)} %bitcast.68), custom_call_target="tpu_custom_call" | custom-call | tf_op jit(solution)/shard_map/flip/pallas_call | solution.py:60
  1.9 18.8 %all_to_all.10.own_ref = bf16[8,200,256]{2,1,0:T(8,128)(2,1)S(1)} all-to-all(bf16[8,200,256]{2,1,0:T(8,128)(2,1)} %flip.1), channel_id=1, replica_groups={{0,2,4,6,8,10,12,14},{15,13,11,9,7,5,3,1},{16,18,20,22,24,26,28,30},{31..., dimensions={0} | all-to-all | bytes 1638400 | tf_op jit(solution)/shard_map/all_to_all | solution.py:330
  20.7 0.0 collective-permute-start
  20.7 0.0 copy-start
  20.7 0.0 copy-start.1
  20.7 9.6 %relayout.1.jac_ref = bf16[128,200,200]{2,1,0:T(8,128)(2,1)} custom-call(bf16[200,200,128]{2,1,0:T(8,128)(2,1)} %bitcast.61), custom_call_target="tpu_custom_call" | custom-call | tf_op jit(solution)/shard_map/relayout/pallas_call | solution.py:124
  31.0 0.0 collective-permute-done.other_ref
  31.0 0.0 copy-done
  31.0 0.0 copy-done.1
  31.0 4.9 %terms.1 = s16[16,208,128]{2,1,0:T(8,128)(2,1)} custom-call(s32[128]{0:T(128)S(1)} %bitcast.59, s32[1,1]{1,0:T(1,128)S(6)} %copy.22.count_ref, s32[1,128]{1,0:T(1,128)S(1)} %bitcast.60, bf16[8,200,256]{2,1,0:T(8,128)(2,1)S(1)} %all_to_all.10.own_ref, bf16[8,200,256]{2,1,0:T(8,128)(2,1)S(1)} %collective-permute-done.other_ref, ...), custom_call_target="tpu_custom_call" | custom-call | tf_op jit(solution)/shard_map/terms/pallas_call | solution.py:220
  35.9 10.0 %all-to-all-start.1 = ((s16[16,208,128]{2,1,0:T(8,128)(2,1)}), s16[16,208,128]{2,1,0:T(8,128)(2,1)S(1)}, u32[]{:S(2)}, u32[]{:S(2)}) async-start(s16[16,208,128]{2,1,0:T(8,128)(2,1)} %terms.1), calls=%async_computation.1 | async-start | bytes 1703936 | tf_op jit(solution)/shard_map/all_to_all | solution.py:334
  45.8 21.9 %all-to-all-done.1.got_ref = s16[16,208,128]{2,1,0:T(8,128)(2,1)S(1)} async-done(((s16[16,208,128]{2,1,0:T(8,128)(2,1)}), s16[16,208,128]{2,1,0:T(8,128)(2,1)S(1)}, u32[]{:S(2)}, u32[]{:S(2)}) %all-to-all-start.1) | async-done | bytes 852000 | tf_op jit(solution)/shard_map/all_to_all | solution.py:334
  67.8 1.2 %add_up.1 = bf16[200,256]{1,0:T(8,128)(2,1)S(1)} custom-call(s16[16,208,128]{2,1,0:T(8,128)(2,1)S(1)} %all-to-all-done.1.got_ref), custom_call_target="tpu_custom_call" | custom-call | tf_op jit(solution)/shard_map/add_up/pallas_call | solution.py:262
  69.0 0.6 collective-permute-start.1
  69.6 2.7 %collective-permute-start.2 = (bf16[200,256]{1,0:T(8,128)(2,1)S(1)}, bf16[200,256]{1,0:T(8,128)(2,1)S(1)}, u32[]{:S(2)}, u32[]{:S(2)}) collective-permute-start(bf16[200,256]{1,0:T(8,128)(2,1)S(1)} %add_up.1), channel_id=1, source_target_pairs={{0,112},{1,17},{16,0},{17,33},{32,16},{33,49},{48,32},{49,65},{64,... | collective-permute-start | bytes 307208 | tf_op jit(solution)/shard_map/ppermute | solution.py:295
  72.3 0.3 collective-permute-start.3
  72.6 0.1 broadcast_in_dim.33
  72.8 3.0 %collective-permute-done.1 = bf16[200,256]{1,0:T(8,128)(2,1)S(1)} collective-permute-done((bf16[200,256]{1,0:T(8,128)(2,1)S(1)}, bf16[200,256]{1,0:T(8,128)(2,1)S(1)}, u32[]{:S(2)}, u32[]{:S(2)}) %collective-permute-start.1) | collective-permute-done | bytes 102432 | tf_op jit(solution)/shard_map/ppermute | solution.py:295
  75.8 0.0 collective-permute-done.2
  75.8 0.3 collective-permute-start.6
  76.1 0.3 collective-permute-start.4
  76.5 2.9 %collective-permute-start.5 = (bf16[200,256]{1,0:T(8,128)(2,1)S(1)}, bf16[200,256]{1,0:T(8,128)(2,1)S(1)}, u32[]{:S(2)}, u32[]{:S(2)}) collective-permute-start(bf16[200,256]{1,0:T(8,128)(2,1)S(1)} %collective-permute-done.2), channel_id=1, source_target_pairs={{0,112},{1,17},{16,0},{17,33},{32,16},{33,49},{48,32},{49,65},{64,... | collective-permute-start | bytes 307208 | tf_op jit(solution)/shard_map/ppermute | solution.py:295
  79.4 0.0 collective-permute-done.3
  79.4 3.4 %collective-permute-done.4 = bf16[200,256]{1,0:T(8,128)(2,1)S(1)} collective-permute-done((bf16[200,256]{1,0:T(8,128)(2,1)S(1)}, bf16[200,256]{1,0:T(8,128)(2,1)S(1)}, u32[]{:S(2)}, u32[]{:S(2)}) %collective-permute-start.4) | collective-permute-done | bytes 102432 | tf_op jit(solution)/shard_map/ppermute | solution.py:295
  82.8 0.0 collective-permute-done.5
  82.8 1.1 %collective-permute-start.9 = (bf16[2,200,256]{2,1,0:T(8,128)(2,1)S(1)}, bf16[2,200,256]{2,1,0:T(8,128)(2,1)S(1)}, u32[]{:S(2)}, u32[]{:S(2)}) collective-permute-start(bf16[2,200,256]{2,1,0:T(8,128)(2,1)S(1)} %pad_maximum_fusion.1), channel_id=1, source_target_pairs={{0,128},{1,129},{16,144},{17,145},{32,160},{33,161},{48,176},{49,1... | collective-permute-start | bytes 614408 | tf_op jit(solution)/shard_map/ppermute | solution.py:295
  83.9 1.0 %collective-permute-start.7 = (bf16[200,256]{1,0:T(8,128)(2,1)S(1)}, bf16[200,256]{1,0:T(8,128)(2,1)S(1)}, u32[]{:S(2)}, u32[]{:S(2)}) collective-permute-start(bf16[200,256]{1,0:T(8,128)(2,1)S(1)} %collective-permute-done.4), channel_id=1, source_target_pairs={{0,16},{1,113},{16,32},{17,1},{32,48},{33,17},{48,64},{49,33},{64,... | collective-permute-start | bytes 307208 | tf_op jit(solution)/shard_map/ppermute | solution.py:295
  85.0 2.2 %collective-permute-start.8 = (bf16[200,256]{1,0:T(8,128)(2,1)S(1)}, bf16[200,256]{1,0:T(8,128)(2,1)S(1)}, u32[]{:S(2)}, u32[]{:S(2)}) collective-permute-start(bf16[200,256]{1,0:T(8,128)(2,1)S(1)} %collective-permute-done.5), channel_id=1, source_target_pairs={{0,112},{1,17},{16,0},{17,33},{32,16},{33,49},{48,32},{49,65},{64,... | collective-permute-start | bytes 307208 | tf_op jit(solution)/shard_map/ppermute | solution.py:295
  87.2 0.0 collective-permute-done.6
  87.3 2.5 %collective-permute-done.7 = bf16[200,256]{1,0:T(8,128)(2,1)S(1)} collective-permute-done((bf16[200,256]{1,0:T(8,128)(2,1)S(1)}, bf16[200,256]{1,0:T(8,128)(2,1)S(1)}, u32[]{:S(2)}, u32[]{:S(2)}) %collective-permute-start.7) | collective-permute-done | bytes 102432 | tf_op jit(solution)/shard_map/ppermute | solution.py:295
  89.8 0.0 collective-permute-done.8
  89.8 1.1 %collective-permute-start.10 = (bf16[2,200,256]{2,1,0:T(8,128)(2,1)S(1)}, bf16[2,200,256]{2,1,0:T(8,128)(2,1)S(1)}, u32[]{:S(2)}, u32[]{:S(2)}) collective-permute-start(bf16[2,200,256]{2,1,0:T(8,128)(2,1)S(1)} %pad_maximum_fusion.2), channel_id=1, source_target_pairs={{0,128},{1,129},{16,144},{17,145},{32,160},{33,161},{48,176},{49,1... | collective-permute-start | bytes 614408 | tf_op jit(solution)/shard_map/ppermute | solution.py:295
  90.9 3.2 %collective-permute-start.11 = (bf16[200,256]{1,0:T(8,128)(2,1)S(1)}, bf16[200,256]{1,0:T(8,128)(2,1)S(1)}, u32[]{:S(2)}, u32[]{:S(2)}) collective-permute-start(bf16[200,256]{1,0:T(8,128)(2,1)S(1)} %collective-permute-done.8), channel_id=1, source_target_pairs={{0,112},{1,17},{16,0},{17,33},{32,16},{33,49},{48,32},{49,65},{64,... | collective-permute-start | bytes 307208 | tf_op jit(solution)/shard_map/ppermute | solution.py:295
  94.2 0.0 collective-permute-start.12
  94.2 0.0 collective-permute-done.9
  94.3 2.5 %collective-permute-done.10 = bf16[2,200,256]{2,1,0:T(8,128)(2,1)S(1)} collective-permute-done((bf16[2,200,256]{2,1,0:T(8,128)(2,1)S(1)}, bf16[2,200,256]{2,1,0:T(8,128)(2,1)S(1)}, u32[]{:S(2)}, u32[]{:S(2)}) %collective-permute-start.10) | collective-permute-done | bytes 204832 | tf_op jit(solution)/shard_map/ppermute | solution.py:295
  96.8 0.0 collective-permute-done.11
  96.8 4.1 %collective-permute-done.12 = bf16[200,256]{1,0:T(8,128)(2,1)S(1)} collective-permute-done((bf16[200,256]{1,0:T(8,128)(2,1)S(1)}, bf16[200,256]{1,0:T(8,128)(2,1)S(1)}, u32[]{:S(2)}, u32[]{:S(2)}) %collective-permute-start.12) | collective-permute-done | bytes 102432 | tf_op jit(solution)/shard_map/ppermute | solution.py:295
  100.9 0.0 copy-start.2
  101.0 1.2 %copy-done.2 = bf16[2,8,200,256]{3,2,1,0:T(8,128)(2,1)} copy-done((bf16[2,8,200,256]{3,2,1,0:T(8,128)(2,1)}, bf16[2,8,200,256]{3,2,1,0:T(8,128)(2,1)S(1)}, u32[]{:S(2)}) %copy-start.2) | copy-done | bytes 1638424
  (19 shorter events, 0.3 us)
Async XLA Ops:
  20.7 10.2 %collective-permute-start = (bf16[8,200,256]{2,1,0:T(8,128)(2,1)S(1)}, bf16[8,200,256]{2,1,0:T(8,128)(2,1)S(1)}, u32[]{:S(2)}, u32[]{:S(2)}) collective-permute-start(bf16[8,200,256]{2,1,0:T(8,128)(2,1)S(1)} %all_to_all.10.own_ref), channel_id=1, source_target_pairs={{0,1},{1,0},{2,3},{3,2},{4,5},{5,4},{6,7},{7,6},{8,9},{9,8},{10,11... | collective-permute-start | bytes 2457608 | tf_op jit(solution)/shard_map/ppermute | solution.py:331
  20.7 10.2 %copy-start = (s32[1,1,128]{2,1,0:T(1,128)S(1)}, s32[1,1,128]{2,1,0:T(1,128)}, u32[]{:S(2)}) copy-start(s32[1,1,128]{2,1,0:T(1,128)} %param.7) | copy-start | bytes 1540
  20.7 10.2 %copy-start.1 = (s32[1,1,128]{2,1,0:T(1,128)S(1)}, s32[1,1,128]{2,1,0:T(1,128)}, u32[]{:S(2)}) copy-start(s32[1,1,128]{2,1,0:T(1,128)} %param.8) | copy-start | bytes 1540
  35.9 31.9 %all-to-all-start.1 = ((s16[16,208,128]{2,1,0:T(8,128)(2,1)}), s16[16,208,128]{2,1,0:T(8,128)(2,1)S(1)}, u32[]{:S(2)}, u32[]{:S(2)}) async-start(s16[16,208,128]{2,1,0:T(8,128)(2,1)} %terms.1), calls=%async_computation.1 | async-start | bytes 1703936 | tf_op jit(solution)/shard_map/all_to_all | solution.py:334
  69.0 6.8 %collective-permute-start.1 = (bf16[200,256]{1,0:T(8,128)(2,1)S(1)}, bf16[200,256]{1,0:T(8,128)(2,1)S(1)}, u32[]{:S(2)}, u32[]{:S(2)}) collective-permute-start(bf16[200,256]{1,0:T(8,128)(2,1)S(1)} %add_up.1), channel_id=1, source_target_pairs={{0,16},{1,113},{16,32},{17,1},{32,48},{33,17},{48,64},{49,33},{64,... | collective-permute-start | bytes 307208 | tf_op jit(solution)/shard_map/ppermute | solution.py:295
  69.6 6.2 %collective-permute-start.2 = (bf16[200,256]{1,0:T(8,128)(2,1)S(1)}, bf16[200,256]{1,0:T(8,128)(2,1)S(1)}, u32[]{:S(2)}, u32[]{:S(2)}) collective-permute-start(bf16[200,256]{1,0:T(8,128)(2,1)S(1)} %add_up.1), channel_id=1, source_target_pairs={{0,112},{1,17},{16,0},{17,33},{32,16},{33,49},{48,32},{49,65},{64,... | collective-permute-start | bytes 307208 | tf_op jit(solution)/shard_map/ppermute | solution.py:295
  72.3 7.1 %collective-permute-start.3 = (bf16[200,256]{1,0:T(8,128)(2,1)S(1)}, bf16[200,256]{1,0:T(8,128)(2,1)S(1)}, u32[]{:S(2)}, u32[]{:S(2)}) collective-permute-start(bf16[200,256]{1,0:T(8,128)(2,1)S(1)} %add_up.1), channel_id=1, source_target_pairs={{0,128},{1,129},{16,144},{17,145},{32,160},{33,161},{48,176},{49,1... | collective-permute-start | bytes 307208 | tf_op jit(solution)/shard_map/ppermute | solution.py:295
  75.8 11.4 %collective-permute-start.6 = (bf16[2,200,256]{2,1,0:T(8,128)(2,1)S(1)}, bf16[2,200,256]{2,1,0:T(8,128)(2,1)S(1)}, u32[]{:S(2)}, u32[]{:S(2)}) collective-permute-start(bf16[2,200,256]{2,1,0:T(8,128)(2,1)S(1)} %pad_maximum_fusion), channel_id=1, source_target_pairs={{0,128},{1,129},{16,144},{17,145},{32,160},{33,161},{48,176},{49,1... | collective-permute-start | bytes 614408 | tf_op jit(solution)/shard_map/ppermute | solution.py:295
  76.1 6.7 %collective-permute-start.4 = (bf16[200,256]{1,0:T(8,128)(2,1)S(1)}, bf16[200,256]{1,0:T(8,128)(2,1)S(1)}, u32[]{:S(2)}, u32[]{:S(2)}) collective-permute-start(bf16[200,256]{1,0:T(8,128)(2,1)S(1)} %collective-permute-done.1), channel_id=1, source_target_pairs={{0,16},{1,113},{16,32},{17,1},{32,48},{33,17},{48,64},{49,33},{64,... | collective-permute-start | bytes 307208 | tf_op jit(solution)/shard_map/ppermute | solution.py:295
  76.5 6.3 %collective-permute-start.5 = (bf16[200,256]{1,0:T(8,128)(2,1)S(1)}, bf16[200,256]{1,0:T(8,128)(2,1)S(1)}, u32[]{:S(2)}, u32[]{:S(2)}) collective-permute-start(bf16[200,256]{1,0:T(8,128)(2,1)S(1)} %collective-permute-done.2), channel_id=1, source_target_pairs={{0,112},{1,17},{16,0},{17,33},{32,16},{33,49},{48,32},{49,65},{64,... | collective-permute-start | bytes 307208 | tf_op jit(solution)/shard_map/ppermute | solution.py:295
  82.8 11.4 %collective-permute-start.9 = (bf16[2,200,256]{2,1,0:T(8,128)(2,1)S(1)}, bf16[2,200,256]{2,1,0:T(8,128)(2,1)S(1)}, u32[]{:S(2)}, u32[]{:S(2)}) collective-permute-start(bf16[2,200,256]{2,1,0:T(8,128)(2,1)S(1)} %pad_maximum_fusion.1), channel_id=1, source_target_pairs={{0,128},{1,129},{16,144},{17,145},{32,160},{33,161},{48,176},{49,1... | collective-permute-start | bytes 614408 | tf_op jit(solution)/shard_map/ppermute | solution.py:295
  83.9 5.9 %collective-permute-start.7 = (bf16[200,256]{1,0:T(8,128)(2,1)S(1)}, bf16[200,256]{1,0:T(8,128)(2,1)S(1)}, u32[]{:S(2)}, u32[]{:S(2)}) collective-permute-start(bf16[200,256]{1,0:T(8,128)(2,1)S(1)} %collective-permute-done.4), channel_id=1, source_target_pairs={{0,16},{1,113},{16,32},{17,1},{32,48},{33,17},{48,64},{49,33},{64,... | collective-permute-start | bytes 307208 | tf_op jit(solution)/shard_map/ppermute | solution.py:295
  85.0 4.8 %collective-permute-start.8 = (bf16[200,256]{1,0:T(8,128)(2,1)S(1)}, bf16[200,256]{1,0:T(8,128)(2,1)S(1)}, u32[]{:S(2)}, u32[]{:S(2)}) collective-permute-start(bf16[200,256]{1,0:T(8,128)(2,1)S(1)} %collective-permute-done.5), channel_id=1, source_target_pairs={{0,112},{1,17},{16,0},{17,33},{32,16},{33,49},{48,32},{49,65},{64,... | collective-permute-start | bytes 307208 | tf_op jit(solution)/shard_map/ppermute | solution.py:295
  89.8 6.9 %collective-permute-start.10 = (bf16[2,200,256]{2,1,0:T(8,128)(2,1)S(1)}, bf16[2,200,256]{2,1,0:T(8,128)(2,1)S(1)}, u32[]{:S(2)}, u32[]{:S(2)}) collective-permute-start(bf16[2,200,256]{2,1,0:T(8,128)(2,1)S(1)} %pad_maximum_fusion.2), channel_id=1, source_target_pairs={{0,128},{1,129},{16,144},{17,145},{32,160},{33,161},{48,176},{49,1... | collective-permute-start | bytes 614408 | tf_op jit(solution)/shard_map/ppermute | solution.py:295
  90.9 5.9 %collective-permute-start.11 = (bf16[200,256]{1,0:T(8,128)(2,1)S(1)}, bf16[200,256]{1,0:T(8,128)(2,1)S(1)}, u32[]{:S(2)}, u32[]{:S(2)}) collective-permute-start(bf16[200,256]{1,0:T(8,128)(2,1)S(1)} %collective-permute-done.8), channel_id=1, source_target_pairs={{0,112},{1,17},{16,0},{17,33},{32,16},{33,49},{48,32},{49,65},{64,... | collective-permute-start | bytes 307208 | tf_op jit(solution)/shard_map/ppermute | solution.py:295
  94.2 6.8 %collective-permute-start.12 = (bf16[200,256]{1,0:T(8,128)(2,1)S(1)}, bf16[200,256]{1,0:T(8,128)(2,1)S(1)}, u32[]{:S(2)}, u32[]{:S(2)}) collective-permute-start(bf16[200,256]{1,0:T(8,128)(2,1)S(1)} %collective-permute-done.7), channel_id=1, source_target_pairs={{0,144},{1,241},{16,160},{17,129},{32,176},{33,145},{48,192},{49,1... | collective-permute-start | bytes 307208 | tf_op jit(solution)/shard_map/ppermute | solution.py:295
  100.9 1.2 %copy-start.2 = (bf16[2,8,200,256]{3,2,1,0:T(8,128)(2,1)}, bf16[2,8,200,256]{3,2,1,0:T(8,128)(2,1)S(1)}, u32[]{:S(2)}) copy-start(bf16[2,8,200,256]{3,2,1,0:T(8,128)(2,1)S(1)} %bitcast_dynamic-update-slice_fusion) | copy-start | bytes 4915204
